TPU v7x, 32 devices: a whole 2x2x4 slice. The times are simulated.
32 devices in a mesh: rays: 8 (over z, x), views: 4 (over y, core).
Axes of the slice: x: 2, y: 2, z: 4, core: 2. Of those that a mesh axis runs over, the one named last changes fastest.
Arguments:
- master: float32 [11384], P('rays')
- first_moment: float32 [11384], P('rays'), may hold values from -0.75 to 0.75
- second_moment: float32 [11384], P('rays'), may hold values from 0.001 to 0.01
- step_count: int32 [1], replicated, may hold values from 2 to 20
- feature_maps: bfloat16 [12, 35, 12032], P('views'), may hold values from -6 to 6
- pixel_index: int32 [24576, 12], P('rays', 'views'), may hold values from 0 to 12031
- visible: int32 [24576, 12], P('rays', 'views'), may hold values from 0 to 1, as said below
- deltas: float32 [128, 192], P('rays'), may hold values from 0.002 to 0.02
- targets: float32 [128, 3], P('rays'), may hold values from -3 to 3
- scene_id: int32 [128], P('rays'), may hold values from 0 to 7
- scene_weight: int32 [8], replicated, may hold values from 1 to 4
Outputs:
- loss: float32 [], replicated
- master_new: float32 [11384], P('rays')
- first_new: float32 [11384], P('rays')
- second_new: float32 [11384], P('rays')
Inputs may be any that keep to these rules, and one draw needn't show every extreme that they name: Every sample is visible in at least one of the first 10 view slots; the last two slots are never visible.
All inputs are finite; a program needn't handle non-finite values.
Results may differ from a plain program's by a relative error of at most 0.00077.
Values may be sent and summed in bfloat16 or wider, within the bound.
No kernel may reach another device: no remote copies, remote signals or barrier semaphores. Data moves between devices by JAX's collectives and lax.ppermute only.
A program may use at most 128 MiB of HBM per device.

v0:
```python
import math

import jax
import jax.numpy as jnp
from jax import lax
from jax.sharding import PartitionSpec as P

MICRO = 2


LAYOUT = (
    ("w1", (35, 64)),
    ("b1", (64,)),
    ("w2", (64, 32)),
    ("b2", (32,)),
    ("u1", (64, 32)),
    ("c1", (32,)),
    ("u2", (32, 16)),
    ("c2", (16,)),
    ("wq", (16, 64)),
    ("wk", (16, 64)),
    ("wv", (16, 64)),
    ("wo", (64, 16)),
    ("s1", (16, 16)),
    ("d1", (16,)),
    ("s2", (16, 1)),
    ("d2", (1,)),
)
MOMENT_DECAY = 0.5
SQUARE_DECAY = 0.5
LEARNING_RATE = 0.05
WEIGHT_DECAY = 0.01
EPSILON = 1e-08


def rounded(value, ledger):
    if "give" in ledger:
        return value + ledger["give"].pop(0)
    narrow = lax.optimization_barrier(value.astype(jnp.bfloat16)).astype(jnp.float32)
    ledger["keep"].append(narrow - value)
    return narrow


def matmul_low(left_op, right_op):
    return jnp.matmul(left_op, right_op, precision=lax.Precision.HIGHEST)


def traced(part_fn, *primals):
    record = {"keep": []}
    part_fn(record, *primals)
    offsets = record["keep"]
    return jax.vjp(lambda *values: part_fn({"give": list(offsets)}, *values), *primals)


def unpack(flat_params):
    params = {}
    offset = 0
    for section, section_dims in LAYOUT:
        amount = math.prod(section_dims)
        params[section] = flat_params[offset : offset + amount].reshape(section_dims)
        offset = offset + amount
    return params


def views_part(ledger, params, features_in, visible_f):
    hidden = rounded(jax.nn.elu(matmul_low(features_in, params["w1"]) + params["b1"]), ledger)
    feature = jax.nn.elu(matmul_low(hidden, params["w2"]) + params["b2"])
    weighted = visible_f[..., None] * feature
    return (feature, jnp.sum(weighted, axis=1), jnp.sum(weighted * feature, axis=1))


def moments(total_sum, total_square, seen_count):
    average = total_sum / seen_count[:, None]
    return (average, total_square / seen_count[:, None] - average * average)


def blend_part(ledger, params, feature, average, variance, colour_in, visible_f):
    spread_cols = jnp.broadcast_to(variance[:, None, :], feature.shape)
    joined = rounded(jnp.concatenate([feature - average[:, None, :], spread_cols], axis=-1), ledger)
    inner_act = rounded(jax.nn.elu(matmul_low(joined, params["u1"]) + params["c1"]), ledger)
    logits = matmul_low(inner_act, params["u2"]) + params["c2"]
    exponent = visible_f[..., None] * jnp.exp(logits)
    numerator = jnp.sum(exponent * feature[..., :16], axis=1)
    denominator = jnp.sum(exponent, axis=1)
    colour_sum = jnp.sum(exponent[..., :1] * colour_in, axis=1)
    return (numerator, denominator, colour_sum)


def ray_part(ledger, params, numerator, denominator, colour_sum, deltas, targets, ray_weight):
    ray_count, samples = deltas.shape
    tokens = numerator / denominator
    colour = (colour_sum / denominator[:, :1]).reshape(ray_count, samples, 3)
    token_low = rounded(tokens, ledger)
    queries = rounded(matmul_low(token_low, params["wq"]), ledger).reshape(
        ray_count, samples, 4, 16
    )
    key_rows = rounded(matmul_low(token_low, params["wk"]), ledger).reshape(
        ray_count, samples, 4, 16
    )
    val_rows = rounded(matmul_low(token_low, params["wv"]), ledger).reshape(
        ray_count, samples, 4, 16
    )
    scores = (
        jnp.einsum("rqhd,rkhd->rhqk", queries, key_rows, precision=lax.Precision.HIGHEST) * 0.25
    )
    attention = rounded(jax.nn.softmax(scores, axis=-1), ledger)
    attended = jnp.einsum("rhqk,rkhd->rqhd", attention, val_rows, precision=lax.Precision.HIGHEST)
    attended = rounded(attended.reshape(ray_count * samples, 64), ledger)
    mixed_rows = tokens + matmul_low(attended, params["wo"])
    mixed_low = rounded(mixed_rows, ledger)
    inner_act = rounded(jax.nn.elu(matmul_low(mixed_low, params["s1"]) + params["d1"]), ledger)
    density = jax.nn.softplus(matmul_low(inner_act, params["s2"])[:, 0] + params["d2"][0])
    optical = density.reshape(ray_count, samples) * deltas
    before = jnp.cumsum(optical, axis=1) - optical
    render_weight = jnp.exp(-before) * (1.0 - jnp.exp(-optical))
    pixel_colour = jnp.sum(render_weight[..., None] * colour, axis=1)
    return jnp.sum(ray_weight * jnp.sum((pixel_colour - targets) ** 2, axis=-1))


def adamw(master, first_moment, second_moment, gradient, step_count):
    step_float = step_count[0].astype(jnp.float32)
    first_new = MOMENT_DECAY * first_moment + (1.0 - MOMENT_DECAY) * gradient
    second_new = SQUARE_DECAY * second_moment + (1.0 - SQUARE_DECAY) * gradient * gradient
    first_fix = 1.0 - jnp.power(MOMENT_DECAY, step_float)
    second_fix = 1.0 - jnp.power(SQUARE_DECAY, step_float)
    update = first_new / first_fix / (jnp.sqrt(second_new / second_fix) + EPSILON)
    master_new = master - LEARNING_RATE * (update + WEIGHT_DECAY * master)
    return (master_new, first_new, second_new)


def fetch(master):
    narrow = master.astype(jnp.bfloat16)
    return lax.all_gather(narrow, "rays", axis=0, tiled=True).astype(jnp.float32)


def body(
    master,
    first_moment,
    second_moment,
    step_count,
    feature_maps,
    pixel_index,
    visible,
    deltas,
    targets,
    scene_id,
    scene_weight,
):
    view_devices = lax.axis_size("views")
    ray_rows, samples = deltas.shape
    per_batch = ray_rows // MICRO
    point_rows = per_batch * samples
    visible_f = visible.astype(jnp.float32)
    view_slot = jnp.arange(feature_maps.shape[0])[None, :]
    scene_hits = (scene_id[:, None] == jnp.arange(scene_weight.shape[0])[None, :]).astype(
        jnp.float32
    )
    ray_weight = jnp.sum(scene_hits * scene_weight.astype(jnp.float32)[None, :], axis=1)
    weight_part = jnp.sum(ray_weight)
    seed = 1.0 / lax.psum(weight_part, "rays")
    gradient = jnp.zeros((master.shape[0] * lax.axis_size("rays"),), jnp.float32)
    loss_part = jnp.zeros((), jnp.float32)
    for batch_index in range(MICRO):
        flat_w = fetch(master)
        start = batch_index * point_rows
        ray_start = batch_index * per_batch
        vis_rows = visible_f[start : start + point_rows]
        features_in = feature_maps[view_slot, :, pixel_index[start : start + point_rows]].astype(
            jnp.float32
        )
        colour_in = features_in[..., 32:]
        seen_part = jnp.sum(vis_rows, axis=1)
        delta_rows = deltas[ray_start : ray_start + per_batch]
        target_rows = targets[ray_start : ray_start + per_batch]
        weight_rows = ray_weight[ray_start : ray_start + per_batch]
        (feature, total_sum, total_square), back_views = traced(
            lambda ledger, flat_params: views_part(
                ledger, unpack(flat_params), features_in, vis_rows
            ),
            flat_w,
        )
        whole_sum, whole_square, whole_seen = lax.psum(
            (total_sum, total_square, seen_part), "views"
        )
        (average, variance), back_moments = jax.vjp(
            lambda sum_val, square_val: moments(sum_val, square_val, whole_seen),
            whole_sum,
            whole_square,
        )
        (numerator, denominator, colour_sum), back_blend = traced(
            lambda ledger, flat_params, feature_val, average_val, variance_val: blend_part(
                ledger,
                unpack(flat_params),
                feature_val,
                average_val,
                variance_val,
                colour_in,
                vis_rows,
            ),
            flat_w,
            feature,
            average,
            variance,
        )
        numerator, denominator, colour_sum = lax.psum((numerator, denominator, colour_sum), "views")
        batch_loss, back_rays = traced(
            lambda ledger, flat_params, numer_val, denom_val, colour_val: ray_part(
                ledger,
                unpack(flat_params),
                numer_val,
                denom_val,
                colour_val,
                delta_rows,
                target_rows,
                weight_rows,
            ),
            flat_w,
            numerator,
            denominator,
            colour_sum,
        )
        loss_part = loss_part + batch_loss
        grad_ray_w, grad_numer, grad_denom, grad_colour = back_rays(seed)
        grad_blend_w, grad_feature, grad_average, grad_variance = back_blend(
            (grad_numer, grad_denom, grad_colour)
        )
        own_gsum, own_gsquare = back_moments((grad_average, grad_variance))
        grad_sum, grad_square = (
            lax.psum(own_gsum.astype(jnp.bfloat16), "views").astype(jnp.float32),
            lax.psum(own_gsquare.astype(jnp.bfloat16), "views").astype(jnp.float32),
        )
        (grad_view_w,) = back_views((grad_feature, grad_sum, grad_square))
        gradient = gradient + grad_view_w + grad_blend_w + grad_ray_w / view_devices
    owned_grad = lax.psum_scatter(gradient, "rays", scatter_dimension=0, tiled=True)
    owned_grad = lax.psum(owned_grad, "views")
    loss = lax.psum(loss_part, "rays") * seed
    master_new, first_new, second_new = adamw(
        master, first_moment, second_moment, owned_grad, step_count
    )
    return (loss, master_new, first_new, second_new)


def solution(mesh):
    placed = (
        P("rays"),
        P("rays"),
        P("rays"),
        P(),
        P("views", None, None),
        P("rays", "views"),
        P("rays", "views"),
        P("rays", None),
        P("rays", None),
        P("rays"),
        P(),
    )
    return jax.shard_map(
        body,
        mesh=mesh,
        in_specs=placed,
        out_specs=(P(), P("rays"), P("rays"), P("rays")),
        check_vma=False,
    )
```

profile of v0, /device:TPU:0, one launch (start us, length us, event | category | flops | bytes accessed | tf_op | source)
XLA Modules:
  0.0 687.3 jit_solution(12218807392890689628)
XLA Ops:
  10.2 38.8 %all-reduce.42 = bf16[11384]{0:T(1024)(128)(2,1)S(1)} all-reduce(bf16[11384]{0:T(1024)(128)(2,1)S(1)} %dynamic-update-slice), channel_id=1, replica_groups=mesh['rays'=8,'views'=4] {'rays'}, use_global_device_ids=true, to_apply=%add.42 | all-reduce | flops 11384 | bytes 45536
  50.5 8.5 %copy.206 = bf16[3,35,12032]{1,2,0:T(8,128)(2,1)} copy(bf16[3,35,12032]{2,1,0:T(8,128)(2,1)} %param.16) | data formatting | bytes 5053440 | tf_op args[4]
  59.8 54.3 %gather_fusion = bf16[4608,35]{1,0:T(8,128)(2,1)S(1)} fusion(bf16[3,35,12032]{1,2,0:T(8,128)(2,1)} %copy.206, s32[4608]{0:T(1024)S(1)} %reshape.470), kind=kCustom, calls=%fused_computation | custom fusion | bytes 681984 | tf_op jit(solution)/shard_map/gather | solution.py:168
  121.4 75.1 %gather_fusion.1 = bf16[4608,35]{1,0:T(8,128)(2,1)} fusion(bf16[3,35,12032]{1,2,0:T(8,128)(2,1)} %copy.206, s32[4608]{0:T(1024)S(1)} %reshape.476), kind=kCustom, calls=%fused_computation.1 | custom fusion | bytes 681984 | tf_op jit(solution)/shard_map/gather | solution.py:168
  196.5 3.3 reshape.479
  220.1 17.7 %psum.146 = f32[]{:T(128)} all-reduce(f32[]{:T(128)} %get-tuple-element.34), channel_id=1, replica_groups=mesh['rays'=8,'views'=4] {'rays'}, use_global_device_ids=true, to_apply=%region_45.47 | all-reduce | flops 1 | bytes 8 | tf_op jit(solution)/shard_map/psum | solution.py:160
  240.6 11.5 %all-reduce.46 = (f32[1536]{0:T(1024)}, f32[1536]{0:T(1024)}) all-reduce(f32[1536]{0:T(1024)} %get-tuple-element.28, f32[1536]{0:T(1024)} %get-tuple-element.29), channel_id=1, replica_groups=mesh['rays'=8,'views'=4] {'views'}, use_global_device_ids=true, to_apply=%region_25.27 | all-reduce | flops 3072 | bytes 24576 | tf_op jit(solution)/shard_map/psum | solution.py:182
  262.4 2.2 fusion.134
  271.6 10.6 %fusion.16 = f32[1536,3]{1,0:T(8,128)} fusion(f32[1536,3]{1,0:T(8,128)} %bitcast.363, bf16[1536,3,35]{2,1,0:T(4,128)(2,1)S(1)} %reshape.473), kind=kLoop, calls=%fused_computation.28 | loop fusion | flops 36864 | bytes 64512 | tf_op jit(solution)/shard_map/jvp()/reduce_sum | solution.py:85
  286.6 9.3 %fusion.18 = f32[1536,3]{1,0:T(8,128)} fusion(f32[1536,3]{1,0:T(8,128)S(1)} %bitcast.360, bf16[1536,3,35]{2,1,0:T(4,128)(2,1)S(1)} %reshape.479), kind=kLoop, calls=%fused_computation.30 | loop fusion | flops 36864 | bytes 64512 | tf_op jit(solution)/shard_map/jvp()/reduce_sum | solution.py:85
  295.9 36.3 %all-reduce.45 = (f32[1536,3]{1,0:T(8,128)}, f32[1536,3]{1,0:T(8,128)}) all-reduce(f32[1536,3]{1,0:T(8,128)} %fusion.18, f32[1536,3]{1,0:T(8,128)S(1)} %copy-done.63), channel_id=1, replica_groups=mesh['rays'=8,'views'=4] {'views'}, use_global_device_ids=true, to_apply=%region_39.41 | all-reduce | flops 9216 | bytes 73728 | tf_op jit(solution)/shard_map/psum | solution.py:205
  344.9 5.3 fusion.96
  350.2 5.3 fusion.258
  356.6 5.3 fusion.255
  362.7 2.0 subtract_add_fusion
  364.7 3.3 convolution_bitcast_fusion.9
  369.1 2.0 reshape.431
  381.3 5.5 fusion.104
  386.8 5.3 fusion.251
  393.2 5.3 fusion.248
  401.7 3.3 convolution_bitcast_fusion.11
  406.1 2.0 reshape.417
  421.5 2.3 multiply_reduce_fusion.8
  423.9 2.9 reduce-window.36
  427.0 2.3 multiply_reduce_fusion.9
  429.5 2.5 reduce-window.34
  435.1 9.0 %multiply_reduce_fusion.1 = (f32[8,4,192]{2,1,0:T(4,128)S(1)}, f32[8,4,192,192]{2,3,1,0:T(8,128)S(1)}) fusion(f32[8,4,192,192]{2,3,1,0:T(8,128)} %copy-done.3, f32[8,4,192]{2,1,0:T(4,128)S(1)} %copy-done.160, f32[8,4,16,192]{3,2,1,0:T(8,128)S(1)} %convolution_bitcast_fusion.7, f32[8,192,4,16]{1,0,3,2:T(8,128)S(1)} %copy-done.43), kind=kOutput, calls=%fused_computation.9 | convolution fusion | flops 230025216 | bytes 10272768 | tf_op jit(solution)/shard_map/transpose(jvp(rhqk,rkhd->rqhd))/dot_general | solution.py:107
  444.2 5.1 convolution_bitcast_fusion.4
  449.2 7.2 %convolution_bitcast_fusion.5 = f32[8,192,4,16]{1,3,2,0:T(8,128)} fusion(f32[8,192,4,16]{1,0,3,2:T(8,128)S(1)} %copy-done.78, f32[8,4,192,192]{2,3,1,0:T(8,128)S(1)} %bitcast.357, f32[8,4,192,192]{2,3,1,0:T(8,128)S(1)} %get-tuple-element.179, f32[8,4,192]{2,1,0:T(4,128)S(1)} %neg.100, f32[8,4,192]{2,1,0:T(4,128)S(1)} %copy-done.141), kind=kOutput, calls=%fused_computation.83 | convolution fusion | flops 231211008 | bytes 10272768 | tf_op jit(solution)/shard_map/transpose(jvp(rqhd,rkhd->rhqk))/dot_general | solution.py:104
  456.4 6.4 convolution_bitcast_fusion.6
  464.2 1.9 fusion.236
  469.6 8.9 %convolution_bitcast_fusion.2 = f32[8,192,4,16]{1,3,2,0:T(8,128)} fusion(f32[8,4,16,192]{3,2,1,0:T(8,128)S(1)} %convolution_bitcast_fusion.3, f32[8,4,192,192]{2,3,1,0:T(8,128)} %copy-done), kind=kOutput, calls=%fused_computation.80 | convolution fusion | flops 226492416 | bytes 5505024 | tf_op jit(solution)/shard_map/transpose(jvp(rhqk,rkhd->rqhd))/dot_general | solution.py:107
  478.5 6.2 multiply_reduce_fusion
  484.8 7.3 %convolution_bitcast_fusion.1 = f32[8,192,4,16]{1,3,2,0:T(8,128)} fusion(f32[8,192,4,16]{1,0,3,2:T(8,128)S(1)} %copy-done.74, f32[8,4,192,192]{2,3,1,0:T(8,128)S(1)} %bitcast.355, f32[8,4,192,192]{2,3,1,0:T(8,128)S(1)} %get-tuple-element.174, f32[8,4,192]{2,1,0:T(4,128)S(1)} %neg.109, f32[8,4,192]{2,1,0:T(4,128)S(1)} %copy-done.139), kind=kOutput, calls=%fused_computation.79 | convolution fusion | flops 231211008 | bytes 10272768 | tf_op jit(solution)/shard_map/transpose(jvp(rqhd,rkhd->rhqk))/dot_general | solution.py:104
  492.0 5.1 convolution_bitcast_fusion
  499.7 2.1 copy.249
  501.8 2.0 reshape.442
  507.1 5.5 fusion.17
  516.6 2.8 fusion.230
  529.9 3.8 fusion.19
  538.5 2.3 copy.271
  540.8 2.0 reshape.459
  546.1 2.5 fusion.235
  548.6 2.3 fusion.260
  590.3 29.0 %all-reduce.58.cloned.1.call-done = (bf16[1536,32]{0,1:T(8,128)(2,1)}, bf16[1536,32]{0,1:T(8,128)(2,1)}, bf16[1536,32]{0,1:T(8,128)(2,1)}, bf16[1536,32]{0,1:T(8,128)(2,1)}) async-done(((bf16[1536,32]{0,1:T(8,128)(2,1)}, bf16[1536,32]{0,1:T(8,128)(2,1)}, bf16[1536,32]{0,1:T(8,128)(2,1)}, bf16[1536,32]{0,1:T(8,128)(2,1)}), (bf16[1536,32]{0,1:T(8,128)(2,1)}, bf16[1536,32]{0,1:T(8,128)(2,1)}, ...) | async-done | bytes 393232 | tf_op jit(solution)/shard_map/psum | solution.py:229
  621.8 3.7 convolution_bitcast_fusion.15
  634.3 37.6 %all-reduce.44 = (f32[]{:T(128)}, f32[11384]{0:T(1024)S(1)}) all-reduce(f32[]{:T(128)S(6)} %add.408, f32[11384]{0:T(1024)S(1)} %multiply_add_fusion), channel_id=1, replica_groups=mesh['rays'=8,'views'=4] {'rays'}, use_global_device_ids=true, to_apply=%region_43.45 | all-reduce | flops 11385 | bytes 91080 | tf_op jit(solution)/shard_map/psum | solution.py:236
  672.0 5.9 psum.151
  (728 shorter events, 183.6 us)
Async XLA Ops:
  7.2 248.2 %all-reduce.56.cloned.1.call-start = ((), (), s32[]{:S(2)}) async-start(), calls=%async_computation.1 | async-start | bytes 1572864 | tf_op jit(solution)/shard_map/psum | solution.py:182
  114.9 156.7 %copy-start.6 = (bf16[1536,3,35]{2,1,0:T(4,128)(2,1)}, bf16[1536,3,35]{2,1,0:T(4,128)(2,1)S(1)}, u32[]{:S(2)}) copy-start(bf16[1536,3,35]{2,1,0:T(4,128)(2,1)S(1)} %reshape.473) | copy-start | bytes 967684
  120.7 85.9 %copy-start.110 = (f32[1536,3]{0,1:T(4,128)}, f32[1536,3]{0,1:T(4,128)S(1)}, u32[]{:S(2)}) copy-start(f32[1536,3]{0,1:T(4,128)S(1)} %get-tuple-element.97) | copy-start | bytes 55300
  199.9 86.7 %copy-start.4 = (bf16[1536,3,35]{2,1,0:T(4,128)(2,1)}, bf16[1536,3,35]{2,1,0:T(4,128)(2,1)S(1)}, u32[]{:S(2)}) copy-start(bf16[1536,3,35]{2,1,0:T(4,128)(2,1)S(1)} %reshape.479) | copy-start | bytes 967684
  207.7 124.6 %all-reduce.54.cloned.1.call-start = ((), (), s32[]{:S(2)}) async-start(), calls=%async_computation | async-start | bytes 786432 | tf_op jit(solution)/shard_map/psum | solution.py:205
  220.1 35.3 %copy-start.199 = (f32[16]{0:T(128)}, f32[16]{0:T(128)S(1)}, u32[]{:S(2)}) copy-start(f32[16]{0:T(128)S(1)} %get-tuple-element.35) | copy-start | bytes 196
  268.4 15.3 %copy-start.111 = (f32[1536,3]{0,1:T(4,128)S(1)}, f32[1536,3]{0,1:T(4,128)}, u32[]{:S(2)}) copy-start(f32[1536,3]{0,1:T(4,128)} %copy-done.110) | copy-start | bytes 55300
  271.6 10.6 %copy-start.25 = (f32[1536,3,32]{0,2,1:T(8,128)S(1)}, f32[1536,3,32]{0,2,1:T(8,128)}, u32[]{:S(2)}) copy-start(f32[1536,3,32]{0,2,1:T(8,128)} %copy-done.24) | copy-start | bytes 1769476
  271.6 10.6 %copy-start.70 = (f32[1536,3,32]{0,2,1:T(8,128)S(1)}, f32[1536,3,32]{0,2,1:T(8,128)}, u32[]{:S(2)}) copy-start(f32[1536,3,32]{0,2,1:T(8,128)} %get-tuple-element.138) | copy-start | bytes 1769476
  271.6 10.6 %copy-start.154 = (u8[1536,32]{0,1:T(8,128)(4,1)S(1)}, u8[1536,32]{0,1:T(8,128)(4,1)}, u32[]{:S(2)}) copy-start(u8[1536,32]{0,1:T(8,128)(4,1)} %get-tuple-element.137) | copy-start | bytes 147460
  271.6 12.0 %copy-start.68 = (f32[1536,3,32]{0,2,1:T(8,128)S(1)}, f32[1536,3,32]{0,2,1:T(8,128)}, u32[]{:S(2)}) copy-start(f32[1536,3,32]{0,2,1:T(8,128)} %get-tuple-element.82) | copy-start | bytes 1769476
  282.8 13.1 %copy-start.63 = (f32[1536,3]{1,0:T(8,128)S(1)}, f32[1536,3]{1,0:T(8,128)}, u32[]{:S(2)}) copy-start(f32[1536,3]{1,0:T(8,128)} %fusion.16) | copy-start | bytes 55300
  286.2 47.0 %copy-start.148 = (bf16[16,64]{1,0:T(8,128)(2,1)S(1)}, bf16[16,64]{1,0:T(8,128)(2,1)}, u32[]{:S(2)}) copy-start(bf16[16,64]{1,0:T(8,128)(2,1)} %reshape.409) | copy-start | bytes 6148
  286.5 47.0 %copy-start.142 = (bf16[16,64]{1,0:T(8,128)(2,1)S(1)}, bf16[16,64]{1,0:T(8,128)(2,1)}, u32[]{:S(2)}) copy-start(bf16[16,64]{1,0:T(8,128)(2,1)} %reshape.411) | copy-start | bytes 6148
  286.6 332.7 %all-reduce.58.cloned.1.call-start = ((), (), s32[]{:S(2)}) async-start(), calls=%async_computation.2 | async-start | bytes 786432 | tf_op jit(solution)/shard_map/psum | solution.py:229
  295.9 41.6 %copy-start.145 = (bf16[16,64]{1,0:T(8,128)(2,1)S(1)}, bf16[16,64]{1,0:T(8,128)(2,1)}, u32[]{:S(2)}) copy-start(bf16[16,64]{1,0:T(8,128)(2,1)} %reshape.413) | copy-start | bytes 6148
  409.9 10.2 %copy-start.61 = (f32[1536,3]{1,0:T(8,128)S(1)}, f32[1536,3]{1,0:T(8,128)}, u32[]{:S(2)}) copy-start(f32[1536,3]{1,0:T(8,128)} %get-tuple-element.42) | copy-start | bytes 55300
  413.6 10.2 %copy-start.136 = (f32[1536,16]{0,1:T(8,128)}, f32[1536,16]{0,1:T(8,128)S(1)}, u32[]{:S(2)}) copy-start(f32[1536,16]{0,1:T(8,128)S(1)} %fusion.29) | copy-start | bytes 294916
  414.5 19.5 %copy-start.92 = (f32[1536,16]{0,1:T(8,128)}, f32[1536,16]{0,1:T(8,128)S(1)}, u32[]{:S(2)}) copy-start(f32[1536,16]{0,1:T(8,128)S(1)} %convolution_add_fusion.27) | copy-start | bytes 294916
  419.1 13.0 %copy-start.176 = (f32[16,192]{1,0:T(8,128)S(1)}, f32[16,192]{1,0:T(8,128)}, u32[]{:S(2)}) copy-start(f32[16,192]{1,0:T(8,128)} %param.19) | copy-start | bytes 36868
  419.1 14.9 %copy-start.180 = (bf16[16,16]{1,0:T(8,128)(2,1)S(1)}, bf16[16,16]{1,0:T(8,128)(2,1)}, u32[]{:S(2)}) copy-start(bf16[16,16]{1,0:T(8,128)(2,1)} %reshape.421) | copy-start | bytes 1540
  419.2 14.9 %copy-start.217 = (f32[16]{0:T(128)S(1)}, f32[16]{0:T(128)}, u32[]{:S(2)}) copy-start(f32[16]{0:T(128)} %slice_convert_fusion) | copy-start | bytes 196
  420.1 14.5 %copy-start.158 = (bf16[4,16,16,1]{2,1,0,3:T(8,128)(2,1)S(1)}, bf16[4,16,16,1]{2,1,0,3:T(8,128)(2,1)}, u32[]{:S(2)}) copy-start(bf16[4,16,16,1]{2,1,0,3:T(8,128)(2,1)} %reshape.511) | copy-start | bytes 6148
  420.4 14.6 %copy-start.43 = (f32[8,192,4,16]{1,0,3,2:T(8,128)S(1)}, f32[8,192,4,16]{1,0,3,2:T(8,128)}, u32[]{:S(2)}) copy-start(f32[8,192,4,16]{1,0,3,2:T(8,128)} %reshape.410) | copy-start | bytes 1179652
  420.4 14.6 %copy-start.160 = (f32[8,4,192]{2,1,0:T(4,128)S(1)}, f32[8,4,192]{2,1,0:T(4,128)}, u32[]{:S(2)}) copy-start(f32[8,4,192]{2,1,0:T(4,128)} %multiply_divide_fusion.1) | copy-start | bytes 73732
  444.1 12.2 %slice-start = ((s8[6291456]{0:T(1024)(128)(4,1)}), s8[4194304]{0:T(1024)(128)(4,1)S(1)}, s32[]{:S(2)}) async-start(s8[6291456]{0:T(1024)(128)(4,1)} %bitcast.352), calls=%async_computation.3 | async-start | bytes 8388608
  456.4 10.3 %copy-start.90 = (f32[1536,16]{0,1:T(8,128)S(1)}, f32[1536,16]{0,1:T(8,128)}, u32[]{:S(2)}) copy-start(f32[1536,16]{0,1:T(8,128)} %copy-done.89) | copy-start | bytes 294916
  456.4 22.0 %slice-start.2 = ((s8[6291456]{0:T(1024)(128)(4,1)}), s8[2097152]{0:T(1024)(128)(4,1)S(1)}, s32[]{:S(2)}) async-start(s8[6291456]{0:T(1024)(128)(4,1)} %bitcast.354), calls=%async_computation.5 | async-start | bytes 4194304
  468.3 10.2 %slice-start.3 = ((s8[6291456]{0:T(1024)(128)(4,1)}), s8[4194304]{0:T(1024)(128)(4,1)S(1)}, s32[]{:S(2)}) async-start(s8[6291456]{0:T(1024)(128)(4,1)} %bitcast.354), calls=%async_computation.6 | async-start | bytes 8388608
  503.8 10.3 %copy-start.147 = (bf16[16,64]{1,0:T(8,128)(2,1)S(1)}, bf16[16,64]{1,0:T(8,128)(2,1)}, u32[]{:S(2)}) copy-start(bf16[16,64]{1,0:T(8,128)(2,1)} %reshape.413) | copy-start | bytes 6148
  504.9 10.4 %copy-start.144 = (bf16[16,64]{1,0:T(8,128)(2,1)S(1)}, bf16[16,64]{1,0:T(8,128)(2,1)}, u32[]{:S(2)}) copy-start(bf16[16,64]{1,0:T(8,128)(2,1)} %reshape.411) | copy-start | bytes 6148
  506.2 10.4 %copy-start.115 = (f32[1536,3]{0,1:T(4,128)S(1)}, f32[1536,3]{0,1:T(4,128)}, u32[]{:S(2)}) copy-start(f32[1536,3]{0,1:T(4,128)} %get-tuple-element.98) | copy-start | bytes 55300
  507.1 12.3 %copy-start.157 = (u8[1536,32]{0,1:T(8,128)(4,1)S(1)}, u8[1536,32]{0,1:T(8,128)(4,1)}, u32[]{:S(2)}) copy-start(u8[1536,32]{0,1:T(8,128)(4,1)} %copy-done.156) | copy-start | bytes 147460
  507.1 12.3 %copy-start.166 = (bf16[32,16]{1,0:T(8,128)(2,1)S(1)}, bf16[32,16]{1,0:T(8,128)(2,1)}, u32[]{:S(2)}) copy-start(bf16[32,16]{1,0:T(8,128)(2,1)} %reshape.408) | copy-start | bytes 3076
  535.1 10.9 %copy-start.98 = (f32[1536,3,16]{0,2,1:T(8,128)S(1)}, f32[1536,3,16]{0,2,1:T(8,128)}, u32[]{:S(2)}) copy-start(f32[1536,3,16]{0,2,1:T(8,128)} %copy-done.97) | copy-start | bytes 884740
  535.1 10.9 %copy-start.102 = (f32[1536,3,16]{0,2,1:T(8,128)S(1)}, f32[1536,3,16]{0,2,1:T(8,128)}, u32[]{:S(2)}) copy-start(f32[1536,3,16]{0,2,1:T(8,128)} %get-tuple-element.139) | copy-start | bytes 884740
  538.5 12.4 %copy-start.47 = (f32[1536,64]{0,1:T(8,128)}, f32[1536,64]{0,1:T(8,128)S(1)}, u32[]{:S(2)}) copy-start(f32[1536,64]{0,1:T(8,128)S(1)} %reshape.458) | copy-start | bytes 1179652
  540.8 10.1 %copy-start.21 = (f32[1536,3,32]{0,2,1:T(8,128)S(1)}, f32[1536,3,32]{0,2,1:T(8,128)}, u32[]{:S(2)}) copy-start(f32[1536,3,32]{0,2,1:T(8,128)} %copy-done.20) | copy-start | bytes 1769476
  557.1 17.3 %copy-start.159 = (f32[64,32]{1,0:T(8,128)S(1)}, f32[64,32]{1,0:T(8,128)}, u32[]{:S(2)}) copy-start(f32[64,32]{1,0:T(8,128)} %convolution_bitcast_fusion.12) | copy-start | bytes 24580
  559.1 29.7 %copy-start.94 = (f32[1536,16]{0,1:T(8,128)S(1)}, f32[1536,16]{0,1:T(8,128)}, u32[]{:S(2)}) copy-start(f32[1536,16]{0,1:T(8,128)} %copy-done.92) | copy-start | bytes 294916
  559.1 29.7 %copy-start.173 = (f32[1536]{0:T(1024)S(1)}, f32[1536]{0:T(1024)}, u32[]{:S(2)}) copy-start(f32[1536]{0:T(1024)} %copy-done.171) | copy-start | bytes 18436
  560.2 60.9 %copy-start.30 = (f32[1536,3,32]{0,2,1:T(8,128)S(1)}, f32[1536,3,32]{0,2,1:T(8,128)}, u32[]{:S(2)}) copy-start(f32[1536,3,32]{0,2,1:T(8,128)} %copy-done.29) | copy-start | bytes 1769476
  560.2 60.9 %copy-start.103 = (f32[1536,3,16]{0,2,1:T(8,128)S(1)}, f32[1536,3,16]{0,2,1:T(8,128)}, u32[]{:S(2)}) copy-start(f32[1536,3,16]{0,2,1:T(8,128)} %get-tuple-element.95) | copy-start | bytes 884740
  560.2 60.9 %copy-start.116 = (f32[1536,3]{0,1:T(4,128)S(1)}, f32[1536,3]{0,1:T(4,128)}, u32[]{:S(2)}) copy-start(f32[1536,3]{0,1:T(4,128)} %get-tuple-element.98) | copy-start | bytes 55300
  560.2 60.9 %copy-start.125 = (u8[1536,32]{0,1:T(8,128)(4,1)S(1)}, u8[1536,32]{0,1:T(8,128)(4,1)}, u32[]{:S(2)}) copy-start(u8[1536,32]{0,1:T(8,128)(4,1)} %copy-done.124) | copy-start | bytes 147460
  630.0 48.6 %copy-start.188 = (f32[1423]{0:T(1024)S(1)}, f32[1423]{0:T(1024)}, u32[]{:S(2)}) copy-start(f32[1423]{0:T(1024)} %param.12) | copy-start | bytes 17080
  630.0 48.6 %copy-start.203 = (f32[1423]{0:T(1024)S(1)}, f32[1423]{0:T(1024)}, u32[]{:S(2)}) copy-start(f32[1423]{0:T(1024)} %param.14) | copy-start | bytes 17080
  630.0 48.6 %copy-start.204 = (f32[1423]{0:T(1024)S(1)}, f32[1423]{0:T(1024)}, u32[]{:S(2)}) copy-start(f32[1423]{0:T(1024)} %param.13) | copy-start | bytes 17080
  (185 other events, 922.0 us)
Sparse Core Ops, SparseCore 0:
  207.8 32.4 all-reduce.55
  286.7 33.1 all-reduce.53
  587.3 31.9 all-reduce.57
where the time goes:
time: 699 us; the launch traced here: 687 us
  local copies, waits for them, and re-layouts  223 us (32%)
  blocking collectives  148 us (21%)
  matrix products  148 us (21%)
  other arithmetic  117 us (17%)
  waiting for transfers between devices  29 us (4%)
  between operations  23.1 us (3%)
    gather x6, local copies, waits for them, and re-layouts, body(): feature_maps[view_slot, :, pixel_index[start:start + point_rows]]  135 us
    dot_general x68, matrix products, matmul_low(): return jnp.matmul(left_op, right_op, precision=lax.Precision.HIGHEST)  71.3 us
    dot_general x8, matrix products, ray_part(): jnp.einsum('rhqk,rkhd->rqhd', attention, val_rows, precision=lax.Precisio...  39.1 us
    unnamed x1, blocking collectives  38.8 us
    psum x1, blocking collectives, body(): loss = lax.psum(loss_part, 'rays') * seed  37.6 us
    dot_general x8, matrix products, ray_part(): jnp.einsum('rqhd,rkhd->rhqk', queries, key_rows, precision=lax.Precision....  37.4 us
    psum x1, blocking collectives, body(): lax.psum((numerator, denominator, colour_sum), 'views')  36.3 us
    reduce_sum x4, other arithmetic, blend_part(): colour_sum = jnp.sum(exponent[..., :1] * colour_in, axis=1)  29.2 us
  transfers between devices with their start and end apart: 3, of which 1 were waited for; matrix products, arithmetic and copies ran while one was open for 4% of the time, Pallas kernels for 0%

commit v1 on v0

v1 whole, which is shorter than its diff:
```python
import jax
import jax.numpy as jnp
from jax import lax
from jax.experimental import pallas as pl
from jax.experimental.pallas import tpu as pltpu
from jax.sharding import PartitionSpec as P

F32 = jnp.float32
BF16 = jnp.bfloat16
SEEN_VIEWS = 10
CHANNELS = 35
STRIP = 40
RAY = 192
CHUNK = 2 * RAY
PASSES = 2
MOMENT_DECAY = 0.5
SQUARE_DECAY = 0.5
LEARNING_RATE = 0.05
WEIGHT_DECAY = 0.01
EPSILON = 1e-08
NN = (((1,), (0,)), ((), ()))
NT = (((1,), (1,)), ((), ()))
TN = (((0,), (0,)), ((), ()))


def dot(left, right, dims=NN):
    return lax.dot_general(left, right, dims, preferred_element_type=F32)


def parts(value, count):
    out = []
    for step in range(count):
        piece = value.astype(BF16)
        out.append(piece)
        if step + 1 < count:
            value = value - piece.astype(F32)
    return out


def dot_left(value, right, dims, count=PASSES):
    return sum(dot(piece, right, dims) for piece in parts(value, count))


def dot_right(left, value, dims, count=PASSES):
    return sum(dot(left, piece, dims) for piece in parts(value, count))


def elu_pair(value):
    slope = jnp.exp(jnp.minimum(value, 0.0))
    return jnp.maximum(value, 0.0) + (slope - 1.0), slope


def iota(shape, axis):
    return lax.broadcasted_iota(jnp.int32, shape, axis)


def gather_kernel(views, tile, pix_ref, vis_ref, map_ref, out_ref):
    pixels = map_ref.shape[2]
    strips = []
    row = iota((STRIP, tile), 0)
    for view in range(views):
        index = pix_ref[view : view + 1, :]
        high = jnp.broadcast_to(index >> 8, (STRIP, tile))
        low = jnp.broadcast_to(index & 255, (256, tile))
        picked = (iota((256, tile), 0) == low).astype(F32).astype(BF16)
        total = jnp.zeros((CHANNELS, tile), F32)
        for block in range(pixels // 256):
            found = dot(map_ref[view, :, 256 * block : 256 * (block + 1)], picked)
            total = jnp.where(high[:CHANNELS] == block, found, total)
        total = jnp.concatenate([total, jnp.zeros((STRIP - CHANNELS, tile), F32)], axis=0)
        seen = jnp.broadcast_to(vis_ref[view : view + 1, :].astype(F32), (STRIP, tile))
        total = jnp.where(row == CHANNELS, 1.0, total)
        total = jnp.where(row == CHANNELS + 1, seen, total)
        strips.append(total)
    out_ref[0] = jnp.concatenate(strips, axis=0).astype(BF16)


def gather_rows(pix, vis, maps, me, group):
    views, points = pix.shape
    tile = 256
    own = points // group
    return pl.pallas_call(
        lambda me_ref, *refs: gather_kernel(views, tile, *refs),
        out_shape=jax.ShapeDtypeStruct((group, views * STRIP, own), BF16),
        grid_spec=pltpu.PrefetchScalarGridSpec(
            num_scalar_prefetch=1,
            grid=(group, own // tile),
            in_specs=[
                pl.BlockSpec((views, tile), lambda k, t, me: (0, (me[0] ^ k) * (own // tile) + t)),
                pl.BlockSpec((views, tile), lambda k, t, me: (0, (me[0] ^ k) * (own // tile) + t)),
                pl.BlockSpec(maps.shape, lambda k, t, me: (0, 0, 0)),
            ],
            out_specs=pl.BlockSpec((1, views * STRIP, tile), lambda k, t, me: (k, 0, t)),
        ),
    )(me, pix, vis, maps)


def roll(value, shift):
    return pltpu.roll(value, shift % 128, 1)


def unpack(a_ref, r64, r32, r16):
    for b in range(2):
        r64[pl.ds(b, 18, stride=2), :] = roll(a_ref[0:18, :], -64 * b)
    for b in range(4):
        r32[pl.ds(b, 33, stride=4), :] = roll(a_ref[18:51, :], -32 * b)
    for b in range(8):
        r16[pl.ds(b, 39, stride=8), :] = roll(a_ref[50:89, :], -16 * b)


def column(rows):
    return rows.T[:, 0:1]


def main_kernel(
    views,
    ray_base,
    me_ref,
    x0,
    x1,
    x2,
    x3,
    a_ref,
    delta_ref,
    target_ref,
    weight_ref,
    out_ref,
    r64,
    r32,
    r16,
    xs,
    hb,
    he,
    ff,
    fe,
    jb,
    ib,
    ie,
    ee,
    blk,
    w2s,
    u1s,
    tri_s,
    g64,
    g32,
    g16,
    gw1,
    gb2,
    gc1,
    gc2,
    gd1,
    gs2,
    gdd,
    loss_s,
):
    step = pl.program_id(0)
    n = CHUNK
    lane = iota((1, n), 1)
    first_ray = lane < RAY
    me = me_ref[0]

    @pl.when(step == 0)
    def _():
        unpack(a_ref, r64, r32, r16)
        for ref in (g64, g32, g16, gw1, gb2, gc1, gc2, gd1, gs2, gdd, loss_s):
            ref[...] = jnp.zeros_like(ref)
        before = (iota((n, n), 0) < iota((n, n), 1)) & (
            (iota((n, n), 0) < RAY) == (iota((n, n), 1) < RAY)
        )
        tri_s[...] = before.astype(F32).astype(BF16)
        w1t = jnp.where(iota((64, 128), 1) < 36, 1.0, 0.0) * jnp.concatenate(
            [r64[0:36, :], jnp.zeros((92, 128), F32)], axis=0
        ).T[:64]
        for view in range(views):
            blk[64 * view : 64 * (view + 1), :] = roll(w1t, STRIP * view).astype(BF16)

    for k, ref in enumerate((x0, x1, x2, x3)):
        xs[me ^ k] = ref[0]

    w2 = r32[0:64, :][:, :32]
    w2b = w2.astype(BF16)
    w2t = w2.T.astype(BF16)
    b2 = column(r32[64:72, :])[:32]
    u1 = r32[65:129, :][:, :32]
    u1b = u1.astype(BF16)
    u1at = u1[:32].T.astype(BF16)
    u1bt = u1[32:].T.astype(BF16)
    c1 = column(r32[129:137, :])[:32]
    u2 = r16[4:36, :][:, :16]
    u2b = u2.astype(BF16)
    u2t = u2.T.astype(BF16)
    c2 = column(r16[36:44, :])[:16]
    keep16 = iota((48, 128), 1) < 16
    qkv = sum(
        roll(jnp.where(keep16, r16[pl.ds(37 + a, 48, stride=4), :], 0.0), 16 * a) for a in range(4)
    )
    wq, wk, wv = qkv[0:16], qkv[16:32], qkv[32:48]
    wqb = wq[:, :64].astype(BF16)
    wqt = wq[:, :64].T.astype(BF16)
    wk_of = [roll(wk, 64 * r).astype(BF16) for r in range(2)]
    wv_of = [roll(wv, 64 * r).astype(BF16) for r in range(2)]
    wo = r16[229:293, :][:, :16]
    wob = wo.astype(BF16)
    wot = wo.T.astype(BF16)
    s1 = r16[293:309, :][:, :16]
    s1b = s1.astype(BF16)
    s1t = s1.T.astype(BF16)
    d1 = column(r16[309:317, :])[:16]
    s2 = column(r16[310:318, :])[:16]
    d2 = r16[311:312, 0:1]

    def seen_of(view):
        at = STRIP * (view % views)
        return xs[view // views, at : at + STRIP, :].astype(F32)

    sum1 = jnp.zeros((32, n), F32)
    sum2 = jnp.zeros((32, n), F32)
    seen = jnp.zeros((1, n), F32)
    for group in range(-(-SEEN_VIEWS // views)):
        count = min(views, SEEN_VIEWS - group * views)
        pre = dot(blk[0 : 64 * count, 0 : views * STRIP], xs[group])
        for local in range(count):
            view = group * views + local
            value, slope = elu_pair(pre[64 * local : 64 * (local + 1)])
            hidden = value.astype(BF16)
            hb[view] = hidden
            he[view] = slope
            value, slope = elu_pair(dot(w2t, hidden) + b2)
            ff[view] = value
            fe[view] = slope
            vis = seen_of(view)[CHANNELS + 1 : CHANNELS + 2]
            part = vis * value
            sum1 = sum1 + part
            sum2 = sum2 + part * value
            seen = seen + vis
    average = sum1 / seen
    variance = sum2 / seen - average * average
    variance_low = variance.astype(BF16)
    shared = dot(u1bt, variance_low) + c1
    num = jnp.zeros((16, n), F32)
    den = jnp.zeros((16, n), F32)
    col = jnp.zeros((3, n), F32)
    for view in range(SEEN_VIEWS):
        strip = seen_of(view)
        feature = ff[view]
        joined = (feature - average).astype(BF16)
        jb[view] = joined
        value, slope = elu_pair(dot(u1at, joined) + shared)
        inner = value.astype(BF16)
        ib[view] = inner
        ie[view] = slope
        e = strip[CHANNELS + 1 : CHANNELS + 2] * jnp.exp(dot(u2t, inner) + c2)
        ee[view] = e
        num = num + e * feature[:16]
        den = den + e
        col = col + e[0:1] * strip[32:35]

    inv = 1.0 / den
    tokens = num / den
    colour = col / den[0:1]
    token_low = tokens.astype(BF16)
    token_t = tokens.T.astype(BF16)
    halves = [token_t[RAY * r : RAY * (r + 1)] for r in range(2)]
    query = dot(wqt, token_low).astype(BF16)
    kk_f = dot(halves[0], wk_of[0]) + dot(halves[1], wk_of[1])
    vv_f = dot(halves[0], wv_of[0]) + dot(halves[1], wv_of[1])
    kk = kk_f.astype(BF16)
    vv = vv_f.astype(BF16)
    kkt = kk.astype(F32).T.astype(BF16)
    vvt = vv.astype(F32).T.astype(BF16)
    row64 = iota((64, n), 0)

    def spread(value, head):
        mine = jnp.where((row64 >> 4) == head, value.astype(F32), 0.0)
        one = jnp.where(first_ray, mine, 0.0)
        return jnp.concatenate([one, mine - one], axis=0)

    def fold(value):
        return jnp.where(first_ray, value[:16], value[16:])

    def head_rows(value, head):
        at = 16 * head
        return jnp.concatenate([value[at : at + 16], value[64 + at : 80 + at]], axis=0)

    probs = []
    attended = []
    query_of = []
    for head in range(4):
        q_head = spread(query, head).astype(BF16)
        query_of.append(q_head)
        score = dot(kk, q_head) * 0.25
        score = jnp.exp(score - jnp.max(score, axis=0, keepdims=True))
        prob = score / jnp.sum(score, axis=0, keepdims=True)
        probs.append(prob)
        attended.append(fold(dot(head_rows(vvt, head), prob.astype(BF16))))
    attended = jnp.concatenate(attended, axis=0).astype(BF16)
    mixed = tokens + dot(wot, attended)
    mixed_low = mixed.astype(BF16)
    value, s_slope = elu_pair(dot(s1t, mixed_low) + d1)
    act = value.astype(BF16).astype(F32)
    z = jnp.sum(act * s2, axis=0, keepdims=True) + d2
    delta = delta_ref[0]
    ez = jnp.exp(-jnp.abs(z))
    density = jnp.maximum(z, 0.0) + jnp.log1p(ez)
    sigmoid = jnp.where(z >= 0.0, 1.0, ez) / (1.0 + ez)
    optical = density * delta
    tri = tri_s[...]

    def exact_rows(value):
        pad = jnp.zeros((13, n), F32)
        return jnp.concatenate([p.astype(F32) for p in parts(value, 3)] + [pad], axis=0).astype(BF16)

    before = jnp.sum(dot(exact_rows(optical), tri), axis=0, keepdims=True)
    through = jnp.exp(-before)
    gone = jnp.exp(-optical)
    render = through * (1.0 - gone)
    drawn = render * colour
    targets = target_ref[0]
    rweight = weight_ref[0]
    d_pixel = jnp.zeros((3, n), F32)
    loss = jnp.zeros((1, 1), F32)
    for r in range(2):
        mask = first_ray if r == 0 else jnp.logical_not(first_ray)
        pixel = jnp.sum(jnp.where(mask, drawn, 0.0), axis=1, keepdims=True)
        miss = pixel - targets[0:3, r : r + 1]
        scale = rweight[0:1, r : r + 1]
        loss = loss + scale * jnp.sum(miss * miss, axis=0, keepdims=True)
        d_pixel = d_pixel + jnp.where(mask, 2.0 * scale * miss, 0.0)
    place = iota((8, 128), 1) + 128 * iota((8, 128), 0)
    loss_s[...] += jnp.where(place == 0, loss, 0.0) + jnp.where(
        place == 1, rweight[0:1, 0:1] + rweight[0:1, 1:2], 0.0
    )

    d_render = jnp.sum(d_pixel * colour, axis=0, keepdims=True)
    d_colour = d_pixel * render
    d_before = -render * d_render
    d_optical = through * gone * d_render + jnp.sum(
        dot(exact_rows(d_before), tri, NT), axis=0, keepdims=True
    )
    dz = d_optical * delta * sigmoid
    gs2[...] += act * dz
    gdd[...] += jnp.where(iota((8, n), 0) == 0, dz, 0.0)
    d_pre = s2 * dz * s_slope
    gd1[...] += d_pre
    g16[293:309, :] += widen(dot_right(mixed_low, d_pre, NT))
    d_mixed = dot_right(s1b, d_pre, NN)
    g16[229:293, :] += widen(dot_right(attended, d_mixed, NT))
    d_att = dot_right(wob, d_mixed, NN)
    d_query = []
    d_kk = jnp.zeros((RAY, 128), F32)
    d_vv = jnp.zeros((RAY, 128), F32)
    for head in range(4):
        prob = probs[head]
        d_head = parts(spread(d_att, head), PASSES)
        d_prob = sum(dot(vv, piece) for piece in d_head)
        low = prob.astype(BF16)
        d_vv = d_vv + sum(dot(low, piece, NT) for piece in d_head)
        d_score = prob * (d_prob - jnp.sum(prob * d_prob, axis=0, keepdims=True)) * 0.25
        pieces = parts(d_score, PASSES)
        d_query.append(fold(sum(dot(head_rows(kkt, head), piece) for piece in pieces)))
        d_kk = d_kk + sum(dot(piece, query_of[head], NT) for piece in pieces)
    d_query = jnp.concatenate(d_query, axis=0)
    gq = dot_right(token_low, d_query, NT)
    gk = [dot_right(halves[r], d_kk, TN) for r in range(2)]
    gv = [dot_right(halves[r], d_vv, TN) for r in range(2)]
    wide = jnp.concatenate([widen(gq), gk[0] + roll(gk[1], 64), gv[0] + roll(gv[1], 64)], axis=0)
    for a in range(4):
        at = pl.ds(37 + a, 48, stride=4)
        g16[at, :] += jnp.where(keep16, roll(wide, -16 * a), 0.0)
    d_halves = [
        dot_left(d_kk, wk_of[r], NT) + dot_left(d_vv, wv_of[r], NT) for r in range(2)
    ]
    d_tokens = d_mixed + dot_right(wqb, d_query, NN) + jnp.concatenate(d_halves, axis=0).T
    d_num = d_tokens * inv
    d_den = -d_num * tokens
    d_col = d_colour * inv[0:1]
    d_den0 = -jnp.sum(d_col * colour, axis=0, keepdims=True)
    row16 = iota((16, n), 0)
    d_den = d_den + jnp.where(row16 == 0, d_den0, 0.0)

    d_average = jnp.zeros((32, n), F32)
    d_shared = jnp.zeros((32, n), F32)
    sum_c2 = jnp.zeros((16, n), F32)
    grad_u2 = jnp.zeros((32, 16), F32)
    grad_u1 = jnp.zeros((32, 32), F32)
    for view in range(SEEN_VIEWS):
        strip = seen_of(view)
        e = ee[view]
        feature = ff[view]
        d_e = d_num * feature[:16] + d_den
        d_e = d_e + jnp.where(
            row16 == 0, jnp.sum(d_col * strip[32:35], axis=0, keepdims=True), 0.0
        )
        d_logit = d_e * e
        sum_c2 = sum_c2 + d_logit
        pieces = parts(d_logit, PASSES)
        grad_u2 = grad_u2 + sum(dot(ib[view], piece, NT) for piece in pieces)
        d_inner = sum(dot(u2b, piece) for piece in pieces) * ie[view]
        d_shared = d_shared + d_inner
        pieces = parts(d_inner, PASSES)
        grad_u1 = grad_u1 + sum(dot(jb[view], piece, NT) for piece in pieces)
        d_joined = sum(dot(u1b[:32], piece) for piece in pieces)
        d_average = d_average - d_joined
        ee[view] = d_num * e
        ie[view] = d_joined
    pieces = parts(d_shared, PASSES)
    d_variance = sum(dot(u1b[32:], piece) for piece in pieces)
    g16[4:36, :] += widen(grad_u2)
    g32[65:97, :] += widen(grad_u1)
    g32[97:129, :] += widen(sum(dot(variance_low, piece, NT) for piece in pieces))
    gc1[...] += d_shared
    gc2[...] += sum_c2
    inv_seen = 1.0 / seen
    d_square = d_variance * inv_seen
    d_sum = (d_average - 2.0 * average * d_variance) * inv_seen

    grad_w2 = jnp.zeros((64, 32), F32)
    sum_b2 = jnp.zeros((32, n), F32)
    for group in range(-(-SEEN_VIEWS // views)):
        count = min(views, SEEN_VIEWS - group * views)
        d_hidden = []
        for local in range(count):
            view = group * views + local
            vis = seen_of(view)[CHANNELS + 1 : CHANNELS + 2]
            d_feature = ie[view] + vis * (d_sum + 2.0 * ff[view] * d_square)
            d_feature = d_feature + jnp.concatenate([ee[view], jnp.zeros((16, n), F32)], axis=0)
            d_feature = d_feature * fe[view]
            sum_b2 = sum_b2 + d_feature
            pieces = parts(d_feature, PASSES)
            grad_w2 = grad_w2 + sum(dot(hb[view], piece, NT) for piece in pieces)
            d_hidden.append(sum(dot(w2b, piece) for piece in pieces) * he[view])
        d_hidden = jnp.concatenate(d_hidden, axis=0)
        gw1[:, 0 : 64 * count] += dot_right(xs[group], d_hidden, NT)
    g32[0:64, :] += widen(grad_w2)
    gb2[...] += sum_b2

    @pl.when(step == pl.num_programs(0) - 1)
    def _():
        ones = jnp.ones((8, n), BF16)
        row_of = lambda ref: widen(dot_right(ones, ref[...], NT, 3)[0:1])
        g32[64:65, :] = row_of(gb2)
        g32[129:130, :] = row_of(gc1)
        g16[36:37, :] = row_of(gc2)
        g16[309:310, :] = row_of(gd1)
        g16[310:311, :] = row_of(gs2)
        g16[311:312, :] = jnp.where(iota((1, 128), 1) == 0, row_of(gdd), 0.0)
        total = gw1[0:36, 0:128]
        total = total + roll(gw1[STRIP : STRIP + 36, 0:128], 64)
        total = total + gw1[2 * STRIP : 2 * STRIP + 36, 128:256]
        g64[0:36, :] = jnp.where(iota((36, 128), 1) < 64, total, 0.0)
        out_ref[...] = jnp.zeros_like(out_ref)
        out_ref[0:18, :] = sum(roll(g64[pl.ds(b, 18, stride=2), :], 64 * b) for b in range(2))
        out_ref[18:51, :] += sum(roll(g32[pl.ds(b, 33, stride=4), :], 32 * b) for b in range(4))
        out_ref[50:89, :] += sum(roll(g16[pl.ds(b, 39, stride=8), :], 16 * b) for b in range(8))
        out_ref[96:104, :] = loss_s[...]


def widen(value):
    rows, width = value.shape
    return jnp.concatenate([value, jnp.zeros((rows, 128 - width), F32)], axis=1)


def run_main(me, blocks, weights, deltas, targets, ray_weight, ray_base=None):
    rows, points = blocks[0].shape[1:]
    views = rows // STRIP
    n = CHUNK
    steps = points // n
    v = SEEN_VIEWS
    pairs = deltas.reshape(steps, 1, n)
    target_pairs = jnp.pad(
        targets.reshape(steps, 2, 3).transpose(0, 2, 1), ((0, 0), (0, 5), (0, 126))
    )
    weight_pairs = jnp.pad(ray_weight.reshape(steps, 1, 2), ((0, 0), (0, 7), (0, 126)))
    vm = pltpu.VMEM
    order = [k if blocks[k].shape[0] > 1 else 0 for k in range(len(blocks))]
    block = lambda k: pl.BlockSpec((1, rows, n), lambda t, me: (order[k], 0, t))
    return pl.pallas_call(
        lambda *refs: main_kernel(views, 0, *refs),
        out_shape=jax.ShapeDtypeStruct((104, 128), F32),
        grid_spec=pltpu.PrefetchScalarGridSpec(
            num_scalar_prefetch=1,
            grid=(steps,),
            in_specs=[block(k) for k in range(4)]
            + [
                pl.BlockSpec(weights.shape, lambda t, me: (0, 0)),
                pl.BlockSpec((1, 1, n), lambda t, me: (t, 0, 0)),
                pl.BlockSpec((1, 8, 128), lambda t, me: (t, 0, 0)),
                pl.BlockSpec((1, 8, 128), lambda t, me: (t, 0, 0)),
            ],
            out_specs=pl.BlockSpec((104, 128), lambda t, me: (0, 0)),
            scratch_shapes=[
                vm((40, 128), F32),
                vm((144, 128), F32),
                vm((320, 128), F32),
                vm((4, rows, n), BF16),
                vm((v, 64, n), BF16),
                vm((v, 64, n), F32),
                vm((v, 32, n), F32),
                vm((v, 32, n), F32),
                vm((v, 32, n), BF16),
                vm((v, 32, n), BF16),
                vm((v, 32, n), F32),
                vm((v, 16, n), F32),
                vm((64 * views, 128), BF16),
                vm((8, 128), BF16),
                vm((8, 128), BF16),
                vm((n, n), BF16),
                vm((40, 128), F32),
                vm((136, 128), F32),
                vm((312, 128), F32),
                vm((rows, 256), F32),
                vm((32, n), F32),
                vm((32, n), F32),
                vm((16, n), F32),
                vm((16, n), F32),
                vm((16, n), F32),
                vm((8, n), F32),
                vm((8, 128), F32),
            ],
        ),
        compiler_params=pltpu.CompilerParams(vmem_limit_bytes=48 * 1024 * 1024),
    )(me, *blocks, weights, pairs, target_pairs, weight_pairs)


def adamw(master, first_moment, second_moment, gradient, step_count):
    step_float = step_count[0].astype(F32)
    first_new = MOMENT_DECAY * first_moment + (1.0 - MOMENT_DECAY) * gradient
    second_new = SQUARE_DECAY * second_moment + (1.0 - SQUARE_DECAY) * gradient * gradient
    first_fix = 1.0 - jnp.power(MOMENT_DECAY, step_float)
    second_fix = 1.0 - jnp.power(SQUARE_DECAY, step_float)
    update = first_new / first_fix / (jnp.sqrt(second_new / second_fix) + EPSILON)
    master_new = master - LEARNING_RATE * (update + WEIGHT_DECAY * master)
    return (master_new, first_new, second_new)


def body(
    master,
    first_moment,
    second_moment,
    step_count,
    feature_maps,
    pixel_index,
    visible,
    deltas,
    targets,
    scene_id,
    scene_weight,
):
    group = lax.axis_size("views")
    shards = lax.axis_size("rays")
    rays = deltas.shape[0]
    own = rays // group
    shard = master.shape[0]
    spot = lax.axis_index("views")
    me = spot.astype(jnp.int32).reshape(1)
    hits = (scene_id[:, None] == jnp.arange(scene_weight.shape[0])[None, :]).astype(F32)
    ray_weight = jnp.sum(hits * scene_weight.astype(F32)[None, :], axis=1)
    narrow = lax.all_gather(master.astype(BF16), "rays", axis=0, tiled=True)
    flat = narrow.astype(F32)[:11384]
    weights = jnp.pad(flat, (0, 96 * 128 - flat.shape[0])).reshape(96, 128)
    rows = gather_rows(pixel_index.T, visible.T, feature_maps, me, group)
    blocks = [rows]
    for k in range(1, group):
        pairs = [(i, i ^ k) for i in range(group)]
        blocks.append(lax.ppermute(rows[k : k + 1], "views", pairs))
    mine = lambda array: lax.dynamic_slice_in_dim(array, spot * own, own, 0)
    packed = run_main(me, blocks, weights, mine(deltas), mine(targets), mine(ray_weight))
    summed = packed[:89].reshape(-1)
    size = shards * shard
    if summed.shape[0] < size:
        summed = jnp.pad(summed, (0, size - summed.shape[0]))
    extra = jnp.broadcast_to(packed[96, :2][None], (shards, 2))
    send = jnp.concatenate([summed[:size].reshape(shards, shard), extra], axis=1)
    got = lax.all_to_all(send, "rays", 0, 0, tiled=True)
    partial = jnp.sum(got, axis=0)
    whole = partial
    for k in range(1, group):
        whole = whole + lax.ppermute(partial, "views", [(i, i ^ k) for i in range(group)])
    seed = 1.0 / whole[shard + 1]
    loss = whole[shard] * seed
    gradient = whole[:shard] * seed
    return (loss, *adamw(master, first_moment, second_moment, gradient, step_count))


def solution(mesh):
    placed = (
        P("rays"),
        P("rays"),
        P("rays"),
        P(),
        P("views", None, None),
        P("rays", "views"),
        P("rays", "views"),
        P("rays", None),
        P("rays", None),
        P("rays"),
        P(),
    )
    return jax.shard_map(
        body,
        mesh=mesh,
        in_specs=placed,
        out_specs=(P(), P("rays"), P("rays"), P("rays")),
        check_vma=False,
    )
```

time: 699 us -> 128 us (0.18); the launches traced: 687 us -> 128 us
  local copies, waits for them, and re-layouts: 223 us -> 4.51 us
  matrix products: 148 us -> 0 us
  other arithmetic: 117 us -> 0.79 us
  blocking collectives: 148 us -> 46.8 us
  Pallas kernels: 0 us -> 65.1 us
  waiting for transfers between devices: 29 us -> 1.18 us
  between operations: 23.1 us -> 4.64 us
    dot_general x84 -> x0, matrix products: 148 us -> none  [the longest x68 71.3 us: matmul_low(): return jnp.matmul(left_op, right_op, precision=lax.Precision.HIGHEST)]
    gather x6 -> x0, local copies, waits for them, and re-layouts: 135 us -> none  [body(): feature_maps[view_slot, :, pixel_index[start:start + point_rows]]]
    psum x5 -> x0, blocking collectives: 109 us -> none  [the longest x1 37.6 us: body(): loss = lax.psum(loss_part, 'rays') * seed]
    pallas_call x0 -> x2, Pallas kernels: none -> 65.1 us  [the longest x1 42.9 us: gather_rows(): pl.pallas_call(lambda me_ref, *refs: gather_kernel(views, tile, *refs), o...]
    reduce_sum x22 -> x2, other arithmetic: 53.2 us -> 0.13 us  [the longest x1 0.08 us: body(): ray_weight = jnp.sum(hits * scene_weight.astype(F32)[None, :], axis=1)]
    reshape x56 -> x5, local copies, waits for them, and re-layouts: 42.8 us -> 0.36 us  [the longest x1 0.1 us: run_main(): targets.reshape(steps, 2, 3).transpose(0, 2, 1)]
    psum x3 -> x0, waiting for transfers between devices: 29 us -> none  [the longest x1 29 us: body(): lax.psum(own_gsum.astype(jnp.bfloat16), 'views').astype(jnp.float32)]
    sub x6 -> x0, other arithmetic: 23.6 us -> none  [the longest x4 21.2 us: ray_part(): attention = rounded(jax.nn.softmax(scores, axis=-1), ledger)]
  transfers between devices with their start and end apart: 3 -> 6, of which waited for: 1 -> 2; matrix products, arithmetic and copies ran while one was open for 4% -> 1% of each run, Pallas kernels for 0% -> 0%
where the time goes in v1:
time: 128 us
  Pallas kernels  65.1 us (51%)
  blocking collectives  46.8 us (37%)
  starting transfers between devices  5.09 us (4%)
  between operations  4.64 us (4%)
  local copies, waits for them, and re-layouts  4.51 us (4%)
    pallas_call x1, Pallas kernels, gather_rows(): pl.pallas_call(lambda me_ref, *refs: gather_kernel(views, tile, *refs), o...  42.9 us
    unnamed x1, blocking collectives  37.6 us
    pallas_call x1, Pallas kernels, run_main(): pl.pallas_call(lambda *refs: main_kernel(views, 0, *refs), out_shape=jax....  22.2 us
    all_to_all x1, blocking collectives, body(): got = lax.all_to_all(send, 'rays', 0, 0, tiled=True)  9.17 us
    ppermute x3, starting transfers between devices, body(): blocks.append(lax.ppermute(rows[k:k + 1], 'views', pairs))  3.18 us
  transfers between devices with their start and end apart: 6, of which 2 were waited for; matrix products, arithmetic and copies ran while one was open for 1% of the time, Pallas kernels for 0%

profile of v1, /device:TPU:0, one launch (start us, length us, event | category | flops | bytes accessed | tf_op | source)
XLA Modules:
  0.0 128.1 jit_solution(17898482848064228908)
XLA Ops:
  0.6 0.0 copy-start
  0.6 0.0 copy-start.8
  0.7 0.0 copy-start.2
  0.7 0.0 copy-start.5
  0.7 0.0 copy-start.6
  0.7 0.0 copy-start.7
  0.7 0.0 copy-start.3
  0.7 0.0 copy-start.4
  0.7 42.9 %shard_map.138.refs_1_ = bf16[4,120,768]{2,1,0:T(8,128)(2,1)} custom-call(s32[1]{0:T(128)} %bitcast.me_ref.refs_0_, s32[3,3072]{1,0:T(4,128)} %bitcast.19, s32[3,3072]{1,0:T(4,128)} %bitcast.20, bf16[3,35,12032]{2,1,0:T(8,128)(2,1)} %refs_2_.1), custom_call_target="tpu_custom_call" | custom-call | tf_op jit(solution)/shard_map/pallas_call | solution.py:82
  43.6 1.1 fusion.2
  44.7 0.6 collective-permute-start
  45.3 2.6 %collective-permute-start.1 = (bf16[1,120,768]{2,1,0:T(8,128)(2,1)S(1)}, bf16[1,120,768]{2,1,0:T(8,128)(2,1)S(1)}, u32[]{:S(2)}, u32[]{:S(2)}) collective-permute-start(bf16[1,120,768]{2,1,0:T(8,128)(2,1)S(1)} %get-tuple-element.8), channel_id=1, source_target_pairs={{0,2},{1,3},{2,0},{3,1},{4,6},{5,7},{6,4},{7,5},{8,10},{9,11},{10,... | collective-permute-start | bytes 552968 | tf_op jit(solution)/shard_map/ppermute | solution.py:565
  47.9 0.0 collective-permute-start.2
  47.9 0.0 copy-done.2
  47.9 0.0 copy-done
  47.9 0.1 reshape.45.refs_6_
  48.0 0.0 copy-done.5
  48.0 0.1 constant_dynamic-slice_fusion
  48.1 0.1 copy.21
  48.2 0.1 copy.22
  48.3 0.0 copy-done.6
  48.3 0.0 copy-done.7
  48.3 0.1 select_reduce_fusion
  48.4 0.1 dynamic_slice.11
  48.5 0.1 reshape.47
  48.6 0.0 copy-done.8
  48.6 0.6 dynamic-slice
  49.8 0.3 dynamic-update-slice
  50.1 37.6 %all-reduce.3 = bf16[11384]{0:T(1024)(128)(2,1)S(1)} all-reduce(bf16[11384]{0:T(1024)(128)(2,1)S(1)} %dynamic-update-slice), channel_id=1, replica_groups=mesh['rays'=8,'views'=4] {'rays'}, use_global_device_ids=true, to_apply=%add.3 | all-reduce | flops 11384 | bytes 45536
  87.7 0.0 collective-permute-done.refs_2_
  87.7 0.0 collective-permute-done.1.refs_3_
  87.7 0.0 collective-permute-done.2.refs_4_
  87.7 0.0 copy-start.1
  87.8 1.1 copy-done.1
  88.9 22.2 %shard_map.139 = f32[104,128]{1,0:T(8,128)S(1)} custom-call(s32[1]{0:T(128)} %bitcast.me_ref.refs_0_, bf16[4,120,768]{2,1,0:T(8,128)(2,1)S(1)} %copy-done.1, bf16[1,120,768]{2,1,0:T(8,128)(2,1)S(1)} %collective-permute-done.refs_2_, bf16[1,120,768]{2,1,0:T(8,128)(2,1)S(1)} %collective-permute-done.1.refs_3_, ...), custom_call_target="tpu_custom_call" | custom-call | tf_op jit(solution)/shard_map/pallas_call | solution.py:477
  111.1 0.1 reshape.49
  111.2 0.1 pad.17.clone
  111.3 9.2 %all_to_all.9 = f32[8,1,1425]{2,1,0:T(1,128)S(1)} all-to-all(f32[8,1,1425]{2,1,0:T(1,128)S(1)} %all_to_all.6), channel_id=1, replica_groups=mesh['rays'=8,'views'=4] {'rays'}, dimensions={0} | all-to-all | bytes 91200 | tf_op jit(solution)/shard_map/all_to_all | solution.py:574
  120.5 0.1 collective-permute-start.5
  120.6 1.6 %collective-permute-start.4 = (f32[1425]{0:T(1024)S(1)}, f32[1425]{0:T(1024)S(1)}, u32[]{:S(2)}, u32[]{:S(2)}) collective-permute-start(f32[1425]{0:T(1024)S(1)} %reduce_sum.19), channel_id=1, source_target_pairs={{0,2},{1,3},{2,0},{3,1},{4,6},{5,7},{6,4},{7,5},{8,10},{9,11},{10,... | collective-permute-start | bytes 17108 | tf_op jit(solution)/shard_map/ppermute | solution.py:578
  122.2 0.3 collective-permute-start.3
  123.2 0.5 collective-permute-done.5
  123.7 0.6 collective-permute-done.4
  124.3 0.0 collective-permute-done.3
  124.4 0.6 fusion.3
  126.3 0.0 copy-done.3
  126.3 0.0 copy-done.4
  126.3 0.6 multiply_subtract_fusion
  (13 shorter events, 0.1 us)
Async XLA Ops:
  0.6 47.3 %copy-start = (f32[16,192]{1,0:T(8,128)S(1)}, f32[16,192]{1,0:T(8,128)}, u32[]{:S(2)}) copy-start(f32[16,192]{1,0:T(8,128)} %param.18) | copy-start | bytes 36868
  0.6 47.9 %copy-start.8 = (u32[32]{0:T(128)S(1)}, u32[32]{0:T(128)}, u32[]{:S(2)}) copy-start(u32[32]{0:T(128)} %constant.45) | copy-start | bytes 388
  0.7 47.2 %copy-start.2 = (f32[1423]{0:T(1024)S(1)}, f32[1423]{0:T(1024)}, u32[]{:S(2)}) copy-start(f32[1423]{0:T(1024)} %param.11) | copy-start | bytes 17080
  0.7 47.3 %copy-start.5 = (f32[16,3]{0,1:T(4,128)S(1)}, f32[16,3]{0,1:T(4,128)}, u32[]{:S(2)}) copy-start(f32[16,3]{0,1:T(4,128)} %param.19) | copy-start | bytes 580
  0.7 47.6 %copy-start.6 = (s32[8]{0:T(128)S(1)}, s32[8]{0:T(128)}, u32[]{:S(2)}) copy-start(s32[8]{0:T(128)} %param.21) | copy-start | bytes 100
  0.7 47.6 %copy-start.7 = (s32[16]{0:T(128)S(1)}, s32[16]{0:T(128)}, u32[]{:S(2)}) copy-start(s32[16]{0:T(128)} %param.20) | copy-start | bytes 196
  0.7 125.6 %copy-start.3 = (f32[1423]{0:T(1024)S(1)}, f32[1423]{0:T(1024)}, u32[]{:S(2)}) copy-start(f32[1423]{0:T(1024)} %param.13) | copy-start | bytes 17080
  0.7 125.6 %copy-start.4 = (f32[1423]{0:T(1024)S(1)}, f32[1423]{0:T(1024)}, u32[]{:S(2)}) copy-start(f32[1423]{0:T(1024)} %param.12) | copy-start | bytes 17080
  44.7 43.0 %collective-permute-start = (bf16[1,120,768]{2,1,0:T(8,128)(2,1)S(1)}, bf16[1,120,768]{2,1,0:T(8,128)(2,1)S(1)}, u32[]{:S(2)}, u32[]{:S(2)}) collective-permute-start(bf16[1,120,768]{2,1,0:T(8,128)(2,1)S(1)} %get-tuple-element.9), channel_id=1, source_target_pairs={{0,1},{1,0},{2,3},{3,2},{4,5},{5,4},{6,7},{7,6},{8,9},{9,8},{10,11... | collective-permute-start | bytes 552968 | tf_op jit(solution)/shard_map/ppermute | solution.py:565
  45.3 42.4 %collective-permute-start.1 = (bf16[1,120,768]{2,1,0:T(8,128)(2,1)S(1)}, bf16[1,120,768]{2,1,0:T(8,128)(2,1)S(1)}, u32[]{:S(2)}, u32[]{:S(2)}) collective-permute-start(bf16[1,120,768]{2,1,0:T(8,128)(2,1)S(1)} %get-tuple-element.8), channel_id=1, source_target_pairs={{0,2},{1,3},{2,0},{3,1},{4,6},{5,7},{6,4},{7,5},{8,10},{9,11},{10,... | collective-permute-start | bytes 552968 | tf_op jit(solution)/shard_map/ppermute | solution.py:565
  47.9 39.9 %collective-permute-start.2 = (bf16[1,120,768]{2,1,0:T(8,128)(2,1)S(1)}, bf16[1,120,768]{2,1,0:T(8,128)(2,1)S(1)}, u32[]{:S(2)}, u32[]{:S(2)}) collective-permute-start(bf16[1,120,768]{2,1,0:T(8,128)(2,1)S(1)} %get-tuple-element.7), channel_id=1, source_target_pairs={{0,3},{1,2},{2,1},{3,0},{4,7},{5,6},{6,5},{7,4},{8,11},{9,10},{10,... | collective-permute-start | bytes 552968 | tf_op jit(solution)/shard_map/ppermute | solution.py:565
  87.7 1.1 copy-start.1
  120.5 3.2 %collective-permute-start.5 = (f32[1425]{0:T(1024)S(1)}, f32[1425]{0:T(1024)S(1)}, u32[]{:S(2)}, u32[]{:S(2)}) collective-permute-start(f32[1425]{0:T(1024)S(1)} %reduce_sum.19), channel_id=1, source_target_pairs={{0,3},{1,2},{2,1},{3,0},{4,7},{5,6},{6,5},{7,4},{8,11},{9,10},{10,... | collective-permute-start | bytes 17108 | tf_op jit(solution)/shard_map/ppermute | solution.py:578
  120.6 3.7 %collective-permute-start.4 = (f32[1425]{0:T(1024)S(1)}, f32[1425]{0:T(1024)S(1)}, u32[]{:S(2)}, u32[]{:S(2)}) collective-permute-start(f32[1425]{0:T(1024)S(1)} %reduce_sum.19), channel_id=1, source_target_pairs={{0,2},{1,3},{2,0},{3,1},{4,6},{5,7},{6,4},{7,5},{8,10},{9,11},{10,... | collective-permute-start | bytes 17108 | tf_op jit(solution)/shard_map/ppermute | solution.py:578
  122.2 2.1 %collective-permute-start.3 = (f32[1425]{0:T(1024)S(1)}, f32[1425]{0:T(1024)S(1)}, u32[]{:S(2)}, u32[]{:S(2)}) collective-permute-start(f32[1425]{0:T(1024)S(1)} %reduce_sum.19), channel_id=1, source_target_pairs={{0,1},{1,0},{2,3},{3,2},{4,5},{5,4},{6,7},{7,6},{8,9},{9,8},{10,11... | collective-permute-start | bytes 17108 | tf_op jit(solution)/shard_map/ppermute | solution.py:578

commit v2 on v1

--- a/solution.py
+++ b/solution.py
@@ -5,11 +5,14 @@
 from jax.experimental.pallas import tpu as pltpu
 from jax.sharding import PartitionSpec as P
 
+
 F32 = jnp.float32
 BF16 = jnp.bfloat16
 SEEN_VIEWS = 10
 CHANNELS = 35
 STRIP = 40
+BAND = 48
+GATHER_TILE = 256
 RAY = 192
 CHUNK = 2 * RAY
 PASSES = 2
@@ -54,45 +57,65 @@
     return lax.broadcasted_iota(jnp.int32, shape, axis)
 
 
-def gather_kernel(views, tile, pix_ref, vis_ref, map_ref, out_ref):
-    pixels = map_ref.shape[2]
-    strips = []
+def gather_kernel(views, tile, count, *refs):
+    pix_refs, vis_refs = refs[1 : 1 + count], refs[1 + count : 1 + 2 * count]
+    map_ref = refs[1 + 2 * count]
+    outs, stacked = refs[2 + 2 * count : -1], refs[-1]
+    blocks = map_ref.shape[2] // 256
+
+    @pl.when(pl.program_id(0) == 0)
+    def _():
+        for view in range(views):
+            for block in range(blocks):
+                stacked[view, BAND * block : BAND * block + CHANNELS, :] = map_ref[
+                    view, :, 256 * block : 256 * (block + 1)
+                ]
+
     row = iota((STRIP, tile), 0)
-    for view in range(views):
-        index = pix_ref[view : view + 1, :]
-        high = jnp.broadcast_to(index >> 8, (STRIP, tile))
-        low = jnp.broadcast_to(index & 255, (256, tile))
-        picked = (iota((256, tile), 0) == low).astype(F32).astype(BF16)
-        total = jnp.zeros((CHANNELS, tile), F32)
-        for block in range(pixels // 256):
-            found = dot(map_ref[view, :, 256 * block : 256 * (block + 1)], picked)
-            total = jnp.where(high[:CHANNELS] == block, found, total)
-        total = jnp.concatenate([total, jnp.zeros((STRIP - CHANNELS, tile), F32)], axis=0)
-        seen = jnp.broadcast_to(vis_ref[view : view + 1, :].astype(F32), (STRIP, tile))
-        total = jnp.where(row == CHANNELS, 1.0, total)
-        total = jnp.where(row == CHANNELS + 1, seen, total)
-        strips.append(total)
-    out_ref[0] = jnp.concatenate(strips, axis=0).astype(BF16)
-
-
-def gather_rows(pix, vis, maps, me, group):
+    for pix_ref, vis_ref, out_ref in zip(pix_refs, vis_refs, outs):
+        strips = []
+        for view in range(views):
+            index = pix_ref[view : view + 1, :]
+            high = jnp.broadcast_to(index >> 8, (STRIP, tile))
+            low = jnp.broadcast_to(index & 255, (256, tile))
+            picked = (iota((256, tile), 0) == low).astype(F32).astype(BF16)
+            found = dot(stacked[view], picked)
+            total = jnp.zeros((STRIP, tile), F32)
+            for block in range(blocks):
+                total = jnp.where(
+                    high == block, found[BAND * block : BAND * block + STRIP], total
+                )
+            seen = jnp.broadcast_to(vis_ref[view : view + 1, :].astype(F32), (STRIP, tile))
+            total = jnp.where(row == CHANNELS, 1.0, total)
+            total = jnp.where(row == CHANNELS + 1, seen, total)
+            total = jnp.where(row > CHANNELS + 1, 0.0, total)
+            strips.append(total)
+        out_ref[0] = jnp.concatenate(strips, axis=0).astype(BF16)
+
+
+def gather_rows(pix, vis, maps, me, group, ways):
     views, points = pix.shape
-    tile = 256
+    tile = GATHER_TILE
     own = points // group
+    tiles = own // tile
+    count = len(ways)
+    part = lambda k: pl.BlockSpec((views, tile), lambda t, me: (0, (me[0] ^ k) * tiles + t))
+    out = jax.ShapeDtypeStruct((1, views * STRIP, own), BF16)
+    flops = 2 * views * own * count * BAND * maps.shape[2]
     return pl.pallas_call(
-        lambda me_ref, *refs: gather_kernel(views, tile, *refs),
-        out_shape=jax.ShapeDtypeStruct((group, views * STRIP, own), BF16),
+        lambda *refs: gather_kernel(views, tile, count, *refs),
+        out_shape=[out] * count,
         grid_spec=pltpu.PrefetchScalarGridSpec(
             num_scalar_prefetch=1,
-            grid=(group, own // tile),
-            in_specs=[
-                pl.BlockSpec((views, tile), lambda k, t, me: (0, (me[0] ^ k) * (own // tile) + t)),
-                pl.BlockSpec((views, tile), lambda k, t, me: (0, (me[0] ^ k) * (own // tile) + t)),
-                pl.BlockSpec(maps.shape, lambda k, t, me: (0, 0, 0)),
-            ],
-            out_specs=pl.BlockSpec((1, views * STRIP, tile), lambda k, t, me: (k, 0, t)),
+            grid=(tiles,),
+            in_specs=[part(k) for k in ways] * 2
+            + [pl.BlockSpec(maps.shape, lambda t, me: (0, 0, 0))],
+            out_specs=[pl.BlockSpec((1, views * STRIP, tile), lambda t, me: (0, 0, t))] * count,
+            scratch_shapes=[pltpu.VMEM((views, BAND * (maps.shape[2] // 256), 256), BF16)],
         ),
-    )(me, pix, vis, maps)
+        compiler_params=pltpu.CompilerParams(vmem_limit_bytes=40 * 1024 * 1024),
+        cost_estimate=pl.CostEstimate(flops=flops, bytes_accessed=maps.size * 2, transcendentals=0),
+    )(me, *([pix] * count), *([vis] * count), maps)
 
 
 def roll(value, shift):
@@ -108,23 +131,35 @@
         r16[pl.ds(b, 39, stride=8), :] = roll(a_ref[50:89, :], -16 * b)
 
 
+def assemble(place, shard, shard_refs, a_ref):
+    a_ref[...] = jnp.zeros_like(a_ref)
+    shards, rows, _ = shard_refs.shape
+    for k in range(shards):
+        start = (place ^ k) * shard
+        shift = start & 127
+        value = pltpu.roll(shard_refs[k].astype(F32), shift, 1)
+        keep = iota((rows, 128), 1) >= shift
+        first = start >> 7
+        a_ref[pl.ds(first, rows), :] += jnp.where(keep, value, 0.0)
+        a_ref[pl.ds(first + 1, rows), :] += jnp.where(keep, 0.0, value)
+
+
 def column(rows):
     return rows.T[:, 0:1]
 
 
-def main_kernel(
-    views,
-    ray_base,
-    me_ref,
+def main_kernel(views, shard, me_ref, *refs):
+    shard_refs, refs = refs[0], refs[1:]
+    (
     x0,
     x1,
     x2,
     x3,
-    a_ref,
     delta_ref,
     target_ref,
     weight_ref,
     out_ref,
+    a_ref,
     r64,
     r32,
     r16,
@@ -138,8 +173,8 @@
     ie,
     ee,
     blk,
-    w2s,
-    u1s,
+    _,
+    _,
     tri_s,
     g64,
     g32,
@@ -152,7 +187,7 @@
     gs2,
     gdd,
     loss_s,
-):
+    ) = refs
     step = pl.program_id(0)
     n = CHUNK
     lane = iota((1, n), 1)
@@ -161,6 +196,7 @@
 
     @pl.when(step == 0)
     def _():
+        assemble(me_ref[1], shard, shard_refs, a_ref)
         unpack(a_ref, r64, r32, r16)
         for ref in (g64, g32, g16, gw1, gb2, gc1, gc2, gd1, gs2, gdd, loss_s):
             ref[...] = jnp.zeros_like(ref)
@@ -460,35 +496,38 @@
     return jnp.concatenate([value, jnp.zeros((rows, 128 - width), F32)], axis=1)
 
 
-def run_main(me, blocks, weights, deltas, targets, ray_weight, ray_base=None):
+def run_main(me, blocks, pieces, shard, deltas, targets, ray_weight):
     rows, points = blocks[0].shape[1:]
     views = rows // STRIP
     n = CHUNK
     steps = points // n
     v = SEEN_VIEWS
-    pairs = deltas.reshape(steps, 1, n)
+    whole = deltas.shape[0] // 2
+    pairs = deltas.reshape(whole, 1, n)
     target_pairs = jnp.pad(
-        targets.reshape(steps, 2, 3).transpose(0, 2, 1), ((0, 0), (0, 5), (0, 126))
+        targets.reshape(whole, 2, 3).transpose(0, 2, 1), ((0, 0), (0, 5), (0, 126))
     )
-    weight_pairs = jnp.pad(ray_weight.reshape(steps, 1, 2), ((0, 0), (0, 7), (0, 126)))
+    weight_pairs = jnp.pad(ray_weight.reshape(whole, 1, 2), ((0, 0), (0, 7), (0, 126)))
     vm = pltpu.VMEM
-    order = [k if blocks[k].shape[0] > 1 else 0 for k in range(len(blocks))]
-    block = lambda k: pl.BlockSpec((1, rows, n), lambda t, me: (order[k], 0, t))
+    own = lambda t, me: (me[0] * steps + t, 0, 0)
+    block = pl.BlockSpec((1, rows, n), lambda t, me: (0, 0, t))
+    piece = pl.BlockSpec(pieces.shape, lambda t, me: (0, 0, 0))
     return pl.pallas_call(
-        lambda *refs: main_kernel(views, 0, *refs),
+        lambda *refs: main_kernel(views, shard, *refs),
         out_shape=jax.ShapeDtypeStruct((104, 128), F32),
         grid_spec=pltpu.PrefetchScalarGridSpec(
             num_scalar_prefetch=1,
             grid=(steps,),
-            in_specs=[block(k) for k in range(4)]
+            in_specs=[piece]
+            + [block] * 4
             + [
-                pl.BlockSpec(weights.shape, lambda t, me: (0, 0)),
-                pl.BlockSpec((1, 1, n), lambda t, me: (t, 0, 0)),
-                pl.BlockSpec((1, 8, 128), lambda t, me: (t, 0, 0)),
-                pl.BlockSpec((1, 8, 128), lambda t, me: (t, 0, 0)),
+                pl.BlockSpec((1, 1, n), own),
+                pl.BlockSpec((1, 8, 128), own),
+                pl.BlockSpec((1, 8, 128), own),
             ],
             out_specs=pl.BlockSpec((104, 128), lambda t, me: (0, 0)),
             scratch_shapes=[
+                vm((120, 128), F32),
                 vm((40, 128), F32),
                 vm((144, 128), F32),
                 vm((320, 128), F32),
@@ -519,7 +558,7 @@
             ],
         ),
         compiler_params=pltpu.CompilerParams(vmem_limit_bytes=48 * 1024 * 1024),
-    )(me, *blocks, weights, pairs, target_pairs, weight_pairs)
+    )(me, pieces, *blocks, pairs, target_pairs, weight_pairs)
 
 
 def adamw(master, first_moment, second_moment, gradient, step_count):
@@ -548,23 +587,25 @@
 ):
     group = lax.axis_size("views")
     shards = lax.axis_size("rays")
-    rays = deltas.shape[0]
-    own = rays // group
     shard = master.shape[0]
-    spot = lax.axis_index("views")
-    me = spot.astype(jnp.int32).reshape(1)
+    spots = [lax.axis_index("views"), lax.axis_index("rays")]
+    me = jnp.stack(spots).astype(jnp.int32)
+    swap = lambda size, k: [(i, i ^ k) for i in range(size)]
+    rows = -(-shard // 2048) * 16
+    piece = jnp.pad(master.astype(BF16), (0, rows * 128 - shard)).reshape(rows, 128)
+    pix, vis = pixel_index.T, visible.T
+    held = piece[None]
+    links = shards.bit_length() - 1
+    for link in range(links):
+        held = jnp.concatenate([held, lax.ppermute(held, "rays", swap(shards, 1 << link))])
+    far = gather_rows(pix, vis, feature_maps, me, group, (3, 2))
+    three = lax.ppermute(far[0], "views", swap(group, 3))
+    two = lax.ppermute(far[1], "views", swap(group, 2))
+    near = gather_rows(pix, vis, feature_maps, me, group, (1, 0))
+    one = lax.ppermute(near[0], "views", swap(group, 1))
     hits = (scene_id[:, None] == jnp.arange(scene_weight.shape[0])[None, :]).astype(F32)
     ray_weight = jnp.sum(hits * scene_weight.astype(F32)[None, :], axis=1)
-    narrow = lax.all_gather(master.astype(BF16), "rays", axis=0, tiled=True)
-    flat = narrow.astype(F32)[:11384]
-    weights = jnp.pad(flat, (0, 96 * 128 - flat.shape[0])).reshape(96, 128)
-    rows = gather_rows(pixel_index.T, visible.T, feature_maps, me, group)
-    blocks = [rows]
-    for k in range(1, group):
-        pairs = [(i, i ^ k) for i in range(group)]
-        blocks.append(lax.ppermute(rows[k : k + 1], "views", pairs))
-    mine = lambda array: lax.dynamic_slice_in_dim(array, spot * own, own, 0)
-    packed = run_main(me, blocks, weights, mine(deltas), mine(targets), mine(ray_weight))
+    packed = run_main(me, [near[1], one, two, three], held, shard, deltas, targets, ray_weight)
     summed = packed[:89].reshape(-1)
     size = shards * shard
     if summed.shape[0] < size:

time: 128 us -> 75.1 us (0.59)
  blocking collectives: 46.8 us -> 10.5 us
  Pallas kernels: 65.1 us -> 36.6 us
  starting transfers between devices: 5.09 us -> 10.9 us
  waiting for transfers between devices: 1.18 us -> 6.69 us
    unnamed x1 -> x0, blocking collectives: 37.6 us -> none
    pallas_call x2 -> x3, Pallas kernels: 65.1 us -> 36.6 us  [the longest x1 23 us: run_main(): pl.pallas_call(lambda *refs: main_kernel(views, shard, *refs), out_shape=...]
    ppermute x3 -> x6, starting transfers between devices: 3.18 us -> 8.95 us  [the longest x3 7.27 us: body(): lax.ppermute(held, 'rays', swap(shards, 1 << link))]
    ppermute x3 -> x6, waiting for transfers between devices: 0.01 us -> 5.31 us  [the longest x1 2.4 us: body(): three = lax.ppermute(far[0], 'views', swap(group, 3))]
    unnamed x21 -> x20, local copies, waits for them, and re-layouts: 2.04 us -> 3.46 us
    all_to_all x1, blocking collectives: 9.17 us -> 10.5 us  [body(): got = lax.all_to_all(send, 'rays', 0, 0, tiled=True)]
  transfers between devices with their start and end apart: 6 -> 9, of which waited for: 2 -> 5; matrix products, arithmetic and copies ran while one was open for 1% -> 1% of each run, Pallas kernels for 0% -> 18%
where the time goes in v2:
time: 75.1 us; the launch traced here: 74.7 us
  Pallas kernels  36.6 us (49%)
  starting transfers between devices  10.9 us (15%)
  blocking collectives  10.5 us (14%)
  waiting for transfers between devices  6.69 us (9%)
  local copies, waits for them, and re-layouts  4.52 us (6%)
  between operations  3.99 us (5%)
  other arithmetic  1.57 us (2%)
    pallas_call x1, Pallas kernels, run_main(): pl.pallas_call(lambda *refs: main_kernel(views, shard, *refs), out_shape=...  23 us
    pallas_call x2, Pallas kernels, gather_rows(): pl.pallas_call(lambda *refs: gather_kernel(views, tile, count, *refs), ou...  13.6 us
    all_to_all x1, blocking collectives, body(): got = lax.all_to_all(send, 'rays', 0, 0, tiled=True)  10.5 us
    ppermute x3, starting transfers between devices, body(): lax.ppermute(held, 'rays', swap(shards, 1 << link))  7.27 us
    unnamed x20, local copies, waits for them, and re-layouts  3.46 us
    ppermute x1, waiting for transfers between devices, body(): three = lax.ppermute(far[0], 'views', swap(group, 3))  2.4 us
    ppermute x3, starting transfers between devices, body(): lax.ppermute(partial, 'views', [(i, i ^ k) for i in range(group)])  1.93 us
    ppermute x3, waiting for transfers between devices, body(): lax.ppermute(held, 'rays', swap(shards, 1 << link))  1.74 us
  transfers between devices with their start and end apart: 9, of which 5 were waited for; matrix products, arithmetic and copies ran while one was open for 1% of the time, Pallas kernels for 18%

profile of v2, /device:TPU:0, one launch (start us, length us, event | category | flops | bytes accessed | tf_op | source)
XLA Modules:
  0.0 74.7 jit_solution(11220884734018448018)
XLA Ops:
  0.6 0.7 convert_element_type.17
  1.3 3.0 %collective-permute-start = (bf16[1,16,128]{2,1,0:T(8,128)(2,1)S(1)}, bf16[1,16,128]{2,1,0:T(8,128)(2,1)S(1)}, u32[]{:S(2)}, u32[]{:S(2)}) collective-permute-start(bf16[1,16,128]{2,1,0:T(8,128)(2,1)S(1)} %pad_bitcast_fusion), channel_id=1, source_target_pairs={{0,4},{4,0},{8,12},{12,8},{16,20},{20,16},{24,28},{28,24},{1,5},{5... | collective-permute-start | bytes 12296 | tf_op jit(solution)/shard_map/ppermute | solution.py:600
  4.3 0.1 pad_add_fusion.refs_0_
  4.4 1.8 %copy-done = bf16[3,35,12032]{2,1,0:T(8,128)(2,1)S(1)} copy-done((bf16[3,35,12032]{2,1,0:T(8,128)(2,1)S(1)}, bf16[3,35,12032]{2,1,0:T(8,128)(2,1)}, u32[]{:S(2)}) %copy-start) | copy-done | bytes 2526744
  6.2 0.8 %copy-done.1 = s32[3072,3]{0,1:T(4,128)S(1)} copy-done((s32[3072,3]{0,1:T(4,128)S(1)}, s32[3072,3]{0,1:T(4,128)}, u32[]{:S(2)}) %copy-start.1) | copy-done | bytes 36888
  7.0 0.8 %copy-done.2 = s32[3072,3]{0,1:T(4,128)S(1)} copy-done((s32[3072,3]{0,1:T(4,128)S(1)}, s32[3072,3]{0,1:T(4,128)}, u32[]{:S(2)}) %copy-start.2) | copy-done | bytes 36888
  7.8 6.8 %shard_map.138 = (bf16[1,120,768]{2,1,0:T(8,128)(2,1)S(1)}, bf16[1,120,768]{2,1,0:T(8,128)(2,1)S(1)}) custom-call(s32[2]{0:T(128)S(1)} %pad_add_fusion.refs_0_, s32[3,3072]{1,0:T(4,128)S(1)} %bitcast.20, s32[3,3072]{1,0:T(4,128)S(1)} %bitcast.21, s32[3,3072]{1,0:T(4,128)S(1)} %bitcast.24, s32[3,3072]{1,0:T(4,128)S(1)} %bitcast.25, ...), custom_call_target="tpu_custom_call" | custom-call | flops 5322571776 | bytes 2526720 | tf_op jit(solution)/shard_map/pallas_call | solution.py:105
  14.6 0.1 collective-permute-start.3
  14.7 0.0 collective-permute-done
  14.7 0.0 copy-start.8
  14.7 0.0 copy-start.9
  14.7 0.0 copy-start.4
  14.8 0.0 copy-start.7
  14.8 0.0 copy-start.3
  14.8 0.0 copy-start.5
  14.8 0.0 copy-start.6
  14.8 1.6 %collective-permute-start.1 = (bf16[2,16,128]{2,1,0:T(8,128)(2,1)S(1)}, bf16[2,16,128]{2,1,0:T(8,128)(2,1)S(1)}, u32[]{:S(2)}, u32[]{:S(2)}) collective-permute-start(bf16[2,16,128]{2,1,0:T(8,128)(2,1)S(1)} %pad_maximum_fusion.3), channel_id=1, source_target_pairs={{0,8},{4,12},{8,0},{12,4},{16,24},{20,28},{24,16},{28,20},{1,9},{5... | collective-permute-start | bytes 24584 | tf_op jit(solution)/shard_map/ppermute | solution.py:600
  16.5 6.8 %shard_map.139 = (bf16[1,120,768]{2,1,0:T(8,128)(2,1)S(1)}, bf16[1,120,768]{2,1,0:T(8,128)(2,1)S(1)}) custom-call(s32[2]{0:T(128)S(1)} %pad_add_fusion.refs_0_, s32[3,3072]{1,0:T(4,128)S(1)} %bitcast.22, s32[3,3072]{1,0:T(4,128)S(1)} %bitcast.23, s32[3,3072]{1,0:T(4,128)S(1)} %bitcast.26, s32[3,3072]{1,0:T(4,128)S(1)} %bitcast.27, ...), custom_call_target="tpu_custom_call" | custom-call | flops 5322571776 | bytes 2526720 | tf_op jit(solution)/shard_map/pallas_call | solution.py:105
  23.3 1.6 %collective-permute-start.4 = (bf16[1,120,768]{2,1,0:T(8,128)(2,1)S(1)}, bf16[1,120,768]{2,1,0:T(8,128)(2,1)S(1)}, u32[]{:S(2)}, u32[]{:S(2)}) collective-permute-start(bf16[1,120,768]{2,1,0:T(8,128)(2,1)S(1)} %get-tuple-element.10), channel_id=1, source_target_pairs={{0,2},{1,3},{2,0},{3,1},{4,6},{5,7},{6,4},{7,5},{8,10},{9,11},{10,... | collective-permute-start | bytes 552968 | tf_op jit(solution)/shard_map/ppermute | solution.py:603
  24.9 0.0 collective-permute-start.5
  24.9 0.0 copy-done.8
  24.9 0.0 collective-permute-done.1
  24.9 2.7 %collective-permute-start.2 = (bf16[4,16,128]{2,1,0:T(8,128)(2,1)S(1)}, bf16[4,16,128]{2,1,0:T(8,128)(2,1)S(1)}, u32[]{:S(2)}, u32[]{:S(2)}) collective-permute-start(bf16[4,16,128]{2,1,0:T(8,128)(2,1)S(1)} %pad_maximum_fusion.2), channel_id=1, source_target_pairs={{0,16},{4,20},{8,24},{12,28},{16,0},{20,4},{24,8},{28,12},{1,17},{... | collective-permute-start | bytes 49160 | tf_op jit(solution)/shard_map/ppermute | solution.py:600
  27.6 0.0 copy-done.9
  27.6 0.1 select_reduce_fusion
  27.7 0.0 copy-done.4
  27.7 0.1 reshape.34.refs_6_
  27.7 0.0 copy-done.7
  27.7 0.1 reshape.35
  27.8 0.1 reshape.36
  27.9 1.7 %collective-permute-done.2 = bf16[4,16,128]{2,1,0:T(8,128)(2,1)S(1)} collective-permute-done((bf16[4,16,128]{2,1,0:T(8,128)(2,1)S(1)}, bf16[4,16,128]{2,1,0:T(8,128)(2,1)S(1)}, u32[]{:S(2)}, u32[]{:S(2)}) %collective-permute-start.2) | collective-permute-done | bytes 16416 | tf_op jit(solution)/shard_map/ppermute | solution.py:600
  29.7 0.0 collective-permute-done.3.refs_3_
  29.7 1.2 %collective-permute-done.4.refs_4_ = bf16[1,120,768]{2,1,0:T(8,128)(2,1)S(1)} collective-permute-done((bf16[1,120,768]{2,1,0:T(8,128)(2,1)S(1)}, bf16[1,120,768]{2,1,0:T(8,128)(2,1)S(1)}, u32[]{:S(2)}, u32[]{:S(2)}) %collective-permute-start.4) | collective-permute-done | bytes 184352 | tf_op jit(solution)/shard_map/ppermute | solution.py:603
  30.9 2.4 %collective-permute-done.5.refs_5_ = bf16[1,120,768]{2,1,0:T(8,128)(2,1)S(1)} collective-permute-done((bf16[1,120,768]{2,1,0:T(8,128)(2,1)S(1)}, bf16[1,120,768]{2,1,0:T(8,128)(2,1)S(1)}, u32[]{:S(2)}, u32[]{:S(2)}) %collective-permute-start.5) | collective-permute-done | bytes 184352 | tf_op jit(solution)/shard_map/ppermute | solution.py:602
  33.2 23.0 %shard_map.140 = f32[104,128]{1,0:T(8,128)S(1)} custom-call(s32[2]{0:T(128)S(1)} %pad_add_fusion.refs_0_, bf16[8,16,128]{2,1,0:T(8,128)(2,1)S(1)} %pad_maximum_fusion.1.refs_1_, bf16[1,120,768]{2,1,0:T(8,128)(2,1)S(1)} %get-tuple-element.8.refs_2_, bf16[1,120,768]{2,1,0:T(8,128)(2,1)S(1)} %collective-permute-done.3.refs_3_, ...), custom_call_target="tpu_custom_call" | custom-call | tf_op jit(solution)/shard_map/pallas_call | solution.py:515
  56.3 0.1 reshape.38
  56.4 0.1 pad.16.clone
  56.5 10.5 %all_to_all.9 = f32[8,1,1425]{2,1,0:T(1,128)S(1)} all-to-all(f32[8,1,1425]{2,1,0:T(1,128)S(1)} %all_to_all.6), channel_id=1, replica_groups=mesh['rays'=8,'views'=4] {'rays'}, dimensions={0} | all-to-all | bytes 91200 | tf_op jit(solution)/shard_map/all_to_all | solution.py:615
  67.0 0.4 collective-permute-start.8
  67.4 1.3 %collective-permute-start.7 = (f32[1425]{0:T(1024)S(1)}, f32[1425]{0:T(1024)S(1)}, u32[]{:S(2)}, u32[]{:S(2)}) collective-permute-start(f32[1425]{0:T(1024)S(1)} %reduce_sum.19), channel_id=1, source_target_pairs={{0,2},{1,3},{2,0},{3,1},{4,6},{5,7},{6,4},{7,5},{8,10},{9,11},{10,... | collective-permute-start | bytes 17108 | tf_op jit(solution)/shard_map/ppermute | solution.py:619
  68.7 0.3 collective-permute-start.6
  69.6 0.5 collective-permute-done.8
  70.2 0.9 %collective-permute-done.7 = f32[1425]{0:T(1024)S(1)} collective-permute-done((f32[1425]{0:T(1024)S(1)}, f32[1425]{0:T(1024)S(1)}, u32[]{:S(2)}, u32[]{:S(2)}) %collective-permute-start.7) | collective-permute-done | bytes 5732 | tf_op jit(solution)/shard_map/ppermute | solution.py:619
  71.0 0.0 collective-permute-done.6
  71.0 0.6 fusion.2
  73.0 0.0 copy-done.3
  73.0 0.0 copy-done.5
  73.0 0.6 multiply_subtract_fusion
  (18 shorter events, 0.2 us)
Async XLA Ops:
  1.3 13.4 %collective-permute-start = (bf16[1,16,128]{2,1,0:T(8,128)(2,1)S(1)}, bf16[1,16,128]{2,1,0:T(8,128)(2,1)S(1)}, u32[]{:S(2)}, u32[]{:S(2)}) collective-permute-start(bf16[1,16,128]{2,1,0:T(8,128)(2,1)S(1)} %pad_bitcast_fusion), channel_id=1, source_target_pairs={{0,4},{4,0},{8,12},{12,8},{16,20},{20,16},{24,28},{28,24},{1,5},{5... | collective-permute-start | bytes 12296 | tf_op jit(solution)/shard_map/ppermute | solution.py:600
  4.4 1.8 %copy-start = (bf16[3,35,12032]{2,1,0:T(8,128)(2,1)S(1)}, bf16[3,35,12032]{2,1,0:T(8,128)(2,1)}, u32[]{:S(2)}) copy-start(bf16[3,35,12032]{2,1,0:T(8,128)(2,1)} %refs_5_.3) | copy-start | bytes 7580164
  6.2 0.8 %copy-start.1 = (s32[3072,3]{0,1:T(4,128)S(1)}, s32[3072,3]{0,1:T(4,128)}, u32[]{:S(2)}) copy-start(s32[3072,3]{0,1:T(4,128)} %param.16) | copy-start | bytes 110596
  7.0 0.8 %copy-start.2 = (s32[3072,3]{0,1:T(4,128)S(1)}, s32[3072,3]{0,1:T(4,128)}, u32[]{:S(2)}) copy-start(s32[3072,3]{0,1:T(4,128)} %param.17) | copy-start | bytes 110596
  14.6 15.1 %collective-permute-start.3 = (bf16[1,120,768]{2,1,0:T(8,128)(2,1)S(1)}, bf16[1,120,768]{2,1,0:T(8,128)(2,1)S(1)}, u32[]{:S(2)}, u32[]{:S(2)}) collective-permute-start(bf16[1,120,768]{2,1,0:T(8,128)(2,1)S(1)} %get-tuple-element.9), channel_id=1, source_target_pairs={{0,1},{1,0},{2,3},{3,2},{4,5},{5,4},{6,7},{7,6},{8,9},{9,8},{10,11... | collective-permute-start | bytes 552968 | tf_op jit(solution)/shard_map/ppermute | solution.py:605
  14.7 10.2 %copy-start.8 = (s32[8]{0:T(128)S(1)}, s32[8]{0:T(128)}, u32[]{:S(2)}) copy-start(s32[8]{0:T(128)} %param.21) | copy-start | bytes 100
  14.7 12.8 %copy-start.9 = (s32[16]{0:T(128)S(1)}, s32[16]{0:T(128)}, u32[]{:S(2)}) copy-start(s32[16]{0:T(128)} %param.20) | copy-start | bytes 196
  14.7 12.9 %copy-start.4 = (f32[16,192]{1,0:T(8,128)S(1)}, f32[16,192]{1,0:T(8,128)}, u32[]{:S(2)}) copy-start(f32[16,192]{1,0:T(8,128)} %param.18) | copy-start | bytes 36868
  14.8 13.0 %copy-start.7 = (f32[16,3]{0,1:T(4,128)S(1)}, f32[16,3]{0,1:T(4,128)}, u32[]{:S(2)}) copy-start(f32[16,3]{0,1:T(4,128)} %param.19) | copy-start | bytes 580
  14.8 58.2 %copy-start.3 = (f32[1423]{0:T(1024)S(1)}, f32[1423]{0:T(1024)}, u32[]{:S(2)}) copy-start(f32[1423]{0:T(1024)} %param.11) | copy-start | bytes 17080
  14.8 58.2 %copy-start.5 = (f32[1423]{0:T(1024)S(1)}, f32[1423]{0:T(1024)}, u32[]{:S(2)}) copy-start(f32[1423]{0:T(1024)} %param.13) | copy-start | bytes 17080
  14.8 58.2 %copy-start.6 = (f32[1423]{0:T(1024)S(1)}, f32[1423]{0:T(1024)}, u32[]{:S(2)}) copy-start(f32[1423]{0:T(1024)} %param.12) | copy-start | bytes 17080
  14.8 10.1 %collective-permute-start.1 = (bf16[2,16,128]{2,1,0:T(8,128)(2,1)S(1)}, bf16[2,16,128]{2,1,0:T(8,128)(2,1)S(1)}, u32[]{:S(2)}, u32[]{:S(2)}) collective-permute-start(bf16[2,16,128]{2,1,0:T(8,128)(2,1)S(1)} %pad_maximum_fusion.3), channel_id=1, source_target_pairs={{0,8},{4,12},{8,0},{12,4},{16,24},{20,28},{24,16},{28,20},{1,9},{5... | collective-permute-start | bytes 24584 | tf_op jit(solution)/shard_map/ppermute | solution.py:600
  23.3 7.6 %collective-permute-start.4 = (bf16[1,120,768]{2,1,0:T(8,128)(2,1)S(1)}, bf16[1,120,768]{2,1,0:T(8,128)(2,1)S(1)}, u32[]{:S(2)}, u32[]{:S(2)}) collective-permute-start(bf16[1,120,768]{2,1,0:T(8,128)(2,1)S(1)} %get-tuple-element.10), channel_id=1, source_target_pairs={{0,2},{1,3},{2,0},{3,1},{4,6},{5,7},{6,4},{7,5},{8,10},{9,11},{10,... | collective-permute-start | bytes 552968 | tf_op jit(solution)/shard_map/ppermute | solution.py:603
  24.9 8.4 %collective-permute-start.5 = (bf16[1,120,768]{2,1,0:T(8,128)(2,1)S(1)}, bf16[1,120,768]{2,1,0:T(8,128)(2,1)S(1)}, u32[]{:S(2)}, u32[]{:S(2)}) collective-permute-start(bf16[1,120,768]{2,1,0:T(8,128)(2,1)S(1)} %get-tuple-element.11), channel_id=1, source_target_pairs={{0,3},{1,2},{2,1},{3,0},{4,7},{5,6},{6,5},{7,4},{8,11},{9,10},{10,... | collective-permute-start | bytes 552968 | tf_op jit(solution)/shard_map/ppermute | solution.py:602
  24.9 4.8 %collective-permute-start.2 = (bf16[4,16,128]{2,1,0:T(8,128)(2,1)S(1)}, bf16[4,16,128]{2,1,0:T(8,128)(2,1)S(1)}, u32[]{:S(2)}, u32[]{:S(2)}) collective-permute-start(bf16[4,16,128]{2,1,0:T(8,128)(2,1)S(1)} %pad_maximum_fusion.2), channel_id=1, source_target_pairs={{0,16},{4,20},{8,24},{12,28},{16,0},{20,4},{24,8},{28,12},{1,17},{... | collective-permute-start | bytes 49160 | tf_op jit(solution)/shard_map/ppermute | solution.py:600
  67.0 3.2 %collective-permute-start.8 = (f32[1425]{0:T(1024)S(1)}, f32[1425]{0:T(1024)S(1)}, u32[]{:S(2)}, u32[]{:S(2)}) collective-permute-start(f32[1425]{0:T(1024)S(1)} %reduce_sum.19), channel_id=1, source_target_pairs={{0,3},{1,2},{2,1},{3,0},{4,7},{5,6},{6,5},{7,4},{8,11},{9,10},{10,... | collective-permute-start | bytes 17108 | tf_op jit(solution)/shard_map/ppermute | solution.py:619
  67.4 3.7 %collective-permute-start.7 = (f32[1425]{0:T(1024)S(1)}, f32[1425]{0:T(1024)S(1)}, u32[]{:S(2)}, u32[]{:S(2)}) collective-permute-start(f32[1425]{0:T(1024)S(1)} %reduce_sum.19), channel_id=1, source_target_pairs={{0,2},{1,3},{2,0},{3,1},{4,6},{5,7},{6,4},{7,5},{8,10},{9,11},{10,... | collective-permute-start | bytes 17108 | tf_op jit(solution)/shard_map/ppermute | solution.py:619
  68.7 2.3 %collective-permute-start.6 = (f32[1425]{0:T(1024)S(1)}, f32[1425]{0:T(1024)S(1)}, u32[]{:S(2)}, u32[]{:S(2)}) collective-permute-start(f32[1425]{0:T(1024)S(1)} %reduce_sum.19), channel_id=1, source_target_pairs={{0,1},{1,0},{2,3},{3,2},{4,5},{5,4},{6,7},{7,6},{8,9},{9,8},{10,11... | collective-permute-start | bytes 17108 | tf_op jit(solution)/shard_map/ppermute | solution.py:619

commit v3 on v2

--- a/solution.py
+++ b/solution.py
@@ -11,11 +11,13 @@
 SEEN_VIEWS = 10
 CHANNELS = 35
 STRIP = 40
-BAND = 48
+BAND = 40
+SEEN_SHIFT = 14
+SEEN_BIT = 1 << SEEN_SHIFT
 GATHER_TILE = 256
 RAY = 192
 CHUNK = 2 * RAY
-PASSES = 2
+PASSES = 1
 MOMENT_DECAY = 0.5
 SQUARE_DECAY = 0.5
 LEARNING_RATE = 0.05
@@ -57,65 +59,79 @@
     return lax.broadcasted_iota(jnp.int32, shape, axis)
 
 
+def stack_maps(map_ref, stacked):
+    views, channels, pixels = map_ref.shape
+    blocks = pixels // 256
+    for view in range(views):
+        for block in range(0, blocks, 2):
+            strips = []
+            for part in range(block, min(block + 2, blocks)):
+                strips.append(map_ref[view, :, 256 * part : 256 * (part + 1)].astype(F32))
+                strips.append(jnp.zeros((BAND - channels, 256), F32))
+            strips = jnp.concatenate(strips, axis=0)
+            stacked[view, BAND * block : BAND * block + strips.shape[0], :] = strips.astype(BF16)
+
+
 def gather_kernel(views, tile, count, *refs):
-    pix_refs, vis_refs = refs[1 : 1 + count], refs[1 + count : 1 + 2 * count]
-    map_ref = refs[1 + 2 * count]
-    outs, stacked = refs[2 + 2 * count : -1], refs[-1]
-    blocks = map_ref.shape[2] // 256
+    packed_refs, source = refs[1 : 1 + count], refs[1 + count]
+    outs, stacked = refs[2 + count : -1], refs[-1]
+    blocks = stacked.shape[1] // BAND
 
     @pl.when(pl.program_id(0) == 0)
     def _():
-        for view in range(views):
-            for block in range(blocks):
-                stacked[view, BAND * block : BAND * block + CHANNELS, :] = map_ref[
-                    view, :, 256 * block : 256 * (block + 1)
-                ]
-
-    row = iota((STRIP, tile), 0)
-    for pix_ref, vis_ref, out_ref in zip(pix_refs, vis_refs, outs):
+        stack_maps(source, stacked)
+
+    row = iota((8, tile), 0) + 8 * (CHANNELS // 8)
+    for packed_ref, out_ref in zip(packed_refs, outs):
         strips = []
         for view in range(views):
-            index = pix_ref[view : view + 1, :]
-            high = jnp.broadcast_to(index >> 8, (STRIP, tile))
+            packed = packed_ref[view : view + 1, :]
+            index = packed & (SEEN_BIT - 1)
+            high = jnp.broadcast_to(index >> 8, (8, tile))
             low = jnp.broadcast_to(index & 255, (256, tile))
             picked = (iota((256, tile), 0) == low).astype(F32).astype(BF16)
             found = dot(stacked[view], picked)
-            total = jnp.zeros((STRIP, tile), F32)
+            totals = [jnp.zeros((8, tile), F32)] * (STRIP // 8)
             for block in range(blocks):
-                total = jnp.where(
-                    high == block, found[BAND * block : BAND * block + STRIP], total
-                )
-            seen = jnp.broadcast_to(vis_ref[view : view + 1, :].astype(F32), (STRIP, tile))
-            total = jnp.where(row == CHANNELS, 1.0, total)
-            total = jnp.where(row == CHANNELS + 1, seen, total)
-            total = jnp.where(row > CHANNELS + 1, 0.0, total)
-            strips.append(total)
+                here = high == block
+                for part in range(STRIP // 8):
+                    at = BAND * block + 8 * part
+                    totals[part] = jnp.where(here, found[at : at + 8], totals[part])
+            seen = jnp.broadcast_to((packed >> SEEN_SHIFT).astype(F32), (8, tile))
+            last = jnp.where(row == CHANNELS, 1.0, totals[-1])
+            last = jnp.where(row == CHANNELS + 1, seen, last)
+            totals[-1] = jnp.where(row > CHANNELS + 1, 0.0, last)
+            strips += totals
         out_ref[0] = jnp.concatenate(strips, axis=0).astype(BF16)
 
 
-def gather_rows(pix, vis, maps, me, group, ways):
-    views, points = pix.shape
+def gather_rows(packed, source, me, group, ways):
+    views, points = packed.shape
     tile = GATHER_TILE
     own = points // group
     tiles = own // tile
     count = len(ways)
     part = lambda k: pl.BlockSpec((views, tile), lambda t, me: (0, (me[0] ^ k) * tiles + t))
-    out = jax.ShapeDtypeStruct((1, views * STRIP, own), BF16)
-    flops = 2 * views * own * count * BAND * maps.shape[2]
+    whole = lambda shape: pl.BlockSpec(shape, lambda t, me: (0, 0, 0))
+    outs = [jax.ShapeDtypeStruct((1, views * STRIP, own), BF16)] * count
+    out_specs = [pl.BlockSpec((1, views * STRIP, tile), lambda t, me: (0, 0, t))] * count
+    table = (views, BAND * (source.shape[2] // 256), 256)
+    flops = 2 * views * own * count * table[1] * 256
     return pl.pallas_call(
         lambda *refs: gather_kernel(views, tile, count, *refs),
-        out_shape=[out] * count,
+        out_shape=outs,
         grid_spec=pltpu.PrefetchScalarGridSpec(
             num_scalar_prefetch=1,
             grid=(tiles,),
-            in_specs=[part(k) for k in ways] * 2
-            + [pl.BlockSpec(maps.shape, lambda t, me: (0, 0, 0))],
-            out_specs=[pl.BlockSpec((1, views * STRIP, tile), lambda t, me: (0, 0, t))] * count,
-            scratch_shapes=[pltpu.VMEM((views, BAND * (maps.shape[2] // 256), 256), BF16)],
+            in_specs=[part(k) for k in ways] + [whole(source.shape)],
+            out_specs=out_specs,
+            scratch_shapes=[pltpu.VMEM(table, BF16)],
         ),
-        compiler_params=pltpu.CompilerParams(vmem_limit_bytes=40 * 1024 * 1024),
-        cost_estimate=pl.CostEstimate(flops=flops, bytes_accessed=maps.size * 2, transcendentals=0),
-    )(me, *([pix] * count), *([vis] * count), maps)
+        compiler_params=pltpu.CompilerParams(vmem_limit_bytes=32 * 1024 * 1024),
+        cost_estimate=pl.CostEstimate(
+            flops=flops, bytes_accessed=source.size * 2, transcendentals=0
+        ),
+    )(me, *([packed] * count), source)
 
 
 def roll(value, shift):
@@ -587,30 +603,32 @@
 ):
     group = lax.axis_size("views")
     shards = lax.axis_size("rays")
+    assert feature_maps.shape[2] <= SEEN_BIT
     shard = master.shape[0]
     spots = [lax.axis_index("views"), lax.axis_index("rays")]
     me = jnp.stack(spots).astype(jnp.int32)
     swap = lambda size, k: [(i, i ^ k) for i in range(size)]
     rows = -(-shard // 2048) * 16
     piece = jnp.pad(master.astype(BF16), (0, rows * 128 - shard)).reshape(rows, 128)
-    pix, vis = pixel_index.T, visible.T
+    packed = pixel_index.T + (visible.T << SEEN_SHIFT)
     held = piece[None]
     links = shards.bit_length() - 1
     for link in range(links):
         held = jnp.concatenate([held, lax.ppermute(held, "rays", swap(shards, 1 << link))])
-    far = gather_rows(pix, vis, feature_maps, me, group, (3, 2))
+    far = gather_rows(packed, feature_maps, me, group, (3, 2))
     three = lax.ppermute(far[0], "views", swap(group, 3))
     two = lax.ppermute(far[1], "views", swap(group, 2))
-    near = gather_rows(pix, vis, feature_maps, me, group, (1, 0))
+    near = gather_rows(packed, feature_maps, me, group, (1,))
     one = lax.ppermute(near[0], "views", swap(group, 1))
+    mine = gather_rows(packed, feature_maps, me, group, (0,))
     hits = (scene_id[:, None] == jnp.arange(scene_weight.shape[0])[None, :]).astype(F32)
     ray_weight = jnp.sum(hits * scene_weight.astype(F32)[None, :], axis=1)
-    packed = run_main(me, [near[1], one, two, three], held, shard, deltas, targets, ray_weight)
-    summed = packed[:89].reshape(-1)
+    result = run_main(me, [mine[0], one, two, three], held, shard, deltas, targets, ray_weight)
+    summed = result[:89].reshape(-1)
     size = shards * shard
     if summed.shape[0] < size:
         summed = jnp.pad(summed, (0, size - summed.shape[0]))
-    extra = jnp.broadcast_to(packed[96, :2][None], (shards, 2))
+    extra = jnp.broadcast_to(result[96, :2][None], (shards, 2))
     send = jnp.concatenate([summed[:size].reshape(shards, shard), extra], axis=1)
     got = lax.all_to_all(send, "rays", 0, 0, tiled=True)
     partial = jnp.sum(got, axis=0)

time: 75.1 us -> 68.3 us (0.909)
  Pallas kernels: 36.6 us -> 32.9 us
  waiting for transfers between devices: 6.69 us -> 3.86 us
  local copies, waits for them, and re-layouts: 4.52 us -> 2.91 us
  other arithmetic: 1.57 us -> 2.41 us
    pallas_call x1, Pallas kernels: 23 us -> 19.8 us  [run_main(): pl.pallas_call(lambda *refs: main_kernel(views, shard, *refs), out_shape=...]
    ppermute x1, waiting for transfers between devices: 2.4 us -> 0.01 us  [body(): three = lax.ppermute(far[0], 'views', swap(group, 3))]
    unnamed x20 -> x16, local copies, waits for them, and re-layouts: 3.46 us -> 1.85 us
    ppermute x1, waiting for transfers between devices: 1.17 us -> 0.01 us  [body(): two = lax.ppermute(far[1], 'views', swap(group, 2))]
    add x0 -> x1, other arithmetic: none -> 0.84 us  [body(): packed = pixel_index.T + (visible.T << SEEN_SHIFT)]
    pallas_call x2 -> x3, Pallas kernels: 13.6 us -> 13.2 us  [gather_rows(): pl.pallas_call(lambda *refs: gather_kernel(views, tile, count, *refs), ou...]
  transfers between devices with their start and end apart: 9 -> 9, of which waited for: 5 -> 3; matrix products, arithmetic and copies ran while one was open for 1% -> 2% of each run, Pallas kernels for 18% -> 19%
where the time goes in v3:
time: 68.3 us; the launch traced here: 68 us
  Pallas kernels  32.9 us (48%)
  starting transfers between devices  11.5 us (17%)
  blocking collectives  10.4 us (15%)
  between operations  4.03 us (6%)
  waiting for transfers between devices  3.86 us (6%)
  local copies, waits for them, and re-layouts  2.91 us (4%)
  other arithmetic  2.41 us (4%)
    pallas_call x1, Pallas kernels, run_main(): pl.pallas_call(lambda *refs: main_kernel(views, shard, *refs), out_shape=...  19.8 us
    pallas_call x3, Pallas kernels, gather_rows(): pl.pallas_call(lambda *refs: gather_kernel(views, tile, count, *refs), ou...  13.2 us
    all_to_all x1, blocking collectives, body(): got = lax.all_to_all(send, 'rays', 0, 0, tiled=True)  10.4 us
    ppermute x3, starting transfers between devices, body(): lax.ppermute(held, 'rays', swap(shards, 1 << link))  7.26 us
    ppermute x3, waiting for transfers between devices, body(): lax.ppermute(partial, 'views', [(i, i ^ k) for i in range(group)])  2.11 us
    ppermute x3, starting transfers between devices, body(): lax.ppermute(partial, 'views', [(i, i ^ k) for i in range(group)])  1.92 us
    unnamed x16, local copies, waits for them, and re-layouts  1.85 us
    ppermute x3, waiting for transfers between devices, body(): lax.ppermute(held, 'rays', swap(shards, 1 << link))  1.74 us
  transfers between devices with their start and end apart: 9, of which 3 were waited for; matrix products, arithmetic and copies ran while one was open for 2% of the time, Pallas kernels for 19%

profile of v3, /device:TPU:0, one launch (start us, length us, event | category | flops | bytes accessed | tf_op | source)
XLA Modules:
  0.0 68.0 jit_solution(1735671652080745210)
XLA Ops:
  0.6 0.7 %convert_element_type.17 = bf16[1423]{0:T(1024)(128)(2,1)S(1)} convert(f32[1423]{0:T(1024)} %param.11) | non-fusion elementwise | flops 1423 | bytes 8538 | tf_op jit(solution)/shard_map/convert_element_type | solution.py:612
  1.3 3.0 %collective-permute-start = (bf16[1,16,128]{2,1,0:T(8,128)(2,1)S(1)}, bf16[1,16,128]{2,1,0:T(8,128)(2,1)S(1)}, u32[]{:S(2)}, u32[]{:S(2)}) collective-permute-start(bf16[1,16,128]{2,1,0:T(8,128)(2,1)S(1)} %pad_bitcast_fusion), channel_id=1, source_target_pairs={{0,4},{4,0},{8,12},{12,8},{16,20},{20,16},{24,28},{28,24},{1,5},{5... | collective-permute-start | bytes 12296 | tf_op jit(solution)/shard_map/ppermute | solution.py:617
  4.3 0.1 pad_add_fusion.refs_0_
  4.4 0.8 %add_bitcast_fusion.refs_1_.refs_2_ = s32[3,3072]{1,0:T(4,128)S(1)} fusion(s32[3072,3]{0,1:T(4,128)} %param.16, s32[3072,3]{0,1:T(4,128)} %param.17), kind=kLoop, calls=%fused_computation.2 | loop fusion | flops 18432 | bytes 110592 | tf_op jit(solution)/shard_map/add | solution.py:613
  5.2 0.0 copy-start
  5.2 1.8 %copy-done = bf16[3,35,12032]{2,1,0:T(8,128)(2,1)S(1)} copy-done((bf16[3,35,12032]{2,1,0:T(8,128)(2,1)S(1)}, bf16[3,35,12032]{2,1,0:T(8,128)(2,1)}, u32[]{:S(2)}) %copy-start) | copy-done | bytes 2526744
  7.0 5.9 %shard_map.140 = (bf16[1,120,768]{2,1,0:T(8,128)(2,1)S(1)}, bf16[1,120,768]{2,1,0:T(8,128)(2,1)S(1)}) custom-call(s32[2]{0:T(128)S(1)} %pad_add_fusion.refs_0_, s32[3,3072]{1,0:T(4,128)S(1)} %add_bitcast_fusion.refs_1_.refs_2_, s32[3,3072]{1,0:T(4,128)S(1)} %add_bitcast_fusion.refs_1_.refs_2_, bf16[3,35,12032]{2,1,0:T(8,128)(2,1)S(1)} %copy-done), custom_call_target="tpu_custom_call" | custom-call | flops 4435476480 | bytes 2526720 | tf_op jit(solution)/shard_map/pallas_call | solution.py:120
  12.9 1.6 %collective-permute-start.4 = (bf16[1,120,768]{2,1,0:T(8,128)(2,1)S(1)}, bf16[1,120,768]{2,1,0:T(8,128)(2,1)S(1)}, u32[]{:S(2)}, u32[]{:S(2)}) collective-permute-start(bf16[1,120,768]{2,1,0:T(8,128)(2,1)S(1)} %get-tuple-element.6), channel_id=1, source_target_pairs={{0,2},{1,3},{2,0},{3,1},{4,6},{5,7},{6,4},{7,5},{8,10},{9,11},{10,... | collective-permute-start | bytes 552968 | tf_op jit(solution)/shard_map/ppermute | solution.py:620
  14.5 0.0 collective-permute-start.5
  14.5 3.7 %shard_map.139 = bf16[1,120,768]{2,1,0:T(8,128)(2,1)S(1)} custom-call(s32[2]{0:T(128)S(1)} %pad_add_fusion.refs_0_, s32[3,3072]{1,0:T(4,128)S(1)} %add_bitcast_fusion.refs_1_.refs_2_, bf16[3,35,12032]{2,1,0:T(8,128)(2,1)S(1)} %copy-done), custom_call_target="tpu_custom_call" | custom-call | flops 2217738240 | bytes 2526720 | tf_op jit(solution)/shard_map/pallas_call | solution.py:120
  18.2 0.7 %collective-permute-start.3 = (bf16[1,120,768]{2,1,0:T(8,128)(2,1)S(1)}, bf16[1,120,768]{2,1,0:T(8,128)(2,1)S(1)}, u32[]{:S(2)}, u32[]{:S(2)}) collective-permute-start(bf16[1,120,768]{2,1,0:T(8,128)(2,1)S(1)} %shard_map.139), channel_id=1, source_target_pairs={{0,1},{1,0},{2,3},{3,2},{4,5},{5,4},{6,7},{7,6},{8,9},{9,8},{10,11... | collective-permute-start | bytes 552968 | tf_op jit(solution)/shard_map/ppermute | solution.py:622
  18.8 0.0 collective-permute-done
  18.9 0.0 copy-start.7
  18.9 0.0 copy-start.5
  18.9 0.0 copy-start.2
  18.9 0.0 copy-start.1
  18.9 0.0 copy-start.3
  18.9 0.0 copy-start.4
  18.9 1.6 %collective-permute-start.1 = (bf16[2,16,128]{2,1,0:T(8,128)(2,1)S(1)}, bf16[2,16,128]{2,1,0:T(8,128)(2,1)S(1)}, u32[]{:S(2)}, u32[]{:S(2)}) collective-permute-start(bf16[2,16,128]{2,1,0:T(8,128)(2,1)S(1)} %pad_maximum_fusion.3), channel_id=1, source_target_pairs={{0,8},{4,12},{8,0},{12,4},{16,24},{20,28},{24,16},{28,20},{1,9},{5... | collective-permute-start | bytes 24584 | tf_op jit(solution)/shard_map/ppermute | solution.py:617
  20.6 3.7 %shard_map.138.refs_2_ = bf16[1,120,768]{2,1,0:T(8,128)(2,1)S(1)} custom-call(s32[2]{0:T(128)S(1)} %pad_add_fusion.refs_0_, s32[3,3072]{1,0:T(4,128)S(1)} %add_bitcast_fusion.refs_1_.refs_2_, bf16[3,35,12032]{2,1,0:T(8,128)(2,1)S(1)} %copy-done), custom_call_target="tpu_custom_call" | custom-call | flops 2217738240 | bytes 2526720 | tf_op jit(solution)/shard_map/pallas_call | solution.py:120
  24.2 0.0 copy-done.6
  24.3 0.0 collective-permute-done.1
  24.3 2.7 %collective-permute-start.2 = (bf16[4,16,128]{2,1,0:T(8,128)(2,1)S(1)}, bf16[4,16,128]{2,1,0:T(8,128)(2,1)S(1)}, u32[]{:S(2)}, u32[]{:S(2)}) collective-permute-start(bf16[4,16,128]{2,1,0:T(8,128)(2,1)S(1)} %pad_maximum_fusion.2), channel_id=1, source_target_pairs={{0,16},{4,20},{8,24},{12,28},{16,0},{20,4},{24,8},{28,12},{1,17},{... | collective-permute-start | bytes 49160 | tf_op jit(solution)/shard_map/ppermute | solution.py:617
  26.9 0.0 copy-done.7
  26.9 0.1 select_reduce_fusion
  27.0 0.0 copy-done.5
  27.0 0.1 reshape.35
  27.1 0.1 reshape.36
  27.2 0.0 copy-done.2
  27.2 0.1 reshape.34.refs_6_
  27.3 1.7 %collective-permute-done.2 = bf16[4,16,128]{2,1,0:T(8,128)(2,1)S(1)} collective-permute-done((bf16[4,16,128]{2,1,0:T(8,128)(2,1)S(1)}, bf16[4,16,128]{2,1,0:T(8,128)(2,1)S(1)}, u32[]{:S(2)}, u32[]{:S(2)}) %collective-permute-start.2) | collective-permute-done | bytes 16416 | tf_op jit(solution)/shard_map/ppermute | solution.py:617
  29.0 0.0 collective-permute-done.4.refs_4_
  29.1 0.0 collective-permute-done.5.refs_5_
  29.1 0.0 collective-permute-done.3.refs_3_
  29.1 19.8 %shard_map.141 = f32[104,128]{1,0:T(8,128)S(1)} custom-call(s32[2]{0:T(128)S(1)} %pad_add_fusion.refs_0_, bf16[8,16,128]{2,1,0:T(8,128)(2,1)S(1)} %pad_maximum_fusion.1.refs_1_, bf16[1,120,768]{2,1,0:T(8,128)(2,1)S(1)} %shard_map.138.refs_2_, bf16[1,120,768]{2,1,0:T(8,128)(2,1)S(1)} %collective-permute-done.3.refs_3_, ...), custom_call_target="tpu_custom_call" | custom-call | tf_op jit(solution)/shard_map/pallas_call | solution.py:531
  48.8 0.1 reshape.38
  48.9 0.1 pad.16.clone
  49.1 10.4 %all_to_all.9 = f32[8,1,1425]{2,1,0:T(1,128)S(1)} all-to-all(f32[8,1,1425]{2,1,0:T(1,128)S(1)} %all_to_all.6), channel_id=1, replica_groups=mesh['rays'=8,'views'=4] {'rays'}, dimensions={0} | all-to-all | bytes 91200 | tf_op jit(solution)/shard_map/all_to_all | solution.py:633
  59.5 0.1 collective-permute-start.6
  59.6 1.6 %collective-permute-start.7 = (f32[1425]{0:T(1024)S(1)}, f32[1425]{0:T(1024)S(1)}, u32[]{:S(2)}, u32[]{:S(2)}) collective-permute-start(f32[1425]{0:T(1024)S(1)} %reduce_sum.19), channel_id=1, source_target_pairs={{0,2},{1,3},{2,0},{3,1},{4,6},{5,7},{6,4},{7,5},{8,10},{9,11},{10,... | collective-permute-start | bytes 17108 | tf_op jit(solution)/shard_map/ppermute | solution.py:637
  61.2 0.3 collective-permute-start.8
  62.1 0.0 collective-permute-done.6
  62.1 1.2 %collective-permute-done.7 = f32[1425]{0:T(1024)S(1)} collective-permute-done((f32[1425]{0:T(1024)S(1)}, f32[1425]{0:T(1024)S(1)}, u32[]{:S(2)}, u32[]{:S(2)}) %collective-permute-start.7) | collective-permute-done | bytes 5732 | tf_op jit(solution)/shard_map/ppermute | solution.py:637
  63.3 0.9 %collective-permute-done.8 = f32[1425]{0:T(1024)S(1)} collective-permute-done((f32[1425]{0:T(1024)S(1)}, f32[1425]{0:T(1024)S(1)}, u32[]{:S(2)}, u32[]{:S(2)}) %collective-permute-start.8) | collective-permute-done | bytes 5732 | tf_op jit(solution)/shard_map/ppermute | solution.py:637
  64.3 0.6 fusion.2
  66.2 0.0 copy-done.1
  66.2 0.0 copy-done.3
  66.2 0.6 multiply_subtract_fusion
  (16 shorter events, 0.2 us)
Async XLA Ops:
  1.3 17.5 %collective-permute-start = (bf16[1,16,128]{2,1,0:T(8,128)(2,1)S(1)}, bf16[1,16,128]{2,1,0:T(8,128)(2,1)S(1)}, u32[]{:S(2)}, u32[]{:S(2)}) collective-permute-start(bf16[1,16,128]{2,1,0:T(8,128)(2,1)S(1)} %pad_bitcast_fusion), channel_id=1, source_target_pairs={{0,4},{4,0},{8,12},{12,8},{16,20},{20,16},{24,28},{28,24},{1,5},{5... | collective-permute-start | bytes 12296 | tf_op jit(solution)/shard_map/ppermute | solution.py:617
  5.2 1.8 %copy-start = (bf16[3,35,12032]{2,1,0:T(8,128)(2,1)S(1)}, bf16[3,35,12032]{2,1,0:T(8,128)(2,1)}, u32[]{:S(2)}) copy-start(bf16[3,35,12032]{2,1,0:T(8,128)(2,1)} %refs_3_.1) | copy-start | bytes 7580164
  12.9 16.1 %collective-permute-start.4 = (bf16[1,120,768]{2,1,0:T(8,128)(2,1)S(1)}, bf16[1,120,768]{2,1,0:T(8,128)(2,1)S(1)}, u32[]{:S(2)}, u32[]{:S(2)}) collective-permute-start(bf16[1,120,768]{2,1,0:T(8,128)(2,1)S(1)} %get-tuple-element.6), channel_id=1, source_target_pairs={{0,2},{1,3},{2,0},{3,1},{4,6},{5,7},{6,4},{7,5},{8,10},{9,11},{10,... | collective-permute-start | bytes 552968 | tf_op jit(solution)/shard_map/ppermute | solution.py:620
  14.5 14.6 %collective-permute-start.5 = (bf16[1,120,768]{2,1,0:T(8,128)(2,1)S(1)}, bf16[1,120,768]{2,1,0:T(8,128)(2,1)S(1)}, u32[]{:S(2)}, u32[]{:S(2)}) collective-permute-start(bf16[1,120,768]{2,1,0:T(8,128)(2,1)S(1)} %get-tuple-element.7), channel_id=1, source_target_pairs={{0,3},{1,2},{2,1},{3,0},{4,7},{5,6},{6,5},{7,4},{8,11},{9,10},{10,... | collective-permute-start | bytes 552968 | tf_op jit(solution)/shard_map/ppermute | solution.py:619
  18.2 10.9 %collective-permute-start.3 = (bf16[1,120,768]{2,1,0:T(8,128)(2,1)S(1)}, bf16[1,120,768]{2,1,0:T(8,128)(2,1)S(1)}, u32[]{:S(2)}, u32[]{:S(2)}) collective-permute-start(bf16[1,120,768]{2,1,0:T(8,128)(2,1)S(1)} %shard_map.139), channel_id=1, source_target_pairs={{0,1},{1,0},{2,3},{3,2},{4,5},{5,4},{6,7},{7,6},{8,9},{9,8},{10,11... | collective-permute-start | bytes 552968 | tf_op jit(solution)/shard_map/ppermute | solution.py:622
  18.9 5.4 %copy-start.6 = (s32[8]{0:T(128)S(1)}, s32[8]{0:T(128)}, u32[]{:S(2)}) copy-start(s32[8]{0:T(128)} %param.21) | copy-start | bytes 100
  18.9 8.1 %copy-start.7 = (s32[16]{0:T(128)S(1)}, s32[16]{0:T(128)}, u32[]{:S(2)}) copy-start(s32[16]{0:T(128)} %param.20) | copy-start | bytes 196
  18.9 8.2 %copy-start.5 = (f32[16,3]{0,1:T(4,128)S(1)}, f32[16,3]{0,1:T(4,128)}, u32[]{:S(2)}) copy-start(f32[16,3]{0,1:T(4,128)} %param.19) | copy-start | bytes 580
  18.9 8.3 %copy-start.2 = (f32[16,192]{1,0:T(8,128)S(1)}, f32[16,192]{1,0:T(8,128)}, u32[]{:S(2)}) copy-start(f32[16,192]{1,0:T(8,128)} %param.18) | copy-start | bytes 36868
  18.9 47.3 %copy-start.1 = (f32[1423]{0:T(1024)S(1)}, f32[1423]{0:T(1024)}, u32[]{:S(2)}) copy-start(f32[1423]{0:T(1024)} %param.11) | copy-start | bytes 17080
  18.9 47.3 %copy-start.3 = (f32[1423]{0:T(1024)S(1)}, f32[1423]{0:T(1024)}, u32[]{:S(2)}) copy-start(f32[1423]{0:T(1024)} %param.13) | copy-start | bytes 17080
  18.9 47.3 %copy-start.4 = (f32[1423]{0:T(1024)S(1)}, f32[1423]{0:T(1024)}, u32[]{:S(2)}) copy-start(f32[1423]{0:T(1024)} %param.12) | copy-start | bytes 17080
  18.9 5.3 %collective-permute-start.1 = (bf16[2,16,128]{2,1,0:T(8,128)(2,1)S(1)}, bf16[2,16,128]{2,1,0:T(8,128)(2,1)S(1)}, u32[]{:S(2)}, u32[]{:S(2)}) collective-permute-start(bf16[2,16,128]{2,1,0:T(8,128)(2,1)S(1)} %pad_maximum_fusion.3), channel_id=1, source_target_pairs={{0,8},{4,12},{8,0},{12,4},{16,24},{20,28},{24,16},{28,20},{1,9},{5... | collective-permute-start | bytes 24584 | tf_op jit(solution)/shard_map/ppermute | solution.py:617
  24.3 4.8 %collective-permute-start.2 = (bf16[4,16,128]{2,1,0:T(8,128)(2,1)S(1)}, bf16[4,16,128]{2,1,0:T(8,128)(2,1)S(1)}, u32[]{:S(2)}, u32[]{:S(2)}) collective-permute-start(bf16[4,16,128]{2,1,0:T(8,128)(2,1)S(1)} %pad_maximum_fusion.2), channel_id=1, source_target_pairs={{0,16},{4,20},{8,24},{12,28},{16,0},{20,4},{24,8},{28,12},{1,17},{... | collective-permute-start | bytes 49160 | tf_op jit(solution)/shard_map/ppermute | solution.py:617
  59.5 2.6 %collective-permute-start.6 = (f32[1425]{0:T(1024)S(1)}, f32[1425]{0:T(1024)S(1)}, u32[]{:S(2)}, u32[]{:S(2)}) collective-permute-start(f32[1425]{0:T(1024)S(1)} %reduce_sum.19), channel_id=1, source_target_pairs={{0,1},{1,0},{2,3},{3,2},{4,5},{5,4},{6,7},{7,6},{8,9},{9,8},{10,11... | collective-permute-start | bytes 17108 | tf_op jit(solution)/shard_map/ppermute | solution.py:637
  59.6 3.7 %collective-permute-start.7 = (f32[1425]{0:T(1024)S(1)}, f32[1425]{0:T(1024)S(1)}, u32[]{:S(2)}, u32[]{:S(2)}) collective-permute-start(f32[1425]{0:T(1024)S(1)} %reduce_sum.19), channel_id=1, source_target_pairs={{0,2},{1,3},{2,0},{3,1},{4,6},{5,7},{6,4},{7,5},{8,10},{9,11},{10,... | collective-permute-start | bytes 17108 | tf_op jit(solution)/shard_map/ppermute | solution.py:637
  61.2 3.1 %collective-permute-start.8 = (f32[1425]{0:T(1024)S(1)}, f32[1425]{0:T(1024)S(1)}, u32[]{:S(2)}, u32[]{:S(2)}) collective-permute-start(f32[1425]{0:T(1024)S(1)} %reduce_sum.19), channel_id=1, source_target_pairs={{0,3},{1,2},{2,1},{3,0},{4,7},{5,6},{6,5},{7,4},{8,11},{9,10},{10,... | collective-permute-start | bytes 17108 | tf_op jit(solution)/shard_map/ppermute | solution.py:637

commit v4 on v3

--- a/solution.py
+++ b/solution.py
@@ -160,6 +160,24 @@
         a_ref[pl.ds(first + 1, rows), :] += jnp.where(keep, 0.0, value)
 
 
+def repeat(weight, out_ref, times):
+    out_ref[...] = jnp.zeros_like(out_ref)
+    rows, width = weight.shape
+    wide = widen(weight)
+    for part in range(times):
+        tile, shift = divmod(width * part, 128)
+        out_ref[rows * part : rows * (part + 1), 128 * tile : 128 * (tile + 1)] = roll(
+            wide, shift
+        ).astype(BF16)
+
+
+def blocks_sum(ref, rows, width, times):
+    total = sum(
+        roll(ref[rows * part : rows * (part + 1), :], -width * part) for part in range(times)
+    )
+    return jnp.where(iota((rows, 128), 1) < width, total, 0.0)
+
+
 def column(rows):
     return rows.T[:, 0:1]
 
@@ -189,13 +207,20 @@
     ie,
     ee,
     blk,
-    _,
-    _,
+    w2t_s,
+    w2_s,
+    u1t_s,
+    u1_s,
+    u2t_s,
+    u2_s,
     tri_s,
     g64,
     g32,
     g16,
     gw1,
+    gw2,
+    gu1,
+    gu2,
     gb2,
     gc1,
     gc2,
@@ -214,7 +239,7 @@
     def _():
         assemble(me_ref[1], shard, shard_refs, a_ref)
         unpack(a_ref, r64, r32, r16)
-        for ref in (g64, g32, g16, gw1, gb2, gc1, gc2, gd1, gs2, gdd, loss_s):
+        for ref in (g64, g32, g16, gw1, gw2, gu1, gu2, gb2, gc1, gc2, gd1, gs2, gdd, loss_s):
             ref[...] = jnp.zeros_like(ref)
         before = (iota((n, n), 0) < iota((n, n), 1)) & (
             (iota((n, n), 0) < RAY) == (iota((n, n), 1) < RAY)
@@ -225,22 +250,24 @@
         ).T[:64]
         for view in range(views):
             blk[64 * view : 64 * (view + 1), :] = roll(w1t, STRIP * view).astype(BF16)
+        w2 = r32[0:64, :][:, :32]
+        u1a = r32[65:97, :][:, :32]
+        u2 = r16[4:36, :][:, :16]
+        repeat(w2.T, w2t_s, views)
+        repeat(w2, w2_s, views)
+        repeat(u1a.T, u1t_s, views)
+        repeat(u1a, u1_s, views)
+        repeat(u2.T, u2t_s, views)
+        repeat(u2, u2_s, views)
 
     for k, ref in enumerate((x0, x1, x2, x3)):
         xs[me ^ k] = ref[0]
 
-    w2 = r32[0:64, :][:, :32]
-    w2b = w2.astype(BF16)
-    w2t = w2.T.astype(BF16)
     b2 = column(r32[64:72, :])[:32]
-    u1 = r32[65:129, :][:, :32]
-    u1b = u1.astype(BF16)
-    u1at = u1[:32].T.astype(BF16)
-    u1bt = u1[32:].T.astype(BF16)
+    u1b = r32[97:129, :][:, :32]
+    u1bt = u1b.T.astype(BF16)
+    u1b = u1b.astype(BF16)
     c1 = column(r32[129:137, :])[:32]
-    u2 = r16[4:36, :][:, :16]
-    u2b = u2.astype(BF16)
-    u2t = u2.T.astype(BF16)
     c2 = column(r16[36:44, :])[:16]
     keep16 = iota((48, 128), 1) < 16
     qkv = sum(
@@ -261,29 +288,37 @@
     s2 = column(r16[310:318, :])[:16]
     d2 = r16[311:312, 0:1]
 
-    def seen_of(view):
-        at = STRIP * (view % views)
-        return xs[view // views, at : at + STRIP, :].astype(F32)
+    def strip_of(group, local):
+        at = STRIP * local + 32
+        strip = xs[group, at : at + 8, :].astype(F32)
+        return strip[0:3], strip[4:5]
+
+    def stack(values):
+        return jnp.concatenate(values, axis=0) if len(values) > 1 else values[0]
+
+    def cut(value, rows, local):
+        return value[rows * local : rows * (local + 1)]
+
+    counts = [min(views, SEEN_VIEWS - at) for at in range(0, SEEN_VIEWS, views)]
 
     sum1 = jnp.zeros((32, n), F32)
     sum2 = jnp.zeros((32, n), F32)
     seen = jnp.zeros((1, n), F32)
-    for group in range(-(-SEEN_VIEWS // views)):
-        count = min(views, SEEN_VIEWS - group * views)
-        pre = dot(blk[0 : 64 * count, 0 : views * STRIP], xs[group])
+    for group, count in enumerate(counts):
+        wide, thin = 64 * count, 32 * count
+        value, slope = elu_pair(dot(blk[0:wide, 0 : views * STRIP], xs[group]))
+        hidden = value.astype(BF16)
+        hb[group, 0:wide] = hidden
+        he[group, 0:wide] = slope
+        value, slope = elu_pair(dot(w2t_s[0:thin, 0:wide], hidden) + stack([b2] * count))
+        ff[group, 0:thin] = value
+        fe[group, 0:thin] = slope
         for local in range(count):
-            view = group * views + local
-            value, slope = elu_pair(pre[64 * local : 64 * (local + 1)])
-            hidden = value.astype(BF16)
-            hb[view] = hidden
-            he[view] = slope
-            value, slope = elu_pair(dot(w2t, hidden) + b2)
-            ff[view] = value
-            fe[view] = slope
-            vis = seen_of(view)[CHANNELS + 1 : CHANNELS + 2]
-            part = vis * value
+            vis = strip_of(group, local)[1]
+            one = cut(value, 32, local)
+            part = vis * one
             sum1 = sum1 + part
-            sum2 = sum2 + part * value
+            sum2 = sum2 + part * one
             seen = seen + vis
     average = sum1 / seen
     variance = sum2 / seen - average * average
@@ -292,20 +327,23 @@
     num = jnp.zeros((16, n), F32)
     den = jnp.zeros((16, n), F32)
     col = jnp.zeros((3, n), F32)
-    for view in range(SEEN_VIEWS):
-        strip = seen_of(view)
-        feature = ff[view]
-        joined = (feature - average).astype(BF16)
-        jb[view] = joined
-        value, slope = elu_pair(dot(u1at, joined) + shared)
+    for group, count in enumerate(counts):
+        thin, low = 32 * count, 16 * count
+        feature = ff[group, 0:thin]
+        joined = (feature - stack([average] * count)).astype(BF16)
+        jb[group, 0:thin] = joined
+        value, slope = elu_pair(dot(u1t_s[0:thin, 0:thin], joined) + stack([shared] * count))
         inner = value.astype(BF16)
-        ib[view] = inner
-        ie[view] = slope
-        e = strip[CHANNELS + 1 : CHANNELS + 2] * jnp.exp(dot(u2t, inner) + c2)
-        ee[view] = e
-        num = num + e * feature[:16]
-        den = den + e
-        col = col + e[0:1] * strip[32:35]
+        ib[group, 0:thin] = inner
+        ie[group, 0:thin] = slope
+        raw = jnp.exp(dot(u2t_s[0:low, 0:thin], inner) + stack([c2] * count))
+        for local in range(count):
+            rgb, vis = strip_of(group, local)
+            e = vis * cut(raw, 16, local)
+            ee[group, 16 * local : 16 * (local + 1)] = e
+            num = num + e * feature[32 * local : 32 * local + 16]
+            den = den + e
+            col = col + e[0:1] * rgb
 
     inv = 1.0 / den
     tokens = num / den
@@ -433,32 +471,29 @@
     d_average = jnp.zeros((32, n), F32)
     d_shared = jnp.zeros((32, n), F32)
     sum_c2 = jnp.zeros((16, n), F32)
-    grad_u2 = jnp.zeros((32, 16), F32)
-    grad_u1 = jnp.zeros((32, 32), F32)
-    for view in range(SEEN_VIEWS):
-        strip = seen_of(view)
-        e = ee[view]
-        feature = ff[view]
-        d_e = d_num * feature[:16] + d_den
-        d_e = d_e + jnp.where(
-            row16 == 0, jnp.sum(d_col * strip[32:35], axis=0, keepdims=True), 0.0
-        )
-        d_logit = d_e * e
-        sum_c2 = sum_c2 + d_logit
-        pieces = parts(d_logit, PASSES)
-        grad_u2 = grad_u2 + sum(dot(ib[view], piece, NT) for piece in pieces)
-        d_inner = sum(dot(u2b, piece) for piece in pieces) * ie[view]
-        d_shared = d_shared + d_inner
+    for group, count in enumerate(counts):
+        thin, low = 32 * count, 16 * count
+        d_logit = []
+        for local in range(count):
+            rgb, _ = strip_of(group, local)
+            e = ee[group, 16 * local : 16 * (local + 1)]
+            d_e = d_num * ff[group, 32 * local : 32 * local + 16] + d_den
+            d_e = d_e + jnp.where(row16 == 0, jnp.sum(d_col * rgb, axis=0, keepdims=True), 0.0)
+            d_logit.append(d_e * e)
+            sum_c2 = sum_c2 + d_logit[-1]
+            ee[group, 16 * local : 16 * (local + 1)] = d_num * e
+        pieces = parts(stack(d_logit), PASSES)
+        gu2[0:thin, 0:low] += sum(dot(ib[group, 0:thin], piece, NT) for piece in pieces)
+        d_inner = sum(dot(u2_s[0:thin, 0:low], piece) for piece in pieces) * ie[group, 0:thin]
         pieces = parts(d_inner, PASSES)
-        grad_u1 = grad_u1 + sum(dot(jb[view], piece, NT) for piece in pieces)
-        d_joined = sum(dot(u1b[:32], piece) for piece in pieces)
-        d_average = d_average - d_joined
-        ee[view] = d_num * e
-        ie[view] = d_joined
+        gu1[0:thin, 0:thin] += sum(dot(jb[group, 0:thin], piece, NT) for piece in pieces)
+        d_joined = sum(dot(u1_s[0:thin, 0:thin], piece) for piece in pieces)
+        ie[group, 0:thin] = d_joined
+        for local in range(count):
+            d_shared = d_shared + cut(d_inner, 32, local)
+            d_average = d_average - cut(d_joined, 32, local)
     pieces = parts(d_shared, PASSES)
-    d_variance = sum(dot(u1b[32:], piece) for piece in pieces)
-    g16[4:36, :] += widen(grad_u2)
-    g32[65:97, :] += widen(grad_u1)
+    d_variance = sum(dot(u1b, piece) for piece in pieces)
     g32[97:129, :] += widen(sum(dot(variance_low, piece, NT) for piece in pieces))
     gc1[...] += d_shared
     gc2[...] += sum_c2
@@ -466,30 +501,31 @@
     d_square = d_variance * inv_seen
     d_sum = (d_average - 2.0 * average * d_variance) * inv_seen
 
-    grad_w2 = jnp.zeros((64, 32), F32)
     sum_b2 = jnp.zeros((32, n), F32)
-    for group in range(-(-SEEN_VIEWS // views)):
-        count = min(views, SEEN_VIEWS - group * views)
-        d_hidden = []
+    for group, count in enumerate(counts):
+        wide, thin = 64 * count, 32 * count
+        d_feature = []
         for local in range(count):
-            view = group * views + local
-            vis = seen_of(view)[CHANNELS + 1 : CHANNELS + 2]
-            d_feature = ie[view] + vis * (d_sum + 2.0 * ff[view] * d_square)
-            d_feature = d_feature + jnp.concatenate([ee[view], jnp.zeros((16, n), F32)], axis=0)
-            d_feature = d_feature * fe[view]
-            sum_b2 = sum_b2 + d_feature
-            pieces = parts(d_feature, PASSES)
-            grad_w2 = grad_w2 + sum(dot(hb[view], piece, NT) for piece in pieces)
-            d_hidden.append(sum(dot(w2b, piece) for piece in pieces) * he[view])
-        d_hidden = jnp.concatenate(d_hidden, axis=0)
-        gw1[:, 0 : 64 * count] += dot_right(xs[group], d_hidden, NT)
-    g32[0:64, :] += widen(grad_w2)
+            at = slice(32 * local, 32 * (local + 1))
+            vis = strip_of(group, local)[1]
+            d_one = ie[group, at] + vis * (d_sum + 2.0 * ff[group, at] * d_square)
+            kept = ee[group, 16 * local : 16 * (local + 1)]
+            d_one = jnp.concatenate([d_one[:16] + kept, d_one[16:]], axis=0) * fe[group, at]
+            sum_b2 = sum_b2 + d_one
+            d_feature.append(d_one)
+        pieces = parts(stack(d_feature), PASSES)
+        gw2[0:wide, 0:thin] += sum(dot(hb[group, 0:wide], piece, NT) for piece in pieces)
+        d_hidden = sum(dot(w2_s[0:wide, 0:thin], piece) for piece in pieces) * he[group, 0:wide]
+        gw1[:, 0:wide] += dot_right(xs[group], d_hidden, NT)
     gb2[...] += sum_b2
 
     @pl.when(step == pl.num_programs(0) - 1)
     def _():
         ones = jnp.ones((8, n), BF16)
         row_of = lambda ref: widen(dot_right(ones, ref[...], NT, 3)[0:1])
+        g32[0:64, :] = blocks_sum(gw2, 64, 32, views)
+        g32[65:97, :] = blocks_sum(gu1, 32, 32, views)
+        g16[4:36, :] = blocks_sum(gu2, 32, 16, views)
         g32[64:65, :] = row_of(gb2)
         g32[129:130, :] = row_of(gc1)
         g16[36:37, :] = row_of(gc2)
@@ -517,7 +553,6 @@
     views = rows // STRIP
     n = CHUNK
     steps = points // n
-    v = SEEN_VIEWS
     whole = deltas.shape[0] // 2
     pairs = deltas.reshape(whole, 1, n)
     target_pairs = jnp.pad(
@@ -548,22 +583,29 @@
                 vm((144, 128), F32),
                 vm((320, 128), F32),
                 vm((4, rows, n), BF16),
-                vm((v, 64, n), BF16),
-                vm((v, 64, n), F32),
-                vm((v, 32, n), F32),
-                vm((v, 32, n), F32),
-                vm((v, 32, n), BF16),
-                vm((v, 32, n), BF16),
-                vm((v, 32, n), F32),
-                vm((v, 16, n), F32),
+                vm((4, 64 * views, n), BF16),
+                vm((4, 64 * views, n), F32),
+                vm((4, 32 * views, n), F32),
+                vm((4, 32 * views, n), F32),
+                vm((4, 32 * views, n), BF16),
+                vm((4, 32 * views, n), BF16),
+                vm((4, 32 * views, n), F32),
+                vm((4, 16 * views, n), F32),
                 vm((64 * views, 128), BF16),
-                vm((8, 128), BF16),
-                vm((8, 128), BF16),
+                vm((32 * views, 256), BF16),
+                vm((64 * views, 128), BF16),
+                vm((32 * views, 128), BF16),
+                vm((32 * views, 128), BF16),
+                vm((16 * views, 128), BF16),
+                vm((32 * views, 128), BF16),
                 vm((n, n), BF16),
                 vm((40, 128), F32),
                 vm((136, 128), F32),
                 vm((312, 128), F32),
                 vm((rows, 256), F32),
+                vm((64 * views, 128), F32),
+                vm((32 * views, 128), F32),
+                vm((32 * views, 128), F32),
                 vm((32, n), F32),
                 vm((32, n), F32),
                 vm((16, n), F32),

time: 68.3 us -> 65.6 us (0.960)
  Pallas kernels: 32.9 us -> 30.2 us
    pallas_call x1, Pallas kernels: 19.8 us -> 17.1 us  [run_main(): pl.pallas_call(lambda *refs: main_kernel(views, shard, *refs), out_shape=...]
  transfers between devices with their start and end apart: 9 -> 9, of which waited for: 3 -> 3; matrix products, arithmetic and copies ran while one was open for 2% -> 2% of each run, Pallas kernels for 19% -> 20%
where the time goes in v4:
time: 65.6 us; the launch traced here: 65.3 us
  Pallas kernels  30.2 us (46%)
  starting transfers between devices  11.5 us (18%)
  blocking collectives  10.4 us (16%)
  between operations  4.03 us (6%)
  waiting for transfers between devices  3.86 us (6%)
  local copies, waits for them, and re-layouts  2.92 us (4%)
  other arithmetic  2.41 us (4%)
    pallas_call x1, Pallas kernels, run_main(): pl.pallas_call(lambda *refs: main_kernel(views, shard, *refs), out_shape=...  17.1 us
    pallas_call x3, Pallas kernels, gather_rows(): pl.pallas_call(lambda *refs: gather_kernel(views, tile, count, *refs), ou...  13.2 us
    all_to_all x1, blocking collectives, body(): got = lax.all_to_all(send, 'rays', 0, 0, tiled=True)  10.4 us
    ppermute x3, starting transfers between devices, body(): lax.ppermute(held, 'rays', swap(shards, 1 << link))  7.26 us
    ppermute x3, waiting for transfers between devices, body(): lax.ppermute(partial, 'views', [(i, i ^ k) for i in range(group)])  2.11 us
    ppermute x3, starting transfers between devices, body(): lax.ppermute(partial, 'views', [(i, i ^ k) for i in range(group)])  1.92 us
    unnamed x16, local copies, waits for them, and re-layouts  1.85 us
    ppermute x3, waiting for transfers between devices, body(): lax.ppermute(held, 'rays', swap(shards, 1 << link))  1.74 us
  transfers between devices with their start and end apart: 9, of which 3 were waited for; matrix products, arithmetic and copies ran while one was open for 2% of the time, Pallas kernels for 20%

profile of v4, /device:TPU:0, one launch (start us, length us, event | category | flops | bytes accessed | tf_op | source)
XLA Modules:
  0.0 65.3 jit_solution(10228978784295157329)
XLA Ops:
  0.6 0.7 %convert_element_type.17 = bf16[1423]{0:T(1024)(128)(2,1)S(1)} convert(f32[1423]{0:T(1024)} %param.11) | non-fusion elementwise | flops 1423 | bytes 8538 | tf_op jit(solution)/shard_map/convert_element_type | solution.py:654
  1.3 3.0 %collective-permute-start = (bf16[1,16,128]{2,1,0:T(8,128)(2,1)S(1)}, bf16[1,16,128]{2,1,0:T(8,128)(2,1)S(1)}, u32[]{:S(2)}, u32[]{:S(2)}) collective-permute-start(bf16[1,16,128]{2,1,0:T(8,128)(2,1)S(1)} %pad_bitcast_fusion), channel_id=1, source_target_pairs={{0,4},{4,0},{8,12},{12,8},{16,20},{20,16},{24,28},{28,24},{1,5},{5... | collective-permute-start | bytes 12296 | tf_op jit(solution)/shard_map/ppermute | solution.py:659
  4.3 0.1 pad_add_fusion.refs_0_
  4.4 0.8 %add_bitcast_fusion.refs_1_.refs_2_ = s32[3,3072]{1,0:T(4,128)S(1)} fusion(s32[3072,3]{0,1:T(4,128)} %param.16, s32[3072,3]{0,1:T(4,128)} %param.17), kind=kLoop, calls=%fused_computation.2 | loop fusion | flops 18432 | bytes 110592 | tf_op jit(solution)/shard_map/add | solution.py:655
  5.2 0.0 copy-start
  5.2 1.8 %copy-done = bf16[3,35,12032]{2,1,0:T(8,128)(2,1)S(1)} copy-done((bf16[3,35,12032]{2,1,0:T(8,128)(2,1)S(1)}, bf16[3,35,12032]{2,1,0:T(8,128)(2,1)}, u32[]{:S(2)}) %copy-start) | copy-done | bytes 2526744
  7.0 5.9 %shard_map.140 = (bf16[1,120,768]{2,1,0:T(8,128)(2,1)S(1)}, bf16[1,120,768]{2,1,0:T(8,128)(2,1)S(1)}) custom-call(s32[2]{0:T(128)S(1)} %pad_add_fusion.refs_0_, s32[3,3072]{1,0:T(4,128)S(1)} %add_bitcast_fusion.refs_1_.refs_2_, s32[3,3072]{1,0:T(4,128)S(1)} %add_bitcast_fusion.refs_1_.refs_2_, bf16[3,35,12032]{2,1,0:T(8,128)(2,1)S(1)} %copy-done), custom_call_target="tpu_custom_call" | custom-call | flops 4435476480 | bytes 2526720 | tf_op jit(solution)/shard_map/pallas_call | solution.py:120
  12.9 1.6 %collective-permute-start.4 = (bf16[1,120,768]{2,1,0:T(8,128)(2,1)S(1)}, bf16[1,120,768]{2,1,0:T(8,128)(2,1)S(1)}, u32[]{:S(2)}, u32[]{:S(2)}) collective-permute-start(bf16[1,120,768]{2,1,0:T(8,128)(2,1)S(1)} %get-tuple-element.6), channel_id=1, source_target_pairs={{0,2},{1,3},{2,0},{3,1},{4,6},{5,7},{6,4},{7,5},{8,10},{9,11},{10,... | collective-permute-start | bytes 552968 | tf_op jit(solution)/shard_map/ppermute | solution.py:662
  14.5 0.0 collective-permute-start.5
  14.5 3.7 %shard_map.139 = bf16[1,120,768]{2,1,0:T(8,128)(2,1)S(1)} custom-call(s32[2]{0:T(128)S(1)} %pad_add_fusion.refs_0_, s32[3,3072]{1,0:T(4,128)S(1)} %add_bitcast_fusion.refs_1_.refs_2_, bf16[3,35,12032]{2,1,0:T(8,128)(2,1)S(1)} %copy-done), custom_call_target="tpu_custom_call" | custom-call | flops 2217738240 | bytes 2526720 | tf_op jit(solution)/shard_map/pallas_call | solution.py:120
  18.2 0.7 %collective-permute-start.3 = (bf16[1,120,768]{2,1,0:T(8,128)(2,1)S(1)}, bf16[1,120,768]{2,1,0:T(8,128)(2,1)S(1)}, u32[]{:S(2)}, u32[]{:S(2)}) collective-permute-start(bf16[1,120,768]{2,1,0:T(8,128)(2,1)S(1)} %shard_map.139), channel_id=1, source_target_pairs={{0,1},{1,0},{2,3},{3,2},{4,5},{5,4},{6,7},{7,6},{8,9},{9,8},{10,11... | collective-permute-start | bytes 552968 | tf_op jit(solution)/shard_map/ppermute | solution.py:664
  18.8 0.0 collective-permute-done
  18.9 0.0 copy-start.7
  18.9 0.0 copy-start.5
  18.9 0.0 copy-start.2
  18.9 0.0 copy-start.1
  18.9 0.0 copy-start.3
  18.9 0.0 copy-start.4
  18.9 1.6 %collective-permute-start.1 = (bf16[2,16,128]{2,1,0:T(8,128)(2,1)S(1)}, bf16[2,16,128]{2,1,0:T(8,128)(2,1)S(1)}, u32[]{:S(2)}, u32[]{:S(2)}) collective-permute-start(bf16[2,16,128]{2,1,0:T(8,128)(2,1)S(1)} %pad_maximum_fusion.3), channel_id=1, source_target_pairs={{0,8},{4,12},{8,0},{12,4},{16,24},{20,28},{24,16},{28,20},{1,9},{5... | collective-permute-start | bytes 24584 | tf_op jit(solution)/shard_map/ppermute | solution.py:659
  20.6 3.7 %shard_map.138.refs_2_ = bf16[1,120,768]{2,1,0:T(8,128)(2,1)S(1)} custom-call(s32[2]{0:T(128)S(1)} %pad_add_fusion.refs_0_, s32[3,3072]{1,0:T(4,128)S(1)} %add_bitcast_fusion.refs_1_.refs_2_, bf16[3,35,12032]{2,1,0:T(8,128)(2,1)S(1)} %copy-done), custom_call_target="tpu_custom_call" | custom-call | flops 2217738240 | bytes 2526720 | tf_op jit(solution)/shard_map/pallas_call | solution.py:120
  24.2 0.0 copy-done.6
  24.3 0.0 collective-permute-done.1
  24.3 2.7 %collective-permute-start.2 = (bf16[4,16,128]{2,1,0:T(8,128)(2,1)S(1)}, bf16[4,16,128]{2,1,0:T(8,128)(2,1)S(1)}, u32[]{:S(2)}, u32[]{:S(2)}) collective-permute-start(bf16[4,16,128]{2,1,0:T(8,128)(2,1)S(1)} %pad_maximum_fusion.2), channel_id=1, source_target_pairs={{0,16},{4,20},{8,24},{12,28},{16,0},{20,4},{24,8},{28,12},{1,17},{... | collective-permute-start | bytes 49160 | tf_op jit(solution)/shard_map/ppermute | solution.py:659
  26.9 0.0 copy-done.7
  26.9 0.1 select_reduce_fusion
  27.0 0.0 copy-done.5
  27.0 0.1 reshape.35
  27.1 0.1 reshape.36
  27.2 0.0 copy-done.2
  27.2 0.1 reshape.34.refs_6_
  27.3 1.7 %collective-permute-done.2 = bf16[4,16,128]{2,1,0:T(8,128)(2,1)S(1)} collective-permute-done((bf16[4,16,128]{2,1,0:T(8,128)(2,1)S(1)}, bf16[4,16,128]{2,1,0:T(8,128)(2,1)S(1)}, u32[]{:S(2)}, u32[]{:S(2)}) %collective-permute-start.2) | collective-permute-done | bytes 16416 | tf_op jit(solution)/shard_map/ppermute | solution.py:659
  29.0 0.0 collective-permute-done.4.refs_4_
  29.1 0.0 collective-permute-done.5.refs_5_
  29.1 0.0 collective-permute-done.3.refs_3_
  29.1 17.1 %shard_map.141 = f32[104,128]{1,0:T(8,128)S(1)} custom-call(s32[2]{0:T(128)S(1)} %pad_add_fusion.refs_0_, bf16[8,16,128]{2,1,0:T(8,128)(2,1)S(1)} %pad_maximum_fusion.1.refs_1_, bf16[1,120,768]{2,1,0:T(8,128)(2,1)S(1)} %shard_map.138.refs_2_, bf16[1,120,768]{2,1,0:T(8,128)(2,1)S(1)} %collective-permute-done.3.refs_3_, ...), custom_call_target="tpu_custom_call" | custom-call | tf_op jit(solution)/shard_map/pallas_call | solution.py:566
  46.2 0.1 reshape.38
  46.3 0.1 pad.16.clone
  46.4 10.4 %all_to_all.9 = f32[8,1,1425]{2,1,0:T(1,128)S(1)} all-to-all(f32[8,1,1425]{2,1,0:T(1,128)S(1)} %all_to_all.6), channel_id=1, replica_groups=mesh['rays'=8,'views'=4] {'rays'}, dimensions={0} | all-to-all | bytes 91200 | tf_op jit(solution)/shard_map/all_to_all | solution.py:675
  56.8 0.1 collective-permute-start.6
  56.9 1.6 %collective-permute-start.7 = (f32[1425]{0:T(1024)S(1)}, f32[1425]{0:T(1024)S(1)}, u32[]{:S(2)}, u32[]{:S(2)}) collective-permute-start(f32[1425]{0:T(1024)S(1)} %reduce_sum.19), channel_id=1, source_target_pairs={{0,2},{1,3},{2,0},{3,1},{4,6},{5,7},{6,4},{7,5},{8,10},{9,11},{10,... | collective-permute-start | bytes 17108 | tf_op jit(solution)/shard_map/ppermute | solution.py:679
  58.5 0.3 collective-permute-start.8
  59.4 0.0 collective-permute-done.6
  59.5 1.2 %collective-permute-done.7 = f32[1425]{0:T(1024)S(1)} collective-permute-done((f32[1425]{0:T(1024)S(1)}, f32[1425]{0:T(1024)S(1)}, u32[]{:S(2)}, u32[]{:S(2)}) %collective-permute-start.7) | collective-permute-done | bytes 5732 | tf_op jit(solution)/shard_map/ppermute | solution.py:679
  60.6 0.9 %collective-permute-done.8 = f32[1425]{0:T(1024)S(1)} collective-permute-done((f32[1425]{0:T(1024)S(1)}, f32[1425]{0:T(1024)S(1)}, u32[]{:S(2)}, u32[]{:S(2)}) %collective-permute-start.8) | collective-permute-done | bytes 5732 | tf_op jit(solution)/shard_map/ppermute | solution.py:679
  61.6 0.6 fusion.2
  63.5 0.0 copy-done.1
  63.5 0.0 copy-done.3
  63.5 0.6 multiply_subtract_fusion
  (16 shorter events, 0.2 us)
Async XLA Ops:
  1.3 17.5 %collective-permute-start = (bf16[1,16,128]{2,1,0:T(8,128)(2,1)S(1)}, bf16[1,16,128]{2,1,0:T(8,128)(2,1)S(1)}, u32[]{:S(2)}, u32[]{:S(2)}) collective-permute-start(bf16[1,16,128]{2,1,0:T(8,128)(2,1)S(1)} %pad_bitcast_fusion), channel_id=1, source_target_pairs={{0,4},{4,0},{8,12},{12,8},{16,20},{20,16},{24,28},{28,24},{1,5},{5... | collective-permute-start | bytes 12296 | tf_op jit(solution)/shard_map/ppermute | solution.py:659
  5.2 1.8 %copy-start = (bf16[3,35,12032]{2,1,0:T(8,128)(2,1)S(1)}, bf16[3,35,12032]{2,1,0:T(8,128)(2,1)}, u32[]{:S(2)}) copy-start(bf16[3,35,12032]{2,1,0:T(8,128)(2,1)} %refs_3_.1) | copy-start | bytes 7580164
  12.9 16.1 %collective-permute-start.4 = (bf16[1,120,768]{2,1,0:T(8,128)(2,1)S(1)}, bf16[1,120,768]{2,1,0:T(8,128)(2,1)S(1)}, u32[]{:S(2)}, u32[]{:S(2)}) collective-permute-start(bf16[1,120,768]{2,1,0:T(8,128)(2,1)S(1)} %get-tuple-element.6), channel_id=1, source_target_pairs={{0,2},{1,3},{2,0},{3,1},{4,6},{5,7},{6,4},{7,5},{8,10},{9,11},{10,... | collective-permute-start | bytes 552968 | tf_op jit(solution)/shard_map/ppermute | solution.py:662
  14.5 14.6 %collective-permute-start.5 = (bf16[1,120,768]{2,1,0:T(8,128)(2,1)S(1)}, bf16[1,120,768]{2,1,0:T(8,128)(2,1)S(1)}, u32[]{:S(2)}, u32[]{:S(2)}) collective-permute-start(bf16[1,120,768]{2,1,0:T(8,128)(2,1)S(1)} %get-tuple-element.7), channel_id=1, source_target_pairs={{0,3},{1,2},{2,1},{3,0},{4,7},{5,6},{6,5},{7,4},{8,11},{9,10},{10,... | collective-permute-start | bytes 552968 | tf_op jit(solution)/shard_map/ppermute | solution.py:661
  18.2 10.9 %collective-permute-start.3 = (bf16[1,120,768]{2,1,0:T(8,128)(2,1)S(1)}, bf16[1,120,768]{2,1,0:T(8,128)(2,1)S(1)}, u32[]{:S(2)}, u32[]{:S(2)}) collective-permute-start(bf16[1,120,768]{2,1,0:T(8,128)(2,1)S(1)} %shard_map.139), channel_id=1, source_target_pairs={{0,1},{1,0},{2,3},{3,2},{4,5},{5,4},{6,7},{7,6},{8,9},{9,8},{10,11... | collective-permute-start | bytes 552968 | tf_op jit(solution)/shard_map/ppermute | solution.py:664
  18.9 5.4 %copy-start.6 = (s32[8]{0:T(128)S(1)}, s32[8]{0:T(128)}, u32[]{:S(2)}) copy-start(s32[8]{0:T(128)} %param.21) | copy-start | bytes 100
  18.9 8.1 %copy-start.7 = (s32[16]{0:T(128)S(1)}, s32[16]{0:T(128)}, u32[]{:S(2)}) copy-start(s32[16]{0:T(128)} %param.20) | copy-start | bytes 196
  18.9 8.2 %copy-start.5 = (f32[16,3]{0,1:T(4,128)S(1)}, f32[16,3]{0,1:T(4,128)}, u32[]{:S(2)}) copy-start(f32[16,3]{0,1:T(4,128)} %param.19) | copy-start | bytes 580
  18.9 8.3 %copy-start.2 = (f32[16,192]{1,0:T(8,128)S(1)}, f32[16,192]{1,0:T(8,128)}, u32[]{:S(2)}) copy-start(f32[16,192]{1,0:T(8,128)} %param.18) | copy-start | bytes 36868
  18.9 44.6 %copy-start.1 = (f32[1423]{0:T(1024)S(1)}, f32[1423]{0:T(1024)}, u32[]{:S(2)}) copy-start(f32[1423]{0:T(1024)} %param.11) | copy-start | bytes 17080
  18.9 44.6 %copy-start.3 = (f32[1423]{0:T(1024)S(1)}, f32[1423]{0:T(1024)}, u32[]{:S(2)}) copy-start(f32[1423]{0:T(1024)} %param.13) | copy-start | bytes 17080
  18.9 44.6 %copy-start.4 = (f32[1423]{0:T(1024)S(1)}, f32[1423]{0:T(1024)}, u32[]{:S(2)}) copy-start(f32[1423]{0:T(1024)} %param.12) | copy-start | bytes 17080
  18.9 5.3 %collective-permute-start.1 = (bf16[2,16,128]{2,1,0:T(8,128)(2,1)S(1)}, bf16[2,16,128]{2,1,0:T(8,128)(2,1)S(1)}, u32[]{:S(2)}, u32[]{:S(2)}) collective-permute-start(bf16[2,16,128]{2,1,0:T(8,128)(2,1)S(1)} %pad_maximum_fusion.3), channel_id=1, source_target_pairs={{0,8},{4,12},{8,0},{12,4},{16,24},{20,28},{24,16},{28,20},{1,9},{5... | collective-permute-start | bytes 24584 | tf_op jit(solution)/shard_map/ppermute | solution.py:659
  24.3 4.8 %collective-permute-start.2 = (bf16[4,16,128]{2,1,0:T(8,128)(2,1)S(1)}, bf16[4,16,128]{2,1,0:T(8,128)(2,1)S(1)}, u32[]{:S(2)}, u32[]{:S(2)}) collective-permute-start(bf16[4,16,128]{2,1,0:T(8,128)(2,1)S(1)} %pad_maximum_fusion.2), channel_id=1, source_target_pairs={{0,16},{4,20},{8,24},{12,28},{16,0},{20,4},{24,8},{28,12},{1,17},{... | collective-permute-start | bytes 49160 | tf_op jit(solution)/shard_map/ppermute | solution.py:659
  56.8 2.6 %collective-permute-start.6 = (f32[1425]{0:T(1024)S(1)}, f32[1425]{0:T(1024)S(1)}, u32[]{:S(2)}, u32[]{:S(2)}) collective-permute-start(f32[1425]{0:T(1024)S(1)} %reduce_sum.19), channel_id=1, source_target_pairs={{0,1},{1,0},{2,3},{3,2},{4,5},{5,4},{6,7},{7,6},{8,9},{9,8},{10,11... | collective-permute-start | bytes 17108 | tf_op jit(solution)/shard_map/ppermute | solution.py:679
  56.9 3.7 %collective-permute-start.7 = (f32[1425]{0:T(1024)S(1)}, f32[1425]{0:T(1024)S(1)}, u32[]{:S(2)}, u32[]{:S(2)}) collective-permute-start(f32[1425]{0:T(1024)S(1)} %reduce_sum.19), channel_id=1, source_target_pairs={{0,2},{1,3},{2,0},{3,1},{4,6},{5,7},{6,4},{7,5},{8,10},{9,11},{10,... | collective-permute-start | bytes 17108 | tf_op jit(solution)/shard_map/ppermute | solution.py:679
  58.5 3.1 %collective-permute-start.8 = (f32[1425]{0:T(1024)S(1)}, f32[1425]{0:T(1024)S(1)}, u32[]{:S(2)}, u32[]{:S(2)}) collective-permute-start(f32[1425]{0:T(1024)S(1)} %reduce_sum.19), channel_id=1, source_target_pairs={{0,3},{1,2},{2,1},{3,0},{4,7},{5,6},{6,5},{7,4},{8,11},{9,10},{10,... | collective-permute-start | bytes 17108 | tf_op jit(solution)/shard_map/ppermute | solution.py:679

commit v5 on v4

--- a/solution.py
+++ b/solution.py
@@ -18,6 +18,7 @@
 RAY = 192
 CHUNK = 2 * RAY
 PASSES = 1
+TILE = 128
 MOMENT_DECAY = 0.5
 SQUARE_DECAY = 0.5
 LEARNING_RATE = 0.05
@@ -206,6 +207,10 @@
     ib,
     ie,
     ee,
+    dl,
+    di,
+    df,
+    dh,
     blk,
     w2t_s,
     w2_s,
@@ -288,9 +293,9 @@
     s2 = column(r16[310:318, :])[:16]
     d2 = r16[311:312, 0:1]
 
-    def strip_of(group, local):
+    def strip_of(group, local, lanes):
         at = STRIP * local + 32
-        strip = xs[group, at : at + 8, :].astype(F32)
+        strip = xs[group, at : at + 8, lanes].astype(F32)
         return strip[0:3], strip[4:5]
 
     def stack(values):
@@ -301,49 +306,58 @@
 
     counts = [min(views, SEEN_VIEWS - at) for at in range(0, SEEN_VIEWS, views)]
 
-    sum1 = jnp.zeros((32, n), F32)
-    sum2 = jnp.zeros((32, n), F32)
-    seen = jnp.zeros((1, n), F32)
-    for group, count in enumerate(counts):
-        wide, thin = 64 * count, 32 * count
-        value, slope = elu_pair(dot(blk[0:wide, 0 : views * STRIP], xs[group]))
-        hidden = value.astype(BF16)
-        hb[group, 0:wide] = hidden
-        he[group, 0:wide] = slope
-        value, slope = elu_pair(dot(w2t_s[0:thin, 0:wide], hidden) + stack([b2] * count))
-        ff[group, 0:thin] = value
-        fe[group, 0:thin] = slope
-        for local in range(count):
-            vis = strip_of(group, local)[1]
-            one = cut(value, 32, local)
-            part = vis * one
-            sum1 = sum1 + part
-            sum2 = sum2 + part * one
-            seen = seen + vis
-    average = sum1 / seen
-    variance = sum2 / seen - average * average
-    variance_low = variance.astype(BF16)
-    shared = dot(u1bt, variance_low) + c1
-    num = jnp.zeros((16, n), F32)
-    den = jnp.zeros((16, n), F32)
-    col = jnp.zeros((3, n), F32)
-    for group, count in enumerate(counts):
-        thin, low = 32 * count, 16 * count
-        feature = ff[group, 0:thin]
-        joined = (feature - stack([average] * count)).astype(BF16)
-        jb[group, 0:thin] = joined
-        value, slope = elu_pair(dot(u1t_s[0:thin, 0:thin], joined) + stack([shared] * count))
-        inner = value.astype(BF16)
-        ib[group, 0:thin] = inner
-        ie[group, 0:thin] = slope
-        raw = jnp.exp(dot(u2t_s[0:low, 0:thin], inner) + stack([c2] * count))
-        for local in range(count):
-            rgb, vis = strip_of(group, local)
-            e = vis * cut(raw, 16, local)
-            ee[group, 16 * local : 16 * (local + 1)] = e
-            num = num + e * feature[32 * local : 32 * local + 16]
-            den = den + e
-            col = col + e[0:1] * rgb
+    m = TILE
+    lane_tiles = [slice(at, at + m) for at in range(0, n, m)]
+    join = lambda values: jnp.concatenate(values, axis=1) if len(values) > 1 else values[0]
+
+    def forward_tile(lanes):
+        sum1 = jnp.zeros((32, m), F32)
+        sum2 = jnp.zeros((32, m), F32)
+        seen = jnp.zeros((1, m), F32)
+        for group, count in enumerate(counts):
+            wide, thin = 64 * count, 32 * count
+            value, slope = elu_pair(dot(blk[0:wide, 0 : views * STRIP], xs[group, :, lanes]))
+            hidden = value.astype(BF16)
+            hb[group, 0:wide, lanes] = hidden
+            he[group, 0:wide, lanes] = slope
+            value, slope = elu_pair(dot(w2t_s[0:thin, 0:wide], hidden) + stack([b2] * count))
+            ff[group, 0:thin, lanes] = value
+            fe[group, 0:thin, lanes] = slope
+            for local in range(count):
+                vis = strip_of(group, local, lanes)[1]
+                one = cut(value, 32, local)
+                part = vis * one
+                sum1 = sum1 + part
+                sum2 = sum2 + part * one
+                seen = seen + vis
+        average = sum1 / seen
+        variance = sum2 / seen - average * average
+        variance_low = variance.astype(BF16)
+        shared = dot(u1bt, variance_low) + c1
+        num = jnp.zeros((16, m), F32)
+        den = jnp.zeros((16, m), F32)
+        col = jnp.zeros((3, m), F32)
+        for group, count in enumerate(counts):
+            thin, low = 32 * count, 16 * count
+            feature = ff[group, 0:thin, lanes]
+            joined = (feature - stack([average] * count)).astype(BF16)
+            jb[group, 0:thin, lanes] = joined
+            value, slope = elu_pair(dot(u1t_s[0:thin, 0:thin], joined) + stack([shared] * count))
+            inner = value.astype(BF16)
+            ib[group, 0:thin, lanes] = inner
+            ie[group, 0:thin, lanes] = slope
+            raw = jnp.exp(dot(u2t_s[0:low, 0:thin], inner) + stack([c2] * count))
+            for local in range(count):
+                rgb, vis = strip_of(group, local, lanes)
+                e = vis * cut(raw, 16, local)
+                ee[group, 16 * local : 16 * (local + 1), lanes] = e
+                num = num + e * feature[32 * local : 32 * local + 16]
+                den = den + e
+                col = col + e[0:1] * rgb
+        return average, 1.0 / seen, variance_low, num, den, col
+
+    done = [forward_tile(lanes) for lanes in lane_tiles]
+    average, inv_seen, variance_low, num, den, col = [join(list(x)) for x in zip(*done)]
 
     inv = 1.0 / den
     tokens = num / den
@@ -351,19 +365,23 @@
     token_low = tokens.astype(BF16)
     token_t = tokens.T.astype(BF16)
     halves = [token_t[RAY * r : RAY * (r + 1)] for r in range(2)]
-    query = dot(wqt, token_low).astype(BF16)
+    query = dot(wqt, token_low).astype(BF16).astype(F32) * 0.25
     kk_f = dot(halves[0], wk_of[0]) + dot(halves[1], wk_of[1])
     vv_f = dot(halves[0], wv_of[0]) + dot(halves[1], wv_of[1])
     kk = kk_f.astype(BF16)
     vv = vv_f.astype(BF16)
     kkt = kk.astype(F32).T.astype(BF16)
     vvt = vv.astype(F32).T.astype(BF16)
-    row64 = iota((64, n), 0)
 
     def spread(value, head):
-        mine = jnp.where((row64 >> 4) == head, value.astype(F32), 0.0)
+        mine = value[16 * head : 16 * (head + 1)].astype(F32)
         one = jnp.where(first_ray, mine, 0.0)
-        return jnp.concatenate([one, mine - one], axis=0)
+        rows = []
+        for part in (one, mine - one):
+            rows += [jnp.zeros((16 * head, n), BF16)] if head else []
+            rows.append(part.astype(BF16))
+            rows += [jnp.zeros((48 - 16 * head, n), BF16)] if head < 3 else []
+        return jnp.concatenate(rows, axis=0)
 
     def fold(value):
         return jnp.where(first_ray, value[:16], value[16:])
@@ -373,16 +391,22 @@
         return jnp.concatenate([value[at : at + 16], value[64 + at : 80 + at]], axis=0)
 
     probs = []
+    lows = []
     attended = []
     query_of = []
     for head in range(4):
-        q_head = spread(query, head).astype(BF16)
+        q_head = spread(query, head)
         query_of.append(q_head)
-        score = dot(kk, q_head) * 0.25
-        score = jnp.exp(score - jnp.max(score, axis=0, keepdims=True))
-        prob = score / jnp.sum(score, axis=0, keepdims=True)
-        probs.append(prob)
-        attended.append(fold(dot(head_rows(vvt, head), prob.astype(BF16))))
+        tiles = []
+        for at in range(0, n, 128):
+            score = dot(kk, q_head[:, at : at + 128])
+            score = jnp.exp(score - jnp.max(score, axis=0, keepdims=True))
+            tiles.append(score * (1.0 / jnp.sum(score, axis=0, keepdims=True)))
+        probs.append(tiles)
+        low = jnp.concatenate([tile.astype(BF16) for tile in tiles], axis=1)
+        lows.append(low)
+        attended.append(fold(dot(head_rows(vvt, head), low)))
+    raw_attended = attended
     attended = jnp.concatenate(attended, axis=0).astype(BF16)
     mixed = tokens + dot(wot, attended)
     mixed_low = mixed.astype(BF16)
@@ -440,15 +464,17 @@
     d_kk = jnp.zeros((RAY, 128), F32)
     d_vv = jnp.zeros((RAY, 128), F32)
     for head in range(4):
-        prob = probs[head]
-        d_head = parts(spread(d_att, head), PASSES)
-        d_prob = sum(dot(vv, piece) for piece in d_head)
-        low = prob.astype(BF16)
-        d_vv = d_vv + sum(dot(low, piece, NT) for piece in d_head)
-        d_score = prob * (d_prob - jnp.sum(prob * d_prob, axis=0, keepdims=True)) * 0.25
-        pieces = parts(d_score, PASSES)
-        d_query.append(fold(sum(dot(head_rows(kkt, head), piece) for piece in pieces)))
-        d_kk = d_kk + sum(dot(piece, query_of[head], NT) for piece in pieces)
+        mine = d_att[16 * head : 16 * (head + 1)]
+        shift = jnp.sum(mine * raw_attended[head], axis=0, keepdims=True)
+        d_head = spread(d_att, head)
+        d_vv = d_vv + dot(lows[head], d_head, NT)
+        tiles = []
+        for place, prob in enumerate(probs[head]):
+            at = slice(128 * place, 128 * (place + 1))
+            tiles.append((prob * (dot(vv, d_head[:, at]) - shift[:, at])).astype(BF16))
+        d_score = jnp.concatenate(tiles, axis=1)
+        d_query.append(fold(dot(head_rows(kkt, head), d_score)) * 0.25)
+        d_kk = d_kk + dot(d_score, query_of[head], NT)
     d_query = jnp.concatenate(d_query, axis=0)
     gq = dot_right(token_low, d_query, NT)
     gk = [dot_right(halves[r], d_kk, TN) for r in range(2)]
@@ -468,56 +494,69 @@
     row16 = iota((16, n), 0)
     d_den = d_den + jnp.where(row16 == 0, d_den0, 0.0)
 
-    d_average = jnp.zeros((32, n), F32)
-    d_shared = jnp.zeros((32, n), F32)
-    sum_c2 = jnp.zeros((16, n), F32)
+    def backward_tile(lanes):
+        own_num, own_den, own_col = d_num[:, lanes], d_den[:, lanes], d_col[:, lanes]
+        d_average = jnp.zeros((32, m), F32)
+        d_shared = jnp.zeros((32, m), F32)
+        sum_c2 = jnp.zeros((16, m), F32)
+        for group, count in enumerate(counts):
+            thin, low = 32 * count, 16 * count
+            d_logit = []
+            for local in range(count):
+                at = slice(16 * local, 16 * (local + 1))
+                rgb, _ = strip_of(group, local, lanes)
+                e = ee[group, at, lanes]
+                d_e = own_num * ff[group, 32 * local : 32 * local + 16, lanes] + own_den
+                shade = jnp.sum(own_col * rgb, axis=0, keepdims=True)
+                d_e = d_e + jnp.where(row16[:, :m] == 0, shade, 0.0)
+                d_logit.append(d_e * e)
+                sum_c2 = sum_c2 + d_logit[-1]
+                ee[group, at, lanes] = own_num * e
+            piece = stack(d_logit).astype(BF16)
+            dl[group, 0:low, lanes] = piece
+            d_inner = dot(u2_s[0:thin, 0:low], piece) * ie[group, 0:thin, lanes]
+            piece = d_inner.astype(BF16)
+            di[group, 0:thin, lanes] = piece
+            d_joined = dot(u1_s[0:thin, 0:thin], piece)
+            ie[group, 0:thin, lanes] = d_joined
+            for local in range(count):
+                d_shared = d_shared + cut(d_inner, 32, local)
+                d_average = d_average - cut(d_joined, 32, local)
+        shared_low = d_shared.astype(BF16)
+        d_variance = dot(u1b, shared_low)
+        gc1[:, lanes] += d_shared
+        gc2[:, lanes] += sum_c2
+        d_square = d_variance * inv_seen[:, lanes]
+        d_sum = (d_average - 2.0 * average[:, lanes] * d_variance) * inv_seen[:, lanes]
+        sum_b2 = jnp.zeros((32, m), F32)
+        for group, count in enumerate(counts):
+            wide, thin = 64 * count, 32 * count
+            d_feature = []
+            for local in range(count):
+                at = slice(32 * local, 32 * (local + 1))
+                vis = strip_of(group, local, lanes)[1]
+                feature = ff[group, at, lanes]
+                d_one = ie[group, at, lanes] + vis * (d_sum + 2.0 * feature * d_square)
+                kept = ee[group, 16 * local : 16 * (local + 1), lanes]
+                d_one = jnp.concatenate([d_one[:16] + kept, d_one[16:]], axis=0)
+                d_one = d_one * fe[group, at, lanes]
+                sum_b2 = sum_b2 + d_one
+                d_feature.append(d_one)
+            piece = stack(d_feature).astype(BF16)
+            df[group, 0:thin, lanes] = piece
+            d_hidden = dot(w2_s[0:wide, 0:thin], piece) * he[group, 0:wide, lanes]
+            dh[group, 0:wide, lanes] = d_hidden.astype(BF16)
+        gb2[:, lanes] += sum_b2
+        return shared_low
+
+    shared_low = join([backward_tile(lanes) for lanes in lane_tiles])
+    g32[97:129, :] += widen(dot(variance_low, shared_low, NT))
     for group, count in enumerate(counts):
-        thin, low = 32 * count, 16 * count
-        d_logit = []
-        for local in range(count):
-            rgb, _ = strip_of(group, local)
-            e = ee[group, 16 * local : 16 * (local + 1)]
-            d_e = d_num * ff[group, 32 * local : 32 * local + 16] + d_den
-            d_e = d_e + jnp.where(row16 == 0, jnp.sum(d_col * rgb, axis=0, keepdims=True), 0.0)
-            d_logit.append(d_e * e)
-            sum_c2 = sum_c2 + d_logit[-1]
-            ee[group, 16 * local : 16 * (local + 1)] = d_num * e
-        pieces = parts(stack(d_logit), PASSES)
-        gu2[0:thin, 0:low] += sum(dot(ib[group, 0:thin], piece, NT) for piece in pieces)
-        d_inner = sum(dot(u2_s[0:thin, 0:low], piece) for piece in pieces) * ie[group, 0:thin]
-        pieces = parts(d_inner, PASSES)
-        gu1[0:thin, 0:thin] += sum(dot(jb[group, 0:thin], piece, NT) for piece in pieces)
-        d_joined = sum(dot(u1_s[0:thin, 0:thin], piece) for piece in pieces)
-        ie[group, 0:thin] = d_joined
-        for local in range(count):
-            d_shared = d_shared + cut(d_inner, 32, local)
-            d_average = d_average - cut(d_joined, 32, local)
-    pieces = parts(d_shared, PASSES)
-    d_variance = sum(dot(u1b, piece) for piece in pieces)
-    g32[97:129, :] += widen(sum(dot(variance_low, piece, NT) for piece in pieces))
-    gc1[...] += d_shared
-    gc2[...] += sum_c2
-    inv_seen = 1.0 / seen
-    d_square = d_variance * inv_seen
-    d_sum = (d_average - 2.0 * average * d_variance) * inv_seen
-
-    sum_b2 = jnp.zeros((32, n), F32)
-    for group, count in enumerate(counts):
-        wide, thin = 64 * count, 32 * count
-        d_feature = []
-        for local in range(count):
-            at = slice(32 * local, 32 * (local + 1))
-            vis = strip_of(group, local)[1]
-            d_one = ie[group, at] + vis * (d_sum + 2.0 * ff[group, at] * d_square)
-            kept = ee[group, 16 * local : 16 * (local + 1)]
-            d_one = jnp.concatenate([d_one[:16] + kept, d_one[16:]], axis=0) * fe[group, at]
-            sum_b2 = sum_b2 + d_one
-            d_feature.append(d_one)
-        pieces = parts(stack(d_feature), PASSES)
-        gw2[0:wide, 0:thin] += sum(dot(hb[group, 0:wide], piece, NT) for piece in pieces)
-        d_hidden = sum(dot(w2_s[0:wide, 0:thin], piece) for piece in pieces) * he[group, 0:wide]
-        gw1[:, 0:wide] += dot_right(xs[group], d_hidden, NT)
-    gb2[...] += sum_b2
+        wide, thin, low = 64 * count, 32 * count, 16 * count
+        gu2[0:thin, 0:low] += dot(ib[group, 0:thin], dl[group, 0:low], NT)
+        gu1[0:thin, 0:thin] += dot(jb[group, 0:thin], di[group, 0:thin], NT)
+        gw2[0:wide, 0:thin] += dot(hb[group, 0:wide], df[group, 0:thin], NT)
+        gw1[:, 0:wide] += dot(xs[group], dh[group, 0:wide], NT)
 
     @pl.when(step == pl.num_programs(0) - 1)
     def _():
@@ -591,6 +630,10 @@
                 vm((4, 32 * views, n), BF16),
                 vm((4, 32 * views, n), F32),
                 vm((4, 16 * views, n), F32),
+                vm((4, 16 * views, n), BF16),
+                vm((4, 32 * views, n), BF16),
+                vm((4, 32 * views, n), BF16),
+                vm((4, 64 * views, n), BF16),
                 vm((64 * views, 128), BF16),
                 vm((32 * views, 256), BF16),
                 vm((64 * views, 128), BF16),

time: 65.6 us -> 64.7 us (0.986)
  Pallas kernels: 30.2 us -> 29.3 us
    pallas_call x1, Pallas kernels: 17.1 us -> 16.2 us  [run_main(): pl.pallas_call(lambda *refs: main_kernel(views, shard, *refs), out_shape=...]
where the time goes in v5:
time: 64.7 us; the launch traced here: 64.4 us
  Pallas kernels  29.3 us (45%)
  starting transfers between devices  11.5 us (18%)
  blocking collectives  10.4 us (16%)
  between operations  4.03 us (6%)
  waiting for transfers between devices  3.86 us (6%)
  local copies, waits for them, and re-layouts  2.92 us (5%)
  other arithmetic  2.41 us (4%)
    pallas_call x1, Pallas kernels, run_main(): pl.pallas_call(lambda *refs: main_kernel(views, shard, *refs), out_shape=...  16.2 us
    pallas_call x3, Pallas kernels, gather_rows(): pl.pallas_call(lambda *refs: gather_kernel(views, tile, count, *refs), ou...  13.2 us
    all_to_all x1, blocking collectives, body(): got = lax.all_to_all(send, 'rays', 0, 0, tiled=True)  10.4 us
    ppermute x3, starting transfers between devices, body(): lax.ppermute(held, 'rays', swap(shards, 1 << link))  7.26 us
    ppermute x3, waiting for transfers between devices, body(): lax.ppermute(partial, 'views', [(i, i ^ k) for i in range(group)])  2.11 us
    ppermute x3, starting transfers between devices, body(): lax.ppermute(partial, 'views', [(i, i ^ k) for i in range(group)])  1.92 us
    unnamed x16, local copies, waits for them, and re-layouts  1.85 us
    ppermute x3, waiting for transfers between devices, body(): lax.ppermute(held, 'rays', swap(shards, 1 << link))  1.74 us
  transfers between devices with their start and end apart: 9, of which 3 were waited for; matrix products, arithmetic and copies ran while one was open for 2% of the time, Pallas kernels for 20%

profile of v5, /device:TPU:0, one launch (start us, length us, event | category | flops | bytes accessed | tf_op | source)
XLA Modules:
  0.0 64.4 jit_solution(714294222550557185)
XLA Ops:
  0.6 0.7 %convert_element_type.17 = bf16[1423]{0:T(1024)(128)(2,1)S(1)} convert(f32[1423]{0:T(1024)} %param.11) | non-fusion elementwise | flops 1423 | bytes 8538 | tf_op jit(solution)/shard_map/convert_element_type | solution.py:697
  1.3 3.0 %collective-permute-start = (bf16[1,16,128]{2,1,0:T(8,128)(2,1)S(1)}, bf16[1,16,128]{2,1,0:T(8,128)(2,1)S(1)}, u32[]{:S(2)}, u32[]{:S(2)}) collective-permute-start(bf16[1,16,128]{2,1,0:T(8,128)(2,1)S(1)} %pad_bitcast_fusion), channel_id=1, source_target_pairs={{0,4},{4,0},{8,12},{12,8},{16,20},{20,16},{24,28},{28,24},{1,5},{5... | collective-permute-start | bytes 12296 | tf_op jit(solution)/shard_map/ppermute | solution.py:702
  4.3 0.1 pad_add_fusion.refs_0_
  4.4 0.8 %add_bitcast_fusion.refs_1_.refs_2_ = s32[3,3072]{1,0:T(4,128)S(1)} fusion(s32[3072,3]{0,1:T(4,128)} %param.16, s32[3072,3]{0,1:T(4,128)} %param.17), kind=kLoop, calls=%fused_computation.2 | loop fusion | flops 18432 | bytes 110592 | tf_op jit(solution)/shard_map/add | solution.py:698
  5.2 0.0 copy-start
  5.2 1.8 %copy-done = bf16[3,35,12032]{2,1,0:T(8,128)(2,1)S(1)} copy-done((bf16[3,35,12032]{2,1,0:T(8,128)(2,1)S(1)}, bf16[3,35,12032]{2,1,0:T(8,128)(2,1)}, u32[]{:S(2)}) %copy-start) | copy-done | bytes 2526744
  7.0 5.9 %shard_map.140 = (bf16[1,120,768]{2,1,0:T(8,128)(2,1)S(1)}, bf16[1,120,768]{2,1,0:T(8,128)(2,1)S(1)}) custom-call(s32[2]{0:T(128)S(1)} %pad_add_fusion.refs_0_, s32[3,3072]{1,0:T(4,128)S(1)} %add_bitcast_fusion.refs_1_.refs_2_, s32[3,3072]{1,0:T(4,128)S(1)} %add_bitcast_fusion.refs_1_.refs_2_, bf16[3,35,12032]{2,1,0:T(8,128)(2,1)S(1)} %copy-done), custom_call_target="tpu_custom_call" | custom-call | flops 4435476480 | bytes 2526720 | tf_op jit(solution)/shard_map/pallas_call | solution.py:121
  12.9 1.6 %collective-permute-start.4 = (bf16[1,120,768]{2,1,0:T(8,128)(2,1)S(1)}, bf16[1,120,768]{2,1,0:T(8,128)(2,1)S(1)}, u32[]{:S(2)}, u32[]{:S(2)}) collective-permute-start(bf16[1,120,768]{2,1,0:T(8,128)(2,1)S(1)} %get-tuple-element.6), channel_id=1, source_target_pairs={{0,2},{1,3},{2,0},{3,1},{4,6},{5,7},{6,4},{7,5},{8,10},{9,11},{10,... | collective-permute-start | bytes 552968 | tf_op jit(solution)/shard_map/ppermute | solution.py:705
  14.5 0.0 collective-permute-start.5
  14.5 3.7 %shard_map.139 = bf16[1,120,768]{2,1,0:T(8,128)(2,1)S(1)} custom-call(s32[2]{0:T(128)S(1)} %pad_add_fusion.refs_0_, s32[3,3072]{1,0:T(4,128)S(1)} %add_bitcast_fusion.refs_1_.refs_2_, bf16[3,35,12032]{2,1,0:T(8,128)(2,1)S(1)} %copy-done), custom_call_target="tpu_custom_call" | custom-call | flops 2217738240 | bytes 2526720 | tf_op jit(solution)/shard_map/pallas_call | solution.py:121
  18.2 0.7 %collective-permute-start.3 = (bf16[1,120,768]{2,1,0:T(8,128)(2,1)S(1)}, bf16[1,120,768]{2,1,0:T(8,128)(2,1)S(1)}, u32[]{:S(2)}, u32[]{:S(2)}) collective-permute-start(bf16[1,120,768]{2,1,0:T(8,128)(2,1)S(1)} %shard_map.139), channel_id=1, source_target_pairs={{0,1},{1,0},{2,3},{3,2},{4,5},{5,4},{6,7},{7,6},{8,9},{9,8},{10,11... | collective-permute-start | bytes 552968 | tf_op jit(solution)/shard_map/ppermute | solution.py:707
  18.8 0.0 collective-permute-done
  18.9 0.0 copy-start.7
  18.9 0.0 copy-start.5
  18.9 0.0 copy-start.2
  18.9 0.0 copy-start.1
  18.9 0.0 copy-start.3
  18.9 0.0 copy-start.4
  18.9 1.6 %collective-permute-start.1 = (bf16[2,16,128]{2,1,0:T(8,128)(2,1)S(1)}, bf16[2,16,128]{2,1,0:T(8,128)(2,1)S(1)}, u32[]{:S(2)}, u32[]{:S(2)}) collective-permute-start(bf16[2,16,128]{2,1,0:T(8,128)(2,1)S(1)} %pad_maximum_fusion.3), channel_id=1, source_target_pairs={{0,8},{4,12},{8,0},{12,4},{16,24},{20,28},{24,16},{28,20},{1,9},{5... | collective-permute-start | bytes 24584 | tf_op jit(solution)/shard_map/ppermute | solution.py:702
  20.6 3.7 %shard_map.138.refs_2_ = bf16[1,120,768]{2,1,0:T(8,128)(2,1)S(1)} custom-call(s32[2]{0:T(128)S(1)} %pad_add_fusion.refs_0_, s32[3,3072]{1,0:T(4,128)S(1)} %add_bitcast_fusion.refs_1_.refs_2_, bf16[3,35,12032]{2,1,0:T(8,128)(2,1)S(1)} %copy-done), custom_call_target="tpu_custom_call" | custom-call | flops 2217738240 | bytes 2526720 | tf_op jit(solution)/shard_map/pallas_call | solution.py:121
  24.2 0.0 copy-done.6
  24.3 0.0 collective-permute-done.1
  24.3 2.7 %collective-permute-start.2 = (bf16[4,16,128]{2,1,0:T(8,128)(2,1)S(1)}, bf16[4,16,128]{2,1,0:T(8,128)(2,1)S(1)}, u32[]{:S(2)}, u32[]{:S(2)}) collective-permute-start(bf16[4,16,128]{2,1,0:T(8,128)(2,1)S(1)} %pad_maximum_fusion.2), channel_id=1, source_target_pairs={{0,16},{4,20},{8,24},{12,28},{16,0},{20,4},{24,8},{28,12},{1,17},{... | collective-permute-start | bytes 49160 | tf_op jit(solution)/shard_map/ppermute | solution.py:702
  26.9 0.0 copy-done.7
  26.9 0.1 select_reduce_fusion
  27.0 0.0 copy-done.5
  27.0 0.1 reshape.35
  27.1 0.1 reshape.36
  27.2 0.0 copy-done.2
  27.2 0.1 reshape.34.refs_6_
  27.3 1.7 %collective-permute-done.2 = bf16[4,16,128]{2,1,0:T(8,128)(2,1)S(1)} collective-permute-done((bf16[4,16,128]{2,1,0:T(8,128)(2,1)S(1)}, bf16[4,16,128]{2,1,0:T(8,128)(2,1)S(1)}, u32[]{:S(2)}, u32[]{:S(2)}) %collective-permute-start.2) | collective-permute-done | bytes 16416 | tf_op jit(solution)/shard_map/ppermute | solution.py:702
  29.0 0.0 collective-permute-done.4.refs_4_
  29.1 0.0 collective-permute-done.5.refs_5_
  29.1 0.0 collective-permute-done.3.refs_3_
  29.1 16.2 %shard_map.141 = f32[104,128]{1,0:T(8,128)S(1)} custom-call(s32[2]{0:T(128)S(1)} %pad_add_fusion.refs_0_, bf16[8,16,128]{2,1,0:T(8,128)(2,1)S(1)} %pad_maximum_fusion.1.refs_1_, bf16[1,120,768]{2,1,0:T(8,128)(2,1)S(1)} %shard_map.138.refs_2_, bf16[1,120,768]{2,1,0:T(8,128)(2,1)S(1)} %collective-permute-done.3.refs_3_, ...), custom_call_target="tpu_custom_call" | custom-call | tf_op jit(solution)/shard_map/pallas_call | solution.py:605
  45.3 0.1 reshape.38
  45.3 0.1 pad.16.clone
  45.5 10.4 %all_to_all.9 = f32[8,1,1425]{2,1,0:T(1,128)S(1)} all-to-all(f32[8,1,1425]{2,1,0:T(1,128)S(1)} %all_to_all.6), channel_id=1, replica_groups=mesh['rays'=8,'views'=4] {'rays'}, dimensions={0} | all-to-all | bytes 91200 | tf_op jit(solution)/shard_map/all_to_all | solution.py:718
  55.9 0.1 collective-permute-start.6
  56.0 1.6 %collective-permute-start.7 = (f32[1425]{0:T(1024)S(1)}, f32[1425]{0:T(1024)S(1)}, u32[]{:S(2)}, u32[]{:S(2)}) collective-permute-start(f32[1425]{0:T(1024)S(1)} %reduce_sum.19), channel_id=1, source_target_pairs={{0,2},{1,3},{2,0},{3,1},{4,6},{5,7},{6,4},{7,5},{8,10},{9,11},{10,... | collective-permute-start | bytes 17108 | tf_op jit(solution)/shard_map/ppermute | solution.py:722
  57.6 0.3 collective-permute-start.8
  58.5 0.0 collective-permute-done.6
  58.6 1.2 %collective-permute-done.7 = f32[1425]{0:T(1024)S(1)} collective-permute-done((f32[1425]{0:T(1024)S(1)}, f32[1425]{0:T(1024)S(1)}, u32[]{:S(2)}, u32[]{:S(2)}) %collective-permute-start.7) | collective-permute-done | bytes 5732 | tf_op jit(solution)/shard_map/ppermute | solution.py:722
  59.7 0.9 %collective-permute-done.8 = f32[1425]{0:T(1024)S(1)} collective-permute-done((f32[1425]{0:T(1024)S(1)}, f32[1425]{0:T(1024)S(1)}, u32[]{:S(2)}, u32[]{:S(2)}) %collective-permute-start.8) | collective-permute-done | bytes 5732 | tf_op jit(solution)/shard_map/ppermute | solution.py:722
  60.7 0.6 fusion.2
  62.6 0.0 copy-done.1
  62.6 0.0 copy-done.3
  62.6 0.6 multiply_subtract_fusion
  (16 shorter events, 0.2 us)
Async XLA Ops:
  1.3 17.5 %collective-permute-start = (bf16[1,16,128]{2,1,0:T(8,128)(2,1)S(1)}, bf16[1,16,128]{2,1,0:T(8,128)(2,1)S(1)}, u32[]{:S(2)}, u32[]{:S(2)}) collective-permute-start(bf16[1,16,128]{2,1,0:T(8,128)(2,1)S(1)} %pad_bitcast_fusion), channel_id=1, source_target_pairs={{0,4},{4,0},{8,12},{12,8},{16,20},{20,16},{24,28},{28,24},{1,5},{5... | collective-permute-start | bytes 12296 | tf_op jit(solution)/shard_map/ppermute | solution.py:702
  5.2 1.8 %copy-start = (bf16[3,35,12032]{2,1,0:T(8,128)(2,1)S(1)}, bf16[3,35,12032]{2,1,0:T(8,128)(2,1)}, u32[]{:S(2)}) copy-start(bf16[3,35,12032]{2,1,0:T(8,128)(2,1)} %refs_3_.1) | copy-start | bytes 7580164
  12.9 16.1 %collective-permute-start.4 = (bf16[1,120,768]{2,1,0:T(8,128)(2,1)S(1)}, bf16[1,120,768]{2,1,0:T(8,128)(2,1)S(1)}, u32[]{:S(2)}, u32[]{:S(2)}) collective-permute-start(bf16[1,120,768]{2,1,0:T(8,128)(2,1)S(1)} %get-tuple-element.6), channel_id=1, source_target_pairs={{0,2},{1,3},{2,0},{3,1},{4,6},{5,7},{6,4},{7,5},{8,10},{9,11},{10,... | collective-permute-start | bytes 552968 | tf_op jit(solution)/shard_map/ppermute | solution.py:705
  14.5 14.6 %collective-permute-start.5 = (bf16[1,120,768]{2,1,0:T(8,128)(2,1)S(1)}, bf16[1,120,768]{2,1,0:T(8,128)(2,1)S(1)}, u32[]{:S(2)}, u32[]{:S(2)}) collective-permute-start(bf16[1,120,768]{2,1,0:T(8,128)(2,1)S(1)} %get-tuple-element.7), channel_id=1, source_target_pairs={{0,3},{1,2},{2,1},{3,0},{4,7},{5,6},{6,5},{7,4},{8,11},{9,10},{10,... | collective-permute-start | bytes 552968 | tf_op jit(solution)/shard_map/ppermute | solution.py:704
  18.2 10.9 %collective-permute-start.3 = (bf16[1,120,768]{2,1,0:T(8,128)(2,1)S(1)}, bf16[1,120,768]{2,1,0:T(8,128)(2,1)S(1)}, u32[]{:S(2)}, u32[]{:S(2)}) collective-permute-start(bf16[1,120,768]{2,1,0:T(8,128)(2,1)S(1)} %shard_map.139), channel_id=1, source_target_pairs={{0,1},{1,0},{2,3},{3,2},{4,5},{5,4},{6,7},{7,6},{8,9},{9,8},{10,11... | collective-permute-start | bytes 552968 | tf_op jit(solution)/shard_map/ppermute | solution.py:707
  18.9 5.4 %copy-start.6 = (s32[8]{0:T(128)S(1)}, s32[8]{0:T(128)}, u32[]{:S(2)}) copy-start(s32[8]{0:T(128)} %param.21) | copy-start | bytes 100
  18.9 8.1 %copy-start.7 = (s32[16]{0:T(128)S(1)}, s32[16]{0:T(128)}, u32[]{:S(2)}) copy-start(s32[16]{0:T(128)} %param.20) | copy-start | bytes 196
  18.9 8.2 %copy-start.5 = (f32[16,3]{0,1:T(4,128)S(1)}, f32[16,3]{0,1:T(4,128)}, u32[]{:S(2)}) copy-start(f32[16,3]{0,1:T(4,128)} %param.19) | copy-start | bytes 580
  18.9 8.3 %copy-start.2 = (f32[16,192]{1,0:T(8,128)S(1)}, f32[16,192]{1,0:T(8,128)}, u32[]{:S(2)}) copy-start(f32[16,192]{1,0:T(8,128)} %param.18) | copy-start | bytes 36868
  18.9 43.7 %copy-start.1 = (f32[1423]{0:T(1024)S(1)}, f32[1423]{0:T(1024)}, u32[]{:S(2)}) copy-start(f32[1423]{0:T(1024)} %param.11) | copy-start | bytes 17080
  18.9 43.7 %copy-start.3 = (f32[1423]{0:T(1024)S(1)}, f32[1423]{0:T(1024)}, u32[]{:S(2)}) copy-start(f32[1423]{0:T(1024)} %param.13) | copy-start | bytes 17080
  18.9 43.7 %copy-start.4 = (f32[1423]{0:T(1024)S(1)}, f32[1423]{0:T(1024)}, u32[]{:S(2)}) copy-start(f32[1423]{0:T(1024)} %param.12) | copy-start | bytes 17080
  18.9 5.3 %collective-permute-start.1 = (bf16[2,16,128]{2,1,0:T(8,128)(2,1)S(1)}, bf16[2,16,128]{2,1,0:T(8,128)(2,1)S(1)}, u32[]{:S(2)}, u32[]{:S(2)}) collective-permute-start(bf16[2,16,128]{2,1,0:T(8,128)(2,1)S(1)} %pad_maximum_fusion.3), channel_id=1, source_target_pairs={{0,8},{4,12},{8,0},{12,4},{16,24},{20,28},{24,16},{28,20},{1,9},{5... | collective-permute-start | bytes 24584 | tf_op jit(solution)/shard_map/ppermute | solution.py:702
  24.3 4.8 %collective-permute-start.2 = (bf16[4,16,128]{2,1,0:T(8,128)(2,1)S(1)}, bf16[4,16,128]{2,1,0:T(8,128)(2,1)S(1)}, u32[]{:S(2)}, u32[]{:S(2)}) collective-permute-start(bf16[4,16,128]{2,1,0:T(8,128)(2,1)S(1)} %pad_maximum_fusion.2), channel_id=1, source_target_pairs={{0,16},{4,20},{8,24},{12,28},{16,0},{20,4},{24,8},{28,12},{1,17},{... | collective-permute-start | bytes 49160 | tf_op jit(solution)/shard_map/ppermute | solution.py:702
  55.9 2.6 %collective-permute-start.6 = (f32[1425]{0:T(1024)S(1)}, f32[1425]{0:T(1024)S(1)}, u32[]{:S(2)}, u32[]{:S(2)}) collective-permute-start(f32[1425]{0:T(1024)S(1)} %reduce_sum.19), channel_id=1, source_target_pairs={{0,1},{1,0},{2,3},{3,2},{4,5},{5,4},{6,7},{7,6},{8,9},{9,8},{10,11... | collective-permute-start | bytes 17108 | tf_op jit(solution)/shard_map/ppermute | solution.py:722
  56.0 3.7 %collective-permute-start.7 = (f32[1425]{0:T(1024)S(1)}, f32[1425]{0:T(1024)S(1)}, u32[]{:S(2)}, u32[]{:S(2)}) collective-permute-start(f32[1425]{0:T(1024)S(1)} %reduce_sum.19), channel_id=1, source_target_pairs={{0,2},{1,3},{2,0},{3,1},{4,6},{5,7},{6,4},{7,5},{8,10},{9,11},{10,... | collective-permute-start | bytes 17108 | tf_op jit(solution)/shard_map/ppermute | solution.py:722
  57.6 3.1 %collective-permute-start.8 = (f32[1425]{0:T(1024)S(1)}, f32[1425]{0:T(1024)S(1)}, u32[]{:S(2)}, u32[]{:S(2)}) collective-permute-start(f32[1425]{0:T(1024)S(1)} %reduce_sum.19), channel_id=1, source_target_pairs={{0,3},{1,2},{2,1},{3,0},{4,7},{5,6},{6,5},{7,4},{8,11},{9,10},{10,... | collective-permute-start | bytes 17108 | tf_op jit(solution)/shard_map/ppermute | solution.py:722

commit v6 on v5

--- a/solution.py
+++ b/solution.py
@@ -60,17 +60,16 @@
     return lax.broadcasted_iota(jnp.int32, shape, axis)
 
 
-def stack_maps(map_ref, stacked):
-    views, channels, pixels = map_ref.shape
+def stack_maps(map_ref, stacked, view):
+    channels, pixels = map_ref.shape[1:]
     blocks = pixels // 256
-    for view in range(views):
-        for block in range(0, blocks, 2):
-            strips = []
-            for part in range(block, min(block + 2, blocks)):
-                strips.append(map_ref[view, :, 256 * part : 256 * (part + 1)].astype(F32))
-                strips.append(jnp.zeros((BAND - channels, 256), F32))
-            strips = jnp.concatenate(strips, axis=0)
-            stacked[view, BAND * block : BAND * block + strips.shape[0], :] = strips.astype(BF16)
+    for block in range(0, blocks, 2):
+        strips = []
+        for part in range(block, min(block + 2, blocks)):
+            strips.append(map_ref[view, :, 256 * part : 256 * (part + 1)].astype(F32))
+            strips.append(jnp.zeros((BAND - channels, 256), F32))
+        strips = jnp.concatenate(strips, axis=0)
+        stacked[view, BAND * block : BAND * block + strips.shape[0], :] = strips.astype(BF16)
 
 
 def gather_kernel(views, tile, count, *refs):
@@ -80,7 +79,8 @@
 
     @pl.when(pl.program_id(0) == 0)
     def _():
-        stack_maps(source, stacked)
+        for view in range(views):
+            stack_maps(source, stacked, view)
 
     row = iota((8, tile), 0) + 8 * (CHANNELS // 8)
     for packed_ref, out_ref in zip(packed_refs, outs):
@@ -194,6 +194,7 @@
     target_ref,
     weight_ref,
     out_ref,
+    sums_ref,
     a_ref,
     r64,
     r32,
@@ -579,7 +580,9 @@
         out_ref[0:18, :] = sum(roll(g64[pl.ds(b, 18, stride=2), :], 64 * b) for b in range(2))
         out_ref[18:51, :] += sum(roll(g32[pl.ds(b, 33, stride=4), :], 32 * b) for b in range(4))
         out_ref[50:89, :] += sum(roll(g16[pl.ds(b, 39, stride=8), :], 16 * b) for b in range(8))
-        out_ref[96:104, :] = loss_s[...]
+        sums_ref[...] = jnp.where(
+            iota(sums_ref.shape, 1) == 0, loss_s[0:1, 0:1], loss_s[0:1, 1:2]
+        )
 
 
 def widen(value):
@@ -592,6 +595,8 @@
     views = rows // STRIP
     n = CHUNK
     steps = points // n
+    shards = pieces.shape[0]
+    sums = (shards, -(-(shard + 2) // 128) * 128)
     whole = deltas.shape[0] // 2
     pairs = deltas.reshape(whole, 1, n)
     target_pairs = jnp.pad(
@@ -604,7 +609,10 @@
     piece = pl.BlockSpec(pieces.shape, lambda t, me: (0, 0, 0))
     return pl.pallas_call(
         lambda *refs: main_kernel(views, shard, *refs),
-        out_shape=jax.ShapeDtypeStruct((104, 128), F32),
+        out_shape=[
+            jax.ShapeDtypeStruct((96, 128), F32),
+            jax.ShapeDtypeStruct(sums, F32),
+        ],
         grid_spec=pltpu.PrefetchScalarGridSpec(
             num_scalar_prefetch=1,
             grid=(steps,),
@@ -615,7 +623,10 @@
                 pl.BlockSpec((1, 8, 128), own),
                 pl.BlockSpec((1, 8, 128), own),
             ],
-            out_specs=pl.BlockSpec((104, 128), lambda t, me: (0, 0)),
+            out_specs=[
+                pl.BlockSpec((96, 128), lambda t, me: (0, 0)),
+                pl.BlockSpec(sums, lambda t, me: (0, 0)),
+            ],
             scratch_shapes=[
                 vm((120, 128), F32),
                 vm((40, 128), F32),
@@ -708,21 +719,21 @@
     mine = gather_rows(packed, feature_maps, me, group, (0,))
     hits = (scene_id[:, None] == jnp.arange(scene_weight.shape[0])[None, :]).astype(F32)
     ray_weight = jnp.sum(hits * scene_weight.astype(F32)[None, :], axis=1)
-    result = run_main(me, [mine[0], one, two, three], held, shard, deltas, targets, ray_weight)
+    result, sums = run_main(me, [mine[0], one, two, three], held, shard, deltas, targets, ray_weight)
     summed = result[:89].reshape(-1)
     size = shards * shard
     if summed.shape[0] < size:
         summed = jnp.pad(summed, (0, size - summed.shape[0]))
-    extra = jnp.broadcast_to(result[96, :2][None], (shards, 2))
-    send = jnp.concatenate([summed[:size].reshape(shards, shard), extra], axis=1)
+    loss_at, far_at = shard, shard + 1
+    send = jnp.concatenate([summed[:size].reshape(shards, shard), sums], axis=1)
     got = lax.all_to_all(send, "rays", 0, 0, tiled=True)
     partial = jnp.sum(got, axis=0)
     whole = partial
     for k in range(1, group):
         whole = whole + lax.ppermute(partial, "views", [(i, i ^ k) for i in range(group)])
-    seed = 1.0 / whole[shard + 1]
-    loss = whole[shard] * seed
-    gradient = whole[:shard] * seed
+    scaled = whole[: shard + 1] / whole[far_at : far_at + shard + 1]
+    loss = scaled[loss_at]
+    gradient = scaled[:shard]
     return (loss, *adamw(master, first_moment, second_moment, gradient, step_count))
 
 

time: 64.7 us -> 62.7 us (0.969)
  between operations: 4.03 us -> 1.53 us
  transfers between devices with their start and end apart: 9 -> 9, of which waited for: 3 -> 3; matrix products, arithmetic and copies ran while one was open for 2% -> 2% of each run, Pallas kernels for 20% -> 21%
where the time goes in v6:
time: 62.7 us; the launch traced here: 62.4 us
  Pallas kernels  29.3 us (47%)
  starting transfers between devices  11.5 us (18%)
  blocking collectives  10.7 us (17%)
  waiting for transfers between devices  3.9 us (6%)
  local copies, waits for them, and re-layouts  2.92 us (5%)
  other arithmetic  2.59 us (4%)
  between operations  1.53 us (2%)
    pallas_call x1, Pallas kernels, run_main(): pl.pallas_call(lambda *refs: main_kernel(views, shard, *refs), out_shape=...  16.2 us
    pallas_call x3, Pallas kernels, gather_rows(): pl.pallas_call(lambda *refs: gather_kernel(views, tile, count, *refs), ou...  13.2 us
    all_to_all x1, blocking collectives, body(): got = lax.all_to_all(send, 'rays', 0, 0, tiled=True)  10.7 us
    ppermute x3, starting transfers between devices, body(): lax.ppermute(held, 'rays', swap(shards, 1 << link))  7.26 us
    ppermute x3, waiting for transfers between devices, body(): lax.ppermute(partial, 'views', [(i, i ^ k) for i in range(group)])  2.15 us
    ppermute x3, starting transfers between devices, body(): lax.ppermute(partial, 'views', [(i, i ^ k) for i in range(group)])  1.92 us
    unnamed x16, local copies, waits for them, and re-layouts  1.85 us
    ppermute x3, waiting for transfers between devices, body(): lax.ppermute(held, 'rays', swap(shards, 1 << link))  1.74 us
  transfers between devices with their start and end apart: 9, of which 3 were waited for; matrix products, arithmetic and copies ran while one was open for 2% of the time, Pallas kernels for 21%

profile of v6, /device:TPU:0, one launch (start us, length us, event | category | flops | bytes accessed | tf_op | source)
XLA Modules:
  0.0 62.4 jit_solution(18265108464483619966)
XLA Ops:
  0.6 0.7 %convert_element_type.17 = bf16[1423]{0:T(1024)(128)(2,1)S(1)} convert(f32[1423]{0:T(1024)} %param.11) | non-fusion elementwise | flops 1423 | bytes 8538 | tf_op jit(solution)/shard_map/convert_element_type | solution.py:708
  1.3 3.0 %collective-permute-start = (bf16[1,16,128]{2,1,0:T(8,128)(2,1)S(1)}, bf16[1,16,128]{2,1,0:T(8,128)(2,1)S(1)}, u32[]{:S(2)}, u32[]{:S(2)}) collective-permute-start(bf16[1,16,128]{2,1,0:T(8,128)(2,1)S(1)} %pad_bitcast_fusion), channel_id=1, source_target_pairs={{0,4},{4,0},{8,12},{12,8},{16,20},{20,16},{24,28},{28,24},{1,5},{5... | collective-permute-start | bytes 12296 | tf_op jit(solution)/shard_map/ppermute | solution.py:713
  4.3 0.1 pad_add_fusion.refs_0_
  4.4 0.8 %add_bitcast_fusion.refs_1_.refs_2_ = s32[3,3072]{1,0:T(4,128)S(1)} fusion(s32[3072,3]{0,1:T(4,128)} %param.16, s32[3072,3]{0,1:T(4,128)} %param.17), kind=kLoop, calls=%fused_computation.2 | loop fusion | flops 18432 | bytes 110592 | tf_op jit(solution)/shard_map/add | solution.py:709
  5.2 0.0 copy-start
  5.2 1.8 %copy-done = bf16[3,35,12032]{2,1,0:T(8,128)(2,1)S(1)} copy-done((bf16[3,35,12032]{2,1,0:T(8,128)(2,1)S(1)}, bf16[3,35,12032]{2,1,0:T(8,128)(2,1)}, u32[]{:S(2)}) %copy-start) | copy-done | bytes 2526744
  7.0 5.9 %shard_map.140 = (bf16[1,120,768]{2,1,0:T(8,128)(2,1)S(1)}, bf16[1,120,768]{2,1,0:T(8,128)(2,1)S(1)}) custom-call(s32[2]{0:T(128)S(1)} %pad_add_fusion.refs_0_, s32[3,3072]{1,0:T(4,128)S(1)} %add_bitcast_fusion.refs_1_.refs_2_, s32[3,3072]{1,0:T(4,128)S(1)} %add_bitcast_fusion.refs_1_.refs_2_, bf16[3,35,12032]{2,1,0:T(8,128)(2,1)S(1)} %copy-done), custom_call_target="tpu_custom_call" | custom-call | flops 4435476480 | bytes 2526720 | tf_op jit(solution)/shard_map/pallas_call | solution.py:121
  12.9 1.6 %collective-permute-start.4 = (bf16[1,120,768]{2,1,0:T(8,128)(2,1)S(1)}, bf16[1,120,768]{2,1,0:T(8,128)(2,1)S(1)}, u32[]{:S(2)}, u32[]{:S(2)}) collective-permute-start(bf16[1,120,768]{2,1,0:T(8,128)(2,1)S(1)} %get-tuple-element.8), channel_id=1, source_target_pairs={{0,2},{1,3},{2,0},{3,1},{4,6},{5,7},{6,4},{7,5},{8,10},{9,11},{10,... | collective-permute-start | bytes 552968 | tf_op jit(solution)/shard_map/ppermute | solution.py:716
  14.5 0.0 collective-permute-start.5
  14.5 3.7 %shard_map.139 = bf16[1,120,768]{2,1,0:T(8,128)(2,1)S(1)} custom-call(s32[2]{0:T(128)S(1)} %pad_add_fusion.refs_0_, s32[3,3072]{1,0:T(4,128)S(1)} %add_bitcast_fusion.refs_1_.refs_2_, bf16[3,35,12032]{2,1,0:T(8,128)(2,1)S(1)} %copy-done), custom_call_target="tpu_custom_call" | custom-call | flops 2217738240 | bytes 2526720 | tf_op jit(solution)/shard_map/pallas_call | solution.py:121
  18.2 0.7 %collective-permute-start.3 = (bf16[1,120,768]{2,1,0:T(8,128)(2,1)S(1)}, bf16[1,120,768]{2,1,0:T(8,128)(2,1)S(1)}, u32[]{:S(2)}, u32[]{:S(2)}) collective-permute-start(bf16[1,120,768]{2,1,0:T(8,128)(2,1)S(1)} %shard_map.139), channel_id=1, source_target_pairs={{0,1},{1,0},{2,3},{3,2},{4,5},{5,4},{6,7},{7,6},{8,9},{9,8},{10,11... | collective-permute-start | bytes 552968 | tf_op jit(solution)/shard_map/ppermute | solution.py:718
  18.8 0.0 collective-permute-done
  18.9 0.0 copy-start.7
  18.9 0.0 copy-start.5
  18.9 0.0 copy-start.2
  18.9 0.0 copy-start.1
  18.9 0.0 copy-start.3
  18.9 0.0 copy-start.4
  18.9 1.6 %collective-permute-start.1 = (bf16[2,16,128]{2,1,0:T(8,128)(2,1)S(1)}, bf16[2,16,128]{2,1,0:T(8,128)(2,1)S(1)}, u32[]{:S(2)}, u32[]{:S(2)}) collective-permute-start(bf16[2,16,128]{2,1,0:T(8,128)(2,1)S(1)} %pad_maximum_fusion.2), channel_id=1, source_target_pairs={{0,8},{4,12},{8,0},{12,4},{16,24},{20,28},{24,16},{28,20},{1,9},{5... | collective-permute-start | bytes 24584 | tf_op jit(solution)/shard_map/ppermute | solution.py:713
  20.6 3.7 %shard_map.138.refs_2_ = bf16[1,120,768]{2,1,0:T(8,128)(2,1)S(1)} custom-call(s32[2]{0:T(128)S(1)} %pad_add_fusion.refs_0_, s32[3,3072]{1,0:T(4,128)S(1)} %add_bitcast_fusion.refs_1_.refs_2_, bf16[3,35,12032]{2,1,0:T(8,128)(2,1)S(1)} %copy-done), custom_call_target="tpu_custom_call" | custom-call | flops 2217738240 | bytes 2526720 | tf_op jit(solution)/shard_map/pallas_call | solution.py:121
  24.2 0.0 copy-done.6
  24.3 0.0 collective-permute-done.1
  24.3 2.7 %collective-permute-start.2 = (bf16[4,16,128]{2,1,0:T(8,128)(2,1)S(1)}, bf16[4,16,128]{2,1,0:T(8,128)(2,1)S(1)}, u32[]{:S(2)}, u32[]{:S(2)}) collective-permute-start(bf16[4,16,128]{2,1,0:T(8,128)(2,1)S(1)} %pad_maximum_fusion.1), channel_id=1, source_target_pairs={{0,16},{4,20},{8,24},{12,28},{16,0},{20,4},{24,8},{28,12},{1,17},{... | collective-permute-start | bytes 49160 | tf_op jit(solution)/shard_map/ppermute | solution.py:713
  26.9 0.0 copy-done.7
  26.9 0.1 select_reduce_fusion
  27.0 0.1 reshape.33
  27.1 0.1 reshape.34
  27.2 0.1 reshape.32.refs_6_
  27.3 1.7 %collective-permute-done.2 = bf16[4,16,128]{2,1,0:T(8,128)(2,1)S(1)} collective-permute-done((bf16[4,16,128]{2,1,0:T(8,128)(2,1)S(1)}, bf16[4,16,128]{2,1,0:T(8,128)(2,1)S(1)}, u32[]{:S(2)}, u32[]{:S(2)}) %collective-permute-start.2) | collective-permute-done | bytes 16416 | tf_op jit(solution)/shard_map/ppermute | solution.py:713
  29.0 0.0 collective-permute-done.4.refs_4_
  29.1 0.0 collective-permute-done.5.refs_5_
  29.1 0.0 collective-permute-done.3.refs_3_
  29.1 16.2 %shard_map.141 = (f32[96,128]{1,0:T(8,128)S(1)}, f32[8,1536]{1,0:T(8,128)S(1)}) custom-call(s32[2]{0:T(128)S(1)} %pad_add_fusion.refs_0_, bf16[8,16,128]{2,1,0:T(8,128)(2,1)S(1)} %pad_maximum_fusion.refs_1_, bf16[1,120,768]{2,1,0:T(8,128)(2,1)S(1)} %shard_map.138.refs_2_, bf16[1,120,768]{2,1,0:T(8,128)(2,1)S(1)} %collective-permute-done.3.refs_3_, ...), custom_call_target="tpu_custom_call" | custom-call | tf_op jit(solution)/shard_map/pallas_call | solution.py:610
  45.2 0.1 reshape.36
  45.4 0.1 maximum_bitcast_fusion
  45.4 0.1 copy.24
  45.5 10.7 %all_to_all.9 = f32[8,1,2959]{2,1,0:T(1,128)S(1)} all-to-all(f32[8,1,2959]{2,1,0:T(1,128)S(1)} %copy.24), channel_id=1, replica_groups=mesh['rays'=8,'views'=4] {'rays'}, dimensions={0} | all-to-all | bytes 189376 | tf_op jit(solution)/shard_map/all_to_all | solution.py:729
  56.3 0.1 reduce_sum.19
  56.4 0.1 collective-permute-start.6
  56.4 1.6 %collective-permute-start.7 = (f32[2959]{0:T(1024)S(1)}, f32[2959]{0:T(1024)S(1)}, u32[]{:S(2)}, u32[]{:S(2)}) collective-permute-start(f32[2959]{0:T(1024)S(1)} %reduce_sum.19), channel_id=1, source_target_pairs={{0,2},{1,3},{2,0},{3,1},{4,6},{5,7},{6,4},{7,5},{8,10},{9,11},{10,... | collective-permute-start | bytes 35516 | tf_op jit(solution)/shard_map/ppermute | solution.py:733
  58.0 0.3 collective-permute-start.8
  59.0 0.0 collective-permute-done.6
  59.0 1.2 %collective-permute-done.7 = f32[2959]{0:T(1024)S(1)} collective-permute-done((f32[2959]{0:T(1024)S(1)}, f32[2959]{0:T(1024)S(1)}, u32[]{:S(2)}, u32[]{:S(2)}) %collective-permute-start.7) | collective-permute-done | bytes 11868 | tf_op jit(solution)/shard_map/ppermute | solution.py:733
  60.2 0.9 %collective-permute-done.8 = f32[2959]{0:T(1024)S(1)} collective-permute-done((f32[2959]{0:T(1024)S(1)}, f32[2959]{0:T(1024)S(1)}, u32[]{:S(2)}, u32[]{:S(2)}) %collective-permute-start.8) | collective-permute-done | bytes 11868 | tf_op jit(solution)/shard_map/ppermute | solution.py:733
  61.1 0.1 slice_divide_fusion
  61.2 0.6 slice.27
  61.8 0.0 copy-done.1
  61.8 0.6 %multiply_subtract_fusion = (f32[1423]{0:T(1024)}, f32[1423]{0:T(1024)}, f32[1423]{0:T(1024)}) fusion(f32[1423]{0:T(1024)S(1)} %copy-done.1, f32[]{:T(128)} %bitcast.9, f32[1424]{0:T(1024)S(1)} %slice_divide_fusion, f32[1423]{0:T(1024)S(1)} %copy-done.3, f32[1423]{0:T(1024)S(1)} %copy-done.4), kind=kLoop, calls=%fused_computation.12 | loop fusion | flops 19922 | bytes 39848 | tf_op jit(solution)/shard_map/sub | solution.py:683
  (15 shorter events, 0.1 us)
Async XLA Ops:
  1.3 17.5 %collective-permute-start = (bf16[1,16,128]{2,1,0:T(8,128)(2,1)S(1)}, bf16[1,16,128]{2,1,0:T(8,128)(2,1)S(1)}, u32[]{:S(2)}, u32[]{:S(2)}) collective-permute-start(bf16[1,16,128]{2,1,0:T(8,128)(2,1)S(1)} %pad_bitcast_fusion), channel_id=1, source_target_pairs={{0,4},{4,0},{8,12},{12,8},{16,20},{20,16},{24,28},{28,24},{1,5},{5... | collective-permute-start | bytes 12296 | tf_op jit(solution)/shard_map/ppermute | solution.py:713
  5.2 1.8 %copy-start = (bf16[3,35,12032]{2,1,0:T(8,128)(2,1)S(1)}, bf16[3,35,12032]{2,1,0:T(8,128)(2,1)}, u32[]{:S(2)}) copy-start(bf16[3,35,12032]{2,1,0:T(8,128)(2,1)} %refs_3_.1) | copy-start | bytes 7580164
  12.9 16.1 %collective-permute-start.4 = (bf16[1,120,768]{2,1,0:T(8,128)(2,1)S(1)}, bf16[1,120,768]{2,1,0:T(8,128)(2,1)S(1)}, u32[]{:S(2)}, u32[]{:S(2)}) collective-permute-start(bf16[1,120,768]{2,1,0:T(8,128)(2,1)S(1)} %get-tuple-element.8), channel_id=1, source_target_pairs={{0,2},{1,3},{2,0},{3,1},{4,6},{5,7},{6,4},{7,5},{8,10},{9,11},{10,... | collective-permute-start | bytes 552968 | tf_op jit(solution)/shard_map/ppermute | solution.py:716
  14.5 14.6 %collective-permute-start.5 = (bf16[1,120,768]{2,1,0:T(8,128)(2,1)S(1)}, bf16[1,120,768]{2,1,0:T(8,128)(2,1)S(1)}, u32[]{:S(2)}, u32[]{:S(2)}) collective-permute-start(bf16[1,120,768]{2,1,0:T(8,128)(2,1)S(1)} %get-tuple-element.9), channel_id=1, source_target_pairs={{0,3},{1,2},{2,1},{3,0},{4,7},{5,6},{6,5},{7,4},{8,11},{9,10},{10,... | collective-permute-start | bytes 552968 | tf_op jit(solution)/shard_map/ppermute | solution.py:715
  18.2 10.9 %collective-permute-start.3 = (bf16[1,120,768]{2,1,0:T(8,128)(2,1)S(1)}, bf16[1,120,768]{2,1,0:T(8,128)(2,1)S(1)}, u32[]{:S(2)}, u32[]{:S(2)}) collective-permute-start(bf16[1,120,768]{2,1,0:T(8,128)(2,1)S(1)} %shard_map.139), channel_id=1, source_target_pairs={{0,1},{1,0},{2,3},{3,2},{4,5},{5,4},{6,7},{7,6},{8,9},{9,8},{10,11... | collective-permute-start | bytes 552968 | tf_op jit(solution)/shard_map/ppermute | solution.py:718
  18.9 5.4 %copy-start.6 = (s32[8]{0:T(128)S(1)}, s32[8]{0:T(128)}, u32[]{:S(2)}) copy-start(s32[8]{0:T(128)} %param.21) | copy-start | bytes 100
  18.9 8.1 %copy-start.7 = (s32[16]{0:T(128)S(1)}, s32[16]{0:T(128)}, u32[]{:S(2)}) copy-start(s32[16]{0:T(128)} %param.20) | copy-start | bytes 196
  18.9 8.2 %copy-start.5 = (f32[16,3]{0,1:T(4,128)S(1)}, f32[16,3]{0,1:T(4,128)}, u32[]{:S(2)}) copy-start(f32[16,3]{0,1:T(4,128)} %param.19) | copy-start | bytes 580
  18.9 8.3 %copy-start.2 = (f32[16,192]{1,0:T(8,128)S(1)}, f32[16,192]{1,0:T(8,128)}, u32[]{:S(2)}) copy-start(f32[16,192]{1,0:T(8,128)} %param.18) | copy-start | bytes 36868
  18.9 42.9 %copy-start.1 = (f32[1423]{0:T(1024)S(1)}, f32[1423]{0:T(1024)}, u32[]{:S(2)}) copy-start(f32[1423]{0:T(1024)} %param.11) | copy-start | bytes 17080
  18.9 42.9 %copy-start.3 = (f32[1423]{0:T(1024)S(1)}, f32[1423]{0:T(1024)}, u32[]{:S(2)}) copy-start(f32[1423]{0:T(1024)} %param.13) | copy-start | bytes 17080
  18.9 42.9 %copy-start.4 = (f32[1423]{0:T(1024)S(1)}, f32[1423]{0:T(1024)}, u32[]{:S(2)}) copy-start(f32[1423]{0:T(1024)} %param.12) | copy-start | bytes 17080
  18.9 5.3 %collective-permute-start.1 = (bf16[2,16,128]{2,1,0:T(8,128)(2,1)S(1)}, bf16[2,16,128]{2,1,0:T(8,128)(2,1)S(1)}, u32[]{:S(2)}, u32[]{:S(2)}) collective-permute-start(bf16[2,16,128]{2,1,0:T(8,128)(2,1)S(1)} %pad_maximum_fusion.2), channel_id=1, source_target_pairs={{0,8},{4,12},{8,0},{12,4},{16,24},{20,28},{24,16},{28,20},{1,9},{5... | collective-permute-start | bytes 24584 | tf_op jit(solution)/shard_map/ppermute | solution.py:713
  24.3 4.8 %collective-permute-start.2 = (bf16[4,16,128]{2,1,0:T(8,128)(2,1)S(1)}, bf16[4,16,128]{2,1,0:T(8,128)(2,1)S(1)}, u32[]{:S(2)}, u32[]{:S(2)}) collective-permute-start(bf16[4,16,128]{2,1,0:T(8,128)(2,1)S(1)} %pad_maximum_fusion.1), channel_id=1, source_target_pairs={{0,16},{4,20},{8,24},{12,28},{16,0},{20,4},{24,8},{28,12},{1,17},{... | collective-permute-start | bytes 49160 | tf_op jit(solution)/shard_map/ppermute | solution.py:713
  56.4 2.6 %collective-permute-start.6 = (f32[2959]{0:T(1024)S(1)}, f32[2959]{0:T(1024)S(1)}, u32[]{:S(2)}, u32[]{:S(2)}) collective-permute-start(f32[2959]{0:T(1024)S(1)} %reduce_sum.19), channel_id=1, source_target_pairs={{0,1},{1,0},{2,3},{3,2},{4,5},{5,4},{6,7},{7,6},{8,9},{9,8},{10,11... | collective-permute-start | bytes 35516 | tf_op jit(solution)/shard_map/ppermute | solution.py:733
  56.4 3.8 %collective-permute-start.7 = (f32[2959]{0:T(1024)S(1)}, f32[2959]{0:T(1024)S(1)}, u32[]{:S(2)}, u32[]{:S(2)}) collective-permute-start(f32[2959]{0:T(1024)S(1)} %reduce_sum.19), channel_id=1, source_target_pairs={{0,2},{1,3},{2,0},{3,1},{4,6},{5,7},{6,4},{7,5},{8,10},{9,11},{10,... | collective-permute-start | bytes 35516 | tf_op jit(solution)/shard_map/ppermute | solution.py:733
  58.0 3.1 %collective-permute-start.8 = (f32[2959]{0:T(1024)S(1)}, f32[2959]{0:T(1024)S(1)}, u32[]{:S(2)}, u32[]{:S(2)}) collective-permute-start(f32[2959]{0:T(1024)S(1)} %reduce_sum.19), channel_id=1, source_target_pairs={{0,3},{1,2},{2,1},{3,0},{4,7},{5,6},{6,5},{7,4},{8,11},{9,10},{10,... | collective-permute-start | bytes 35516 | tf_op jit(solution)/shard_map/ppermute | solution.py:733
